TPU v7x, 32 devices: a whole 2x2x4 slice. The times are simulated.
32 devices in a mesh: dp: 8 (over z, core), expert: 4 (over y, x).
Axes of the slice: x: 2, y: 2, z: 4, core: 2. Of those that a mesh axis runs over, the one named last changes fastest.
Arguments:
- tokens: bfloat16 [8192, 1024], P(('dp', 'expert')), may hold values from -6 to 6
- cotangent: bfloat16 [8192, 1024], P(('dp', 'expert')), may hold values from -6 to 6
- qkv_weight: bfloat16 [1024, 3072], P(('dp', 'expert')), may hold values from -0.1875 to 0.1875
- out_weight: bfloat16 [1024, 1024], P(('dp', 'expert')), may hold values from -0.75 to 0.75
- router_weight: bfloat16 [1024, 4], P(('dp', 'expert')), may hold values from -0.1875 to 0.1875
- first_gain: bfloat16 [1024], P(('dp', 'expert')), may hold values from 0.5 to 1.5
- second_gain: bfloat16 [1024], P(('dp', 'expert')), may hold values from 0.5 to 1.5
- bias_table: bfloat16 [512], P(('dp', 'expert')), may hold values from -4 to 4
- gate_weight: bfloat16 [4, 1024, 2816], P('expert', 'dp'), may hold values from -0.1875 to 0.1875
- up_weight: bfloat16 [4, 1024, 2816], P('expert', 'dp'), may hold values from -0.1875 to 0.1875
- down_weight: bfloat16 [4, 2816, 1024], P('expert', 'dp'), may hold values from -0.109375 to 0.109375
- lengths: int32 [8, 4], P('dp', 'expert'), may hold values from 1 to 256, 768 in all within a row
- routes: int32 [8192, 2], P(('dp', 'expert')), may hold values from 0 to 3, all different within a row; in each aligned block of 256 rows (0 to 255, 256 to 511, ...) at most 256 rows name the same one
- priority: int32 [8, 1024], P('dp', 'expert'), may hold values from 0 to 1023, each once within a row
Outputs:
- output: bfloat16 [8192, 1024], P(('dp', 'expert'))
- grad_tokens: float32 [8192, 1024], P(('dp', 'expert'))
- grad_qkv_weight: float32 [1024, 3072], P(('dp', 'expert'))
- output_weight_gradient: float32 [1024, 1024], P(('dp', 'expert'))
- grad_router_weight: float32 [1024, 4], P(('dp', 'expert'))
- grad_first_gain: float32 [1024], P(('dp', 'expert'))
- grad_second_gain: float32 [1024], P(('dp', 'expert'))
- grad_bias_table: float32 [512], P(('dp', 'expert'))
- grad_gate_weight: float32 [4, 1024, 2816], P('expert', 'dp')
- grad_up_weight: float32 [4, 1024, 2816], P('expert', 'dp')
- grad_down_weight: float32 [4, 2816, 1024], P('expert', 'dp')
Inputs may be any that keep to these rules, and one draw needn't show every extreme that they name: The lengths of the 4 sequences of one group sum to 768, and one of them is 256. `routes`: A slot's two experts differ. Among the 256 slots of one device no expert is named more than 256 times; on some device one expert is named exactly 256 times. `priority`: each row is a permutation.
All inputs are finite; a program needn't handle non-finite values.
Results may differ from a plain program's by a relative error of at most 0.02.
Values may be sent and summed in bfloat16 or wider, within the bound.
A program may use at most 192 MiB of HBM per device.

v0:
```python
import math

import jax
import jax.numpy as jnp
import numpy as np
from jax import lax
from jax.sharding import PartitionSpec as P

HEADS = 16
HD = 64
BUCKETS = 32
CAP = 480


epsilon = 1e-06
masked_value = -1e30
max_distance = 128.0
block_rows = 512
largest_value = lax.Precision.HIGHEST


def bucket_table(seq_slots, bucket_count):
    halfway = bucket_count // 2
    exact_span = bucket_count // 4
    offset = np.arange(seq_slots)[:, None] - np.arange(seq_slots)[None, :]
    distance = np.abs(offset)
    log_part = np.log(np.maximum(distance, 1) / float(exact_span)) / np.log(
        max_distance / exact_span
    )
    far_bucket = np.minimum(
        exact_span + np.floor(log_part * exact_span).astype(np.int64), halfway - 1
    )
    inside = np.where(distance < exact_span, distance, far_bucket)
    return (np.where(offset < 0, halfway, 0) + inside).astype(np.int32)


def bucket_onehot(bucket_rows, bucket_count):
    return (
        jnp.asarray(bucket_rows)[None, :, :]
        == jnp.arange(bucket_count, dtype=jnp.int32)[:, None, None]
    ).astype(jnp.bfloat16)


def take_rows(matrix_in, row_index):
    padded = jnp.concatenate([matrix_in, jnp.zeros((1, matrix_in.shape[1]), matrix_in.dtype)])
    return padded[row_index]


def into_slots(pair_rows, row_index, slot_total):
    return (
        jnp.zeros((slot_total, pair_rows.shape[1]), pair_rows.dtype)
        .at[row_index]
        .set(pair_rows, mode="drop")
    )


def gelu_tanh(value_in):
    return jax.nn.gelu(value_in, approximate=True)


def on_device(
    tokens,
    cotangent,
    qkv_weight,
    out_weight,
    router_weight,
    first_gain,
    second_gain,
    bias_table,
    gate_weight,
    up_weight,
    down_weight,
    lengths,
    routes,
    priority,
):
    seq_slots, model_width = tokens.shape
    head_count = HEADS
    head_size = HD
    expert_count = lax.axis_size("expert")
    slot_count = min(seq_slots, 4 * seq_slots // expert_count)
    slot_total = expert_count * slot_count
    group_tokens = expert_count * seq_slots
    capacity = CAP
    block_size = min(seq_slots, block_rows)
    score_scale = 1.0 / math.sqrt(head_size)
    qkv_full, out_full, router_full, first_full, second_full, position_bias_matrix = (
        lax.all_gather(qkv_weight, ("dp", "expert"), axis=0, tiled=True),
        lax.all_gather(out_weight, ("dp", "expert"), axis=0, tiled=True),
        lax.all_gather(router_weight, ("dp", "expert"), axis=0, tiled=True),
        lax.all_gather(first_gain, ("dp", "expert"), axis=0, tiled=True),
        lax.all_gather(second_gain, ("dp", "expert"), axis=0, tiled=True),
        lax.all_gather(bias_table, ("dp", "expert"), axis=0, tiled=True),
    )
    gate_full, up_full, down_full = (
        lax.all_gather(gate_weight, "dp", axis=1, tiled=True),
        lax.all_gather(up_weight, "dp", axis=1, tiled=True),
        lax.all_gather(down_weight, "dp", axis=1, tiled=True),
    )
    group_routes, group_rank, group_lengths = (
        lax.all_gather(routes, "expert", axis=0, tiled=True),
        lax.all_gather(priority[0], "expert", axis=0, tiled=True),
        lax.all_gather(lengths[0], "expert", axis=0, tiled=True),
    )
    own_index = lax.axis_index("expert")
    group_slot = jnp.arange(group_tokens, dtype=jnp.int32) % seq_slots
    group_valid = group_slot < jnp.repeat(group_lengths, seq_slots)
    inverse = (
        jnp.zeros((group_tokens,), jnp.int32)
        .at[group_rank]
        .set(jnp.arange(group_tokens, dtype=jnp.int32))
    )
    order_routes = jnp.concatenate([group_routes[inverse, 0], group_routes[inverse, 1]])
    order_valid = jnp.concatenate([group_valid[inverse], group_valid[inverse]])
    expert_range = jnp.arange(expert_count, dtype=jnp.int32)
    order_onehot = ((order_routes[:, None] == expert_range[None, :]) & order_valid[:, None]).astype(
        jnp.int32
    )
    earlier = jnp.cumsum(order_onehot, axis=0) - order_onehot
    order_pos = jnp.sum(earlier * order_onehot, axis=1)
    own_rank = lax.dynamic_slice_in_dim(group_rank, own_index * seq_slots, seq_slots)
    positions = jnp.stack([order_pos[own_rank], order_pos[group_tokens + own_rank]], axis=1)
    valid_rows = jnp.arange(seq_slots, dtype=jnp.int32) < lengths[0, 0]
    valid_float = valid_rows.astype(jnp.float32)
    kept_mask = valid_rows[:, None] & (positions < capacity)
    kept_float = kept_mask.astype(jnp.float32)
    pair_routes = routes.reshape(-1)
    pair_kept = kept_mask.reshape(-1)
    pair_onehot = ((pair_routes[:, None] == expert_range[None, :]) & pair_kept[:, None]).astype(
        jnp.int32
    )
    local_slot = jnp.sum((jnp.cumsum(pair_onehot, axis=0) - pair_onehot) * pair_onehot, axis=1)
    dispatch_index = jnp.where(pair_kept, pair_routes * slot_count + local_slot, slot_total)
    send_pos = (
        jnp.full((slot_total,), capacity, jnp.int32)
        .at[dispatch_index]
        .set(positions.reshape(-1), mode="drop")
    )
    x_float = tokens.astype(jnp.float32)
    inv_one = lax.rsqrt(jnp.mean(x_float * x_float, axis=1, keepdims=True) + epsilon)
    unit_one = x_float * inv_one
    first_float = first_full.astype(jnp.float32)
    normed = (unit_one * first_float).astype(jnp.bfloat16)
    qkv_rows = jnp.dot(normed, qkv_full, preferred_element_type=jnp.float32).astype(jnp.bfloat16)
    queries = qkv_rows[:, :model_width].reshape(seq_slots, head_count, head_size)
    keys_all = qkv_rows[:, model_width : 2 * model_width].reshape(seq_slots, head_count, head_size)
    values_all = qkv_rows[:, 2 * model_width :].reshape(seq_slots, head_count, head_size)
    bucket_rows = bucket_table(seq_slots, BUCKETS)
    per_head_bias = position_bias_matrix.reshape(head_count, BUCKETS)

    def block_scores(row_start, query_block):
        indicator_matrix = bucket_onehot(bucket_rows[row_start : row_start + block_size], BUCKETS)
        bias_block = jnp.einsum(
            "crd,wc->wrd", indicator_matrix, per_head_bias, preferred_element_type=jnp.float32
        )
        raw_scores = (
            jnp.einsum("qhd,khd->hqk", query_block, keys_all, preferred_element_type=jnp.float32)
            * score_scale
            + bias_block
        )
        return (jnp.where(valid_rows[None, None, :], raw_scores, masked_value), indicator_matrix)

    row_start = 0
    query_block = queries
    scores, indicator_matrix = block_scores(row_start, query_block)
    row_max = jnp.max(scores, axis=2, keepdims=True)
    exponent = jnp.exp(scores - row_max)
    row_total = jnp.sum(exponent, axis=2, keepdims=True)
    attn_probs = (exponent / row_total).astype(jnp.bfloat16)
    lse_parts = [row_max + jnp.log(row_total)]
    attended_parts = jnp.einsum(
        "hqk,khd->qhd", attn_probs, values_all, preferred_element_type=jnp.float32
    ).reshape(block_size, model_width)
    attended = attended_parts.astype(jnp.bfloat16)
    branch = jnp.dot(attended, out_full, preferred_element_type=jnp.float32)
    residual = x_float + branch
    inv_two = lax.rsqrt(jnp.mean(residual * residual, axis=1, keepdims=True) + epsilon)
    unit_two = residual * inv_two
    second_float = second_full.astype(jnp.float32)
    normed_two = (unit_two * second_float).astype(jnp.bfloat16)
    logits = jnp.dot(normed_two, router_full, preferred_element_type=jnp.float32)
    picker = (routes[:, :, None] == expert_range[None, None, :]).astype(jnp.float32)
    chosen = jnp.einsum("se,sje->sj", logits, picker, precision=largest_value)
    gate_probs = jax.nn.softmax(chosen, axis=1)
    weights_pair = kept_float * gate_probs
    pair_rows = jnp.repeat(normed_two, 2, axis=0)
    send_rows = into_slots(pair_rows, dispatch_index, slot_total).reshape(
        expert_count, slot_count, model_width
    )
    recv_rows, recv_pos = (
        lax.all_to_all(send_rows, "expert", split_axis=0, concat_axis=0, tiled=True),
        lax.all_to_all(
            send_pos.reshape(expert_count, slot_count),
            "expert",
            split_axis=0,
            concat_axis=0,
            tiled=True,
        ),
    )
    flat_pos = recv_pos.reshape(-1)
    buffer = (
        jnp.zeros((capacity, model_width), jnp.bfloat16)
        .at[flat_pos]
        .set(recv_rows.reshape(-1, model_width), mode="drop")
    )
    gate_matrix = gate_full[0]
    up_matrix = up_full[0]
    down_matrix = down_full[0]
    gate_in = jnp.dot(buffer, gate_matrix, preferred_element_type=jnp.float32)
    up_in = jnp.dot(buffer, up_matrix, preferred_element_type=jnp.float32)
    activated = gelu_tanh(gate_in)
    hidden = (activated * up_in).astype(jnp.bfloat16)
    expert_out = jnp.dot(hidden, down_matrix, preferred_element_type=jnp.float32).astype(
        jnp.bfloat16
    )
    out_slots = take_rows(expert_out, flat_pos).reshape(expert_count, slot_count, model_width)
    returned = lax.all_to_all(out_slots, "expert", split_axis=0, concat_axis=0, tiled=True)
    pair_out = take_rows(returned.reshape(-1, model_width), dispatch_index).reshape(
        seq_slots, 2, model_width
    )
    expert_mix = weights_pair[:, 0:1] * pair_out[:, 0].astype(jnp.float32) + weights_pair[
        :, 1:2
    ] * pair_out[:, 1].astype(jnp.float32)
    output = (valid_float[:, None] * (residual + expert_mix)).astype(jnp.bfloat16)
    grad_resid0 = valid_float[:, None] * cotangent.astype(jnp.float32)
    grad_pair = (
        (weights_pair[:, :, None] * grad_resid0[:, None, :])
        .astype(jnp.bfloat16)
        .reshape(2 * seq_slots, model_width)
    )
    grad_slots = into_slots(grad_pair, dispatch_index, slot_total).reshape(
        expert_count, slot_count, model_width
    )
    grad_recv = lax.all_to_all(grad_slots, "expert", split_axis=0, concat_axis=0, tiled=True)
    grad_expert_out = (
        jnp.zeros((capacity, model_width), jnp.bfloat16)
        .at[flat_pos]
        .set(grad_recv.reshape(-1, model_width), mode="drop")
    )
    grad_gates = kept_float * jnp.stack(
        [
            jnp.sum(grad_resid0 * pair_out[:, 0].astype(jnp.float32), axis=1),
            jnp.sum(grad_resid0 * pair_out[:, 1].astype(jnp.float32), axis=1),
        ],
        axis=1,
    )
    grad_chosen = gate_probs * (
        grad_gates - jnp.sum(gate_probs * grad_gates, axis=1, keepdims=True)
    )
    grad_logits = jnp.einsum("sj,sje->se", grad_chosen, picker, precision=largest_value)
    grad_router = jnp.einsum(
        "sd,se->de", normed_two.astype(jnp.float32), grad_logits, precision=largest_value
    )
    grad_hidden = jnp.dot(grad_expert_out, down_matrix.T, preferred_element_type=jnp.float32)
    grad_down_local = jnp.dot(hidden.T, grad_expert_out, preferred_element_type=jnp.float32)
    gelu_pull = jax.vjp(gelu_tanh, gate_in)[1]
    grad_gate_in = gelu_pull(grad_hidden * up_in)[0].astype(jnp.bfloat16)
    grad_up_in = (grad_hidden * activated).astype(jnp.bfloat16)
    grad_buffer = (
        jnp.dot(grad_gate_in, gate_matrix.T, preferred_element_type=jnp.float32)
        + jnp.dot(grad_up_in, up_matrix.T, preferred_element_type=jnp.float32)
    ).astype(jnp.bfloat16)
    grad_gate_local = jnp.dot(buffer.T, grad_gate_in, preferred_element_type=jnp.float32)
    grad_up_local = jnp.dot(buffer.T, grad_up_in, preferred_element_type=jnp.float32)
    expert_shares = (
        lax.psum_scatter(
            grad_gate_local[None].astype(jnp.bfloat16), "dp", scatter_dimension=1, tiled=True
        ).astype(jnp.float32),
        lax.psum_scatter(
            grad_up_local[None].astype(jnp.bfloat16), "dp", scatter_dimension=1, tiled=True
        ).astype(jnp.float32),
        lax.psum_scatter(
            grad_down_local[None].astype(jnp.bfloat16), "dp", scatter_dimension=1, tiled=True
        ).astype(jnp.float32),
    )
    back_slots = take_rows(grad_buffer, flat_pos).reshape(expert_count, slot_count, model_width)
    grad_home = lax.all_to_all(back_slots, "expert", split_axis=0, concat_axis=0, tiled=True)
    grad_pair_in = take_rows(grad_home.reshape(-1, model_width), dispatch_index).reshape(
        seq_slots, 2, model_width
    )
    grad_normed_two = (
        grad_pair_in[:, 0].astype(jnp.float32)
        + grad_pair_in[:, 1].astype(jnp.float32)
        + jnp.dot(grad_logits, router_full.astype(jnp.float32).T, precision=largest_value)
    )
    scaled_two = second_float * grad_normed_two
    grad_second = jnp.sum(grad_normed_two * unit_two, axis=0)
    grad_resid = grad_resid0 + inv_two * (
        scaled_two - unit_two * jnp.mean(scaled_two * unit_two, axis=1, keepdims=True)
    )
    grad_branch = grad_resid.astype(jnp.bfloat16)
    grad_out = jnp.dot(attended.T, grad_branch, preferred_element_type=jnp.float32)
    grad_attended = (
        jnp.dot(grad_branch, out_full.T, preferred_element_type=jnp.float32)
        .astype(jnp.bfloat16)
        .reshape(seq_slots, head_count, head_size)
    )
    grad_keys = jnp.zeros((seq_slots, head_count, head_size), jnp.float32)
    grad_values = jnp.zeros((seq_slots, head_count, head_size), jnp.float32)
    grad_bias = jnp.zeros((head_count, BUCKETS), jnp.float32)
    grad_query_parts = []
    for block_index, row_start in enumerate(range(0, seq_slots, block_size)):
        query_block = queries
        scores, indicator_matrix = block_scores(row_start, query_block)
        attn_probs = jnp.exp(scores - lse_parts[block_index])
        grad_probs = jnp.einsum(
            "qhd,khd->hqk", grad_attended, values_all, preferred_element_type=jnp.float32
        )
        score_gradient = (
            attn_probs * (grad_probs - jnp.sum(attn_probs * grad_probs, axis=2, keepdims=True))
        ).astype(jnp.bfloat16)
        grad_bias = grad_bias + jnp.einsum(
            "lyv,oyv->ol", indicator_matrix, score_gradient, preferred_element_type=jnp.float32
        )
        grad_query_parts.append(
            jnp.einsum("hqk,khd->qhd", score_gradient, keys_all, preferred_element_type=jnp.float32)
            * score_scale
        )
        grad_keys = (
            grad_keys
            + jnp.einsum(
                "hqk,qhd->khd", score_gradient, query_block, preferred_element_type=jnp.float32
            )
            * score_scale
        )
        grad_values = grad_values + jnp.einsum(
            "hqk,qhd->khd",
            attn_probs.astype(jnp.bfloat16),
            grad_attended,
            preferred_element_type=jnp.float32,
        )
    grad_queries = jnp.concatenate(grad_query_parts, axis=0)
    grad_qkv = jnp.concatenate(
        [
            grad_queries.reshape(seq_slots, model_width),
            grad_keys.reshape(seq_slots, model_width),
            grad_values.reshape(seq_slots, model_width),
        ],
        axis=1,
    ).astype(jnp.bfloat16)
    grad_qkv_full = jnp.dot(normed.T, grad_qkv, preferred_element_type=jnp.float32)
    grad_normed = jnp.dot(grad_qkv, qkv_full.T, preferred_element_type=jnp.float32)
    scaled_one = first_float * grad_normed
    grad_first = jnp.sum(grad_normed * unit_one, axis=0)
    grad_tokens = grad_resid + inv_one * (
        scaled_one - unit_one * jnp.mean(scaled_one * unit_one, axis=1, keepdims=True)
    )
    grad_bias_flat = grad_bias.reshape(-1)
    dense_shares = (
        lax.psum_scatter(grad_qkv_full, ("dp", "expert"), scatter_dimension=0, tiled=True),
        lax.psum_scatter(grad_out, ("dp", "expert"), scatter_dimension=0, tiled=True),
        lax.psum_scatter(grad_router, ("dp", "expert"), scatter_dimension=0, tiled=True),
        lax.psum_scatter(grad_first, ("dp", "expert"), scatter_dimension=0, tiled=True),
        lax.psum_scatter(grad_second, ("dp", "expert"), scatter_dimension=0, tiled=True),
        lax.psum_scatter(grad_bias_flat, ("dp", "expert"), scatter_dimension=0, tiled=True),
    )
    return (
        output,
        grad_tokens,
        dense_shares[0],
        dense_shares[1],
        dense_shares[2],
        dense_shares[3],
        dense_shares[4],
        dense_shares[5],
        expert_shares[0],
        expert_shares[1],
        expert_shares[2],
    )


def solution(mesh):
    placed = (
        P(("dp", "expert"), None),
        P(("dp", "expert"), None),
        P(("dp", "expert"), None),
        P(("dp", "expert"), None),
        P(("dp", "expert"), None),
        P(("dp", "expert")),
        P(("dp", "expert")),
        P(("dp", "expert")),
        P("expert", "dp", None),
        P("expert", "dp", None),
        P("expert", "dp", None),
        P("dp", "expert"),
        P(("dp", "expert"), None),
        P("dp", "expert"),
    )
    return jax.shard_map(
        on_device,
        mesh=mesh,
        in_specs=placed,
        out_specs=(
            P(("dp", "expert"), None),
            P(("dp", "expert"), None),
            P(("dp", "expert"), None),
            P(("dp", "expert"), None),
            P(("dp", "expert"), None),
            P(("dp", "expert")),
            P(("dp", "expert")),
            P(("dp", "expert")),
            P("expert", "dp", None),
            P("expert", "dp", None),
            P("expert", "dp", None),
        ),
        check_vma=False,
    )
```

profile of v0, /device:TPU:0, one launch (start us, length us, event | category | flops | bytes accessed | tf_op | source)
XLA Modules:
  0.0 1094.3 jit_solution(12365729136593654304)
XLA Ops:
  10.6 9.6 all_gather.40
  23.9 7.3 all-reduce.8
  31.2 7.2 all-gather
  38.5 4.3 scatter_custom_fusion
  42.8 6.8 gather_fusion.2
  49.6 9.1 gather_fusion.1
  58.8 9.1 gather_fusion
  79.7 3.2 all-to-all-start
  83.7 41.6 %all-reduce.14 = (bf16[1024]{0:T(1024)(128)(2,1)S(1)}, bf16[512]{0:T(512)(128)(2,1)S(1)}, bf16[1024]{0:T(1024)(128)(2,1)S(1)}) all-reduce(bf16[1024]{0:T(1024)(128)(2,1)S(1)} %dynamic-update-slice, bf16[512]{0:T(512)(128)(2,1)S(1)} %dynamic-update-slice.1, ...), channel_id=1, replica_groups=mesh['dp'=8,'expert'=4] {'dp','expert'}, use_global_device_ids=true, to_apply=%add.6 | all-reduce | flops 2560 | bytes 10240
  126.6 11.5 %copy.71 = pred[32,256,256]{2,0,1:T(32,128)(4,1)S(1)} copy(pred[32,256,256]{1,0,2:T(32,128)(4,1)S(1)} %iota_compare_fusion) | data formatting | bytes 4194304 | tf_op jit(solution)/shard_map/eq | solution.py:39
  141.1 5.5 copy.72
  146.8 5.1 convolution_convert_fusion
  152.7 3.4 fusion.108
  164.4 4.8 scatter_custom_fusion.2
  169.2 3.8 all-to-all-start.1
  173.0 23.9 %all-to-all-done.1 = bf16[4,256,1024]{2,1,0:T(8,128)(2,1)S(1)} async-done(((bf16[4,256,1024]{2,1,0:T(8,128)(2,1)}), bf16[4,256,1024]{2,1,0:T(8,128)(2,1)S(1)}, u32[]{:S(2)}, u32[]{:S(2)}) %all-to-all-start.1) | async-done | bytes 2097184 | tf_op jit(solution)/shard_map/all_to_all | solution.py:191
  196.9 6.2 scatter_custom_fusion.3
  203.1 8.4 fusion.10
  211.6 51.1 %all-gather.15.cloned.1.call-done = bf16[1,1024,2816]{2,1,0:T(8,128)(2,1)} async-done(((bf16[1,128,2816]{2,1,0:T(8,128)(2,1)}), bf16[1,1024,2816]{2,1,0:T(8,128)(2,1)}) %all-gather.15.cloned.1.call-update) | async-done | bytes 5767184 | tf_op jit(solution)/shard_map/all_gather | solution.py:97
  262.6 8.7 multiply_convert_fusion.1
  271.3 51.9 %all-gather.17.cloned.1.call-done = bf16[1,2816,1024]{2,1,0:T(8,128)(2,1)} async-done(((bf16[1,352,1024]{2,1,0:T(8,128)(2,1)}), bf16[1,2816,1024]{2,1,0:T(8,128)(2,1)}) %all-gather.17.cloned.1.call-update) | async-done | bytes 5767184 | tf_op jit(solution)/shard_map/all_gather | solution.py:98
  323.3 6.4 fusion.33
  329.7 5.4 gather_fusion.5
  335.1 3.8 all-to-all-start.2
  338.9 83.4 %all-gather.2 = bf16[32,32,4]{1,2,0:T(4,128)(2,1)S(1)} all-gather(bf16[1,32,4]{1,2,0:T(4,128)(2,1)S(1)} %bitcast.243), channel_id=1, replica_groups=mesh['dp'=8,'expert'=4] {'dp','expert'}, dimensions={0}, use_global_device_ids=true | all-gather | bytes 8448 | tf_op jit(solution)/shard_map/all_gather | solution.py:90
  438.1 3.7 mul.302
  441.7 5.2 scatter_custom_fusion.4
  446.9 4.6 all-to-all-start.3
  454.4 19.3 %all-to-all-done.3 = bf16[4,256,1024]{2,1,0:T(8,128)(2,1)} async-done(((bf16[4,256,1024]{2,1,0:T(8,128)(2,1)}), bf16[4,256,1024]{2,1,0:T(8,128)(2,1)}, u32[]{:S(2)}, u32[]{:S(2)}) %all-to-all-start.3) | async-done | bytes 2097184 | tf_op jit(solution)/shard_map/all_to_all | solution.py:234
  473.7 6.3 scatter_custom_fusion.5
  480.0 6.9 convert_bitcast_fusion
  487.0 12.3 %fusion.18 = (bf16[480,2816]{1,0:T(8,128)(2,1)S(1)}, bf16[480,2816]{1,0:T(8,128)(2,1)}) fusion(f32[480,2816]{1,0:T(8,128)} %fusion.10, f32[480,2816]{1,0:T(8,128)} %get-tuple-element.57, bf16[480,1024]{1,0:T(8,128)(2,1)S(1)} %scatter_custom_fusion.5, bf16[1,2816,1024]{2,1,0:T(8,128)(2,1)} %all-gather.17.cloned.1.call-done), kind=kOutput, calls=%fused_computation.39 | convolution fusion | flops 2800680960 | bytes 22970368 | tf_op jit(solution)/shard_map/dot_general | solution.py:254
  500.9 5.0 convert_bitcast_fusion.2
  506.0 7.0 convert_bitcast_fusion.1
  513.0 6.0 fusion.4
  519.1 5.6 add_convert_fusion
  524.8 5.4 gather_fusion.7
  530.1 3.6 all-to-all-start.4
  533.8 25.2 %all-to-all-done.4 = bf16[4,256,1024]{2,1,0:T(8,128)(2,1)S(1)} async-done(((bf16[4,256,1024]{2,1,0:T(8,128)(2,1)}), bf16[4,256,1024]{2,1,0:T(8,128)(2,1)S(1)}, u32[]{:S(2)}, u32[]{:S(2)}) %all-to-all-start.4) | async-done | bytes 2097184 | tf_op jit(solution)/shard_map/all_to_all | solution.py:277
  576.3 3.4 multiply_reduce_fusion
  583.7 6.6 fusion.63
  593.8 5.2 fusion.56
  599.1 38.8 %all-reduce.13 = (f32[1024]{0:T(1024)S(1)}, f32[1024]{0:T(1024)S(1)}, f32[512]{0:T(512)S(1)}) all-reduce(f32[1024]{0:T(1024)S(1)} %get-tuple-element.13, f32[1024]{0:T(1024)S(1)} %get-tuple-element.11, f32[512]{0:T(512)S(1)} %reshape.385), channel_id=7, replica_groups=mesh['dp'=8,'expert'=4] {'dp','expert'}, use_global_device_ids=true, to_apply=%region_28.29.clone | all-reduce | flops 2560 | bytes 20480
  640.9 11.4 %reduce-scatter.17.cloned.1.call-done = bf16[1,352,1024]{2,1,0:T(8,128)(2,1)} async-done(((bf16[1,2816,1024]{2,1,0:T(8,128)(2,1)}), bf16[1,352,1024]{2,1,0:T(8,128)(2,1)}) %reduce-scatter.17.cloned.1.call-update) | async-done | bytes 720912 | tf_op jit(solution)/shard_map/reduce_scatter | solution.py:272
  654.6 63.3 %reduce-scatter.13.cloned.1.call-done = bf16[1,128,2816]{2,1,0:T(8,128)(2,1)} async-done(((bf16[1,1024,2816]{2,1,0:T(8,128)(2,1)}), bf16[1,128,2816]{2,1,0:T(8,128)(2,1)}) %reduce-scatter.13.cloned.1.call-update) | async-done | bytes 720912 | tf_op jit(solution)/shard_map/reduce_scatter | solution.py:266
  720.2 63.4 %reduce-scatter.15.cloned.1.call-done = bf16[1,128,2816]{2,1,0:T(8,128)(2,1)} async-done(((bf16[1,1024,2816]{2,1,0:T(8,128)(2,1)}), bf16[1,128,2816]{2,1,0:T(8,128)(2,1)}) %reduce-scatter.15.cloned.1.call-update) | async-done | bytes 720912 | tf_op jit(solution)/shard_map/reduce_scatter | solution.py:269
  785.9 140.0 %reduce-scatter.11.cloned.1.call-done = f32[32,1024]{1,0:T(8,128)} async-done(((f32[1024,1024]{1,0:T(8,128)}), f32[32,1024]{1,0:T(8,128)}) %reduce-scatter.11.cloned.1.call-update) | async-done | bytes 131088 | tf_op jit(solution)/shard_map/reduce_scatter | solution.py:351
  925.9 161.4 %reduce-scatter.9.cloned.1.call-done = f32[32,3072]{1,0:T(8,128)} async-done(((f32[1024,3072]{1,0:T(8,128)}), f32[32,3072]{1,0:T(8,128)}) %reduce-scatter.9.cloned.1.call-update) | async-done | bytes 393232 | tf_op jit(solution)/shard_map/reduce_scatter | solution.py:350
  (237 shorter events, 87.3 us)
Async XLA Ops:
  7.2 139.6 %all-gather.9.cloned.1.call-start = ((), (), s32[]{:S(2)}) async-start(), calls=%async_computation.11 | async-start | bytes 6488064 | tf_op jit(solution)/shard_map/all_gather | solution.py:88
  7.9 151.1 %all-gather.11.cloned.1.call-start = ((), (), s32[]{:S(2)}) async-start(), calls=%async_computation.12 | async-start | bytes 2162688 | tf_op jit(solution)/shard_map/all_gather | solution.py:89
  8.7 194.5 %all-gather.13.cloned.1.call-start = ((), (), s32[]{:S(2)}) async-start(), calls=%async_computation.13 | async-start | bytes 6488064 | tf_op jit(solution)/shard_map/all_gather | solution.py:96
  9.4 253.2 %all-gather.15.cloned.1.call-start = ((), (), s32[]{:S(2)}) async-start(), calls=%async_computation.14 | async-start | bytes 6488064 | tf_op jit(solution)/shard_map/all_gather | solution.py:97
  10.0 313.3 %all-gather.17.cloned.1.call-start = ((), (), s32[]{:S(2)}) async-start(), calls=%async_computation.15 | async-start | bytes 6488064 | tf_op jit(solution)/shard_map/all_gather | solution.py:98
  58.7 15.9 %copy-start.32 = (s32[256,2]{0,1:T(2,128)S(1)}, s32[256,2]{0,1:T(2,128)}, u32[]{:S(2)}) copy-start(s32[256,2]{0,1:T(2,128)} %param.28) | copy-start | bytes 6148
  58.7 24.3 %copy-start.34 = (bf16[32]{0:T(256)(128)(2,1)S(1)}, bf16[32]{0:T(256)(128)(2,1)}, u32[]{:S(2)}) copy-start(bf16[32]{0:T(256)(128)(2,1)} %param.21) | copy-start | bytes 196
  58.7 24.5 %copy-start.35 = (bf16[32]{0:T(256)(128)(2,1)S(1)}, bf16[32]{0:T(256)(128)(2,1)}, u32[]{:S(2)}) copy-start(bf16[32]{0:T(256)(128)(2,1)} %param.22) | copy-start | bytes 196
  58.8 24.7 %copy-start.36 = (bf16[16]{0:T(256)(128)(2,1)S(1)}, bf16[16]{0:T(256)(128)(2,1)}, u32[]{:S(2)}) copy-start(bf16[16]{0:T(256)(128)(2,1)} %param.23) | copy-start | bytes 100
  58.8 66.6 %copy-start.30 = (s32[256,256]{0,1:T(8,128)S(1)}, s32[256,256]{0,1:T(8,128)}, u32[]{:S(2)}) copy-start(s32[256,256]{0,1:T(8,128)} %constant.92.clone) | copy-start | bytes 786436
  79.7 89.5 %all-to-all-start = ((s32[4,1,256]{2,1,0:T(1,128)}), s32[4,1,256]{2,1,0:T(1,128)S(1)}, u32[]{:S(2)}, u32[]{:S(2)}) async-start(s32[4,1,256]{2,1,0:T(1,128)} %bitcast.22), calls=%async_computation | async-start | bytes 8192 | tf_op jit(solution)/shard_map/all_to_all | solution.py:192
  141.1 5.5 copy-start.8
  152.2 3.9 copy-start.14
  152.4 3.7 copy-start.16
  152.7 4.1 copy-start.20
  156.1 2.0 copy-start
  159.0 5.4 copy-start.24
  169.2 27.7 %all-to-all-start.1 = ((bf16[4,256,1024]{2,1,0:T(8,128)(2,1)}), bf16[4,256,1024]{2,1,0:T(8,128)(2,1)S(1)}, u32[]{:S(2)}, u32[]{:S(2)}) async-start(bf16[4,256,1024]{2,1,0:T(8,128)(2,1)} %bitcast.25), calls=%async_computation.1 | async-start | bytes 4194304 | tf_op jit(solution)/shard_map/all_to_all | solution.py:191
  203.1 59.5 %copy-start.28 = (bf16[480,1024]{1,0:T(8,128)(2,1)S(1)}, bf16[480,1024]{1,0:T(8,128)(2,1)}, u32[]{:S(2)}) copy-start(bf16[480,1024]{1,0:T(8,128)(2,1)} %scatter_custom_fusion.3) | copy-start | bytes 2949124
  335.1 3.8 copy-start.33
  335.1 90.2 %all-to-all-start.2 = ((bf16[4,256,1024]{2,1,0:T(8,128)(2,1)}), bf16[4,256,1024]{2,1,0:T(8,128)(2,1)S(1)}, u32[]{:S(2)}, u32[]{:S(2)}) async-start(bf16[4,256,1024]{2,1,0:T(8,128)(2,1)} %bitcast.192), calls=%async_computation.2 | async-start | bytes 4194304 | tf_op jit(solution)/shard_map/all_to_all | solution.py:217
  432.6 2.5 copy-start.26
  434.2 7.6 copy-start.4
  446.9 5.9 copy-start.13
  446.9 26.8 %all-to-all-start.3 = ((bf16[4,256,1024]{2,1,0:T(8,128)(2,1)}), bf16[4,256,1024]{2,1,0:T(8,128)(2,1)}, u32[]{:S(2)}, u32[]{:S(2)}) async-start(bf16[4,256,1024]{2,1,0:T(8,128)(2,1)} %bitcast.195), calls=%async_computation.3 | async-start | bytes 4194304 | tf_op jit(solution)/shard_map/all_to_all | solution.py:234
  451.5 138.8 %reduce-scatter.19.cloned.1.call-start = ((), (), s32[]{:S(2)}) async-start(), calls=%async_computation.21 | async-start | bytes 540672
  454.4 197.9 %reduce-scatter.17.cloned.1.call-start = ((), (), s32[]{:S(2)}) async-start(), calls=%async_computation.20 | async-start | bytes 6488064 | tf_op jit(solution)/shard_map/reduce_scatter | solution.py:272
  487.0 231.0 %reduce-scatter.13.cloned.1.call-start = ((), (), s32[]{:S(2)}) async-start(), calls=%async_computation.18 | async-start | bytes 6488064 | tf_op jit(solution)/shard_map/reduce_scatter | solution.py:266
  487.0 13.9 %copy-start.29 = (bf16[480,1024]{1,0:T(8,128)(2,1)S(1)}, bf16[480,1024]{1,0:T(8,128)(2,1)}, u32[]{:S(2)}) copy-start(bf16[480,1024]{1,0:T(8,128)(2,1)} %scatter_custom_fusion.3) | copy-start | bytes 2949124
  499.3 1.5 copy-start.37
  505.9 277.7 %reduce-scatter.15.cloned.1.call-start = ((), (), s32[]{:S(2)}) async-start(), calls=%async_computation.19 | async-start | bytes 6488064 | tf_op jit(solution)/shard_map/reduce_scatter | solution.py:269
  513.0 6.0 copy-start.38
  530.1 28.9 %all-to-all-start.4 = ((bf16[4,256,1024]{2,1,0:T(8,128)(2,1)}), bf16[4,256,1024]{2,1,0:T(8,128)(2,1)S(1)}, u32[]{:S(2)}, u32[]{:S(2)}) async-start(bf16[4,256,1024]{2,1,0:T(8,128)(2,1)} %bitcast.193), calls=%async_computation.4 | async-start | bytes 4194304 | tf_op jit(solution)/shard_map/all_to_all | solution.py:277
  533.7 392.1 %reduce-scatter.11.cloned.1.call-start = ((), (), s32[]{:S(2)}) async-start(), calls=%async_computation.17 | async-start | bytes 4325376 | tf_op jit(solution)/shard_map/reduce_scatter | solution.py:351
  566.3 2.7 copy-start.5
  566.4 2.7 copy-start.7
  566.4 2.7 copy-start.27
  567.9 2.7 copy-start.25
  570.6 3.1 copy-start.2
  573.4 2.9 copy-start.21
  573.4 513.9 %reduce-scatter.9.cloned.1.call-start = ((), (), s32[]{:S(2)}) async-start(), calls=%async_computation.16 | async-start | bytes 12976128 | tf_op jit(solution)/shard_map/reduce_scatter | solution.py:350
  576.3 3.5 copy-start.1
  579.7 1.8 copy-start.15
  581.6 1.3 copy-start.22
  581.6 2.1 copy-start.9
  590.2 1.5 copy-start.31
  590.3 3.6 copy-start.19
  593.8 45.8 %copy-start.3 = (f32[256,1024]{1,0:T(8,128)S(1)}, f32[256,1024]{1,0:T(8,128)}, u32[]{:S(2)}) copy-start(f32[256,1024]{1,0:T(8,128)} %copy-done.2) | copy-start | bytes 3145732
  (7 other events, 7.1 us)
Sparse Core Ops, SparseCore 0:
  10.9 72.2 all-gather.8
  86.1 54.9 all-gather.10
  142.7 59.2 all-gather.12
  203.5 59.0 all-gather.14
  264.1 59.0 all-gather.16
  454.5 133.2 reduce-scatter.18
  590.2 62.0 reduce-scatter.16
  654.7 63.2 reduce-scatter.12
  720.3 63.2 reduce-scatter.14
  786.4 139.4 reduce-scatter.10
  933.5 153.7 reduce-scatter.8
where the time goes:
time: 1100 us; the launch traced here: 1090 us
  waiting for transfers between devices  614 us (56%)
  blocking collectives  188 us (17%)
  local copies, waits for them, and re-layouts  122 us (11%)
  matrix products  111 us (10%)
  other arithmetic  23.2 us (2%)
  starting transfers between devices  19.7 us (2%)
  between operations  16 us (1%)
    reduce_scatter x1, waiting for transfers between devices, on_device(): lax.psum_scatter(grad_qkv_full, ('dp', 'expert'), scatter_dimension=0, ti...  161 us
    reduce_scatter x1, waiting for transfers between devices, on_device(): lax.psum_scatter(grad_out, ('dp', 'expert'), scatter_dimension=0, tiled=T...  140 us
    unnamed x3, blocking collectives  87.6 us
    all_gather x1, blocking collectives, on_device(): lax.all_gather(router_weight, ('dp', 'expert'), axis=0, tiled=True)  83.4 us
    reduce_scatter x1, waiting for transfers between devices, on_device(): lax.psum_scatter(grad_up_local[None].astype(jnp.bfloat16), 'dp', scatter_...  63.4 us
    reduce_scatter x1, waiting for transfers between devices, on_device(): lax.psum_scatter(grad_gate_local[None].astype(jnp.bfloat16), 'dp', scatte...  63.3 us
    all_gather x1, waiting for transfers between devices, on_device(): lax.all_gather(down_weight, 'dp', axis=1, tiled=True)  51.9 us
    all_gather x1, waiting for transfers between devices, on_device(): lax.all_gather(up_weight, 'dp', axis=1, tiled=True)  51.1 us
  transfers between devices with their start and end apart: 16, of which 10 were waited for; matrix products, arithmetic and copies ran while one was open for 20% of the time, Pallas kernels for 0%

commit v1 on v0

v1 whole, which is shorter than its diff:
```python
import functools
import math

import jax
import jax.numpy as jnp
import numpy as np
from jax import lax
from jax.experimental import pallas as pl
from jax.experimental.pallas import tpu as pltpu
from jax.sharding import PartitionSpec as P

HEADS = 16
HD = 64
BUCKETS = 32
CAP = 480
PAIRS = HEADS // 2
LANES = 2 * HD

epsilon = 1e-06
masked_value = -1e30
max_distance = 128.0
SCALE = 1.0 / math.sqrt(HD)
MB = 1 << 20
F32 = jnp.float32
BF16 = jnp.bfloat16


def bucket_of(offset, bucket_count):
    halfway = bucket_count // 2
    exact_span = bucket_count // 4
    distance = np.abs(offset)
    log_part = np.log(np.maximum(distance, 1) / float(exact_span)) / np.log(
        max_distance / exact_span
    )
    far_bucket = np.minimum(
        exact_span + np.floor(log_part * exact_span).astype(np.int64), halfway - 1
    )
    inside = np.where(distance < exact_span, distance, far_bucket)
    return np.where(offset < 0, halfway, 0) + inside


def diagonal_onehot(ahead):
    return (bucket_of(-ahead, BUCKETS)[None, :] == np.arange(BUCKETS)[:, None]).astype(np.float32)


def dot(a, b):
    return jnp.dot(a, b, preferred_element_type=F32)


def dot_nt(a, b):
    return lax.dot_general(a, b, (((1,), (1,)), ((), ())), preferred_element_type=F32)


def dot_tn(a, b):
    return lax.dot_general(a, b, (((0,), (0,)), ((), ())), preferred_element_type=F32)


def two_halves(value):
    high = value.astype(BF16)
    return high, (value - high.astype(F32)).astype(BF16)


def columns(index, width):
    return pl.ds(pl.multiple_of(index * width, width), width)


VMEM_SPEC = pl.BlockSpec(memory_space=pltpu.VMEM)


ANY_SPEC = pl.BlockSpec(memory_space=pl.ANY)
MESH = pl.DeviceIdType.MESH
DMA = pltpu.SemaphoreType.DMA


def call(kernel, out_shape, scratch, vmem, flops, *args, stay=(), land=(), link=None):
    nbytes = sum(a.size * a.dtype.itemsize for a in args)
    params = dict(vmem_limit_bytes=vmem)
    if link is not None:
        params.update(collective_id=link, has_side_effects=True)
    return pl.pallas_call(
        kernel,
        out_shape=out_shape,
        in_specs=[ANY_SPEC if i in stay else VMEM_SPEC for i in range(len(args))],
        out_specs=tuple(ANY_SPEC if i in land else VMEM_SPEC for i in range(len(out_shape))),
        scratch_shapes=scratch,
        compiler_params=pltpu.CompilerParams(**params),
        cost_estimate=pl.CostEstimate(flops=flops, bytes_accessed=nbytes, transcendentals=0),
    )(*args)


def here():
    d, e = lax.axis_index("dp"), lax.axis_index("expert")
    return d, e, d // 2, lax.rem(d, 2)


def flipped(value, bits):
    low, high = lax.rem(value, 2), value // 2
    low = 1 - low if bits & 1 else low
    high = 1 - high if bits & 2 else high
    return 2 * high + low


def meet(partners):
    barrier = pltpu.get_barrier_semaphore()
    for partner in partners:
        pl.semaphore_signal(barrier, inc=1, device_id=partner, device_id_type=MESH)
    pl.semaphore_wait(barrier, len(partners))


def push(src, dst, send, recv, to):
    copy = pltpu.make_async_remote_copy(
        src_ref=src, dst_ref=dst, send_sem=send, recv_sem=recv, device_id=to, device_id_type=MESH
    )
    copy.start()
    return copy


def group(d, e):
    return [None] + [(d, flipped(e, q)) for q in (1, 2, 3)]


class Spread:
    def __init__(self, src, dst, send, recv, d, e):
        self.src, self.dst, self.send, self.recv = src, dst, send, recv
        self.to = group(d, e)
        self.half = src.shape[0] // 2
        self.copies = {}

    def part(self, ref, half):
        return ref.at[pl.ds(half * self.half, self.half)]

    def start(self):
        for turn in range(2):
            for q in (1, 2):
                half = turn if q == 1 else 1 - turn
                at = 2 * (q - 1) + half
                self.copies[q, half] = push(
                    self.part(self.src, half),
                    self.part(self.dst.at[q], half),
                    self.send.at[at],
                    self.recv.at[at],
                    self.to[q],
                )

    def forward(self):
        for q, half, across, at in ((1, 0, 2, 4), (2, 1, 1, 5)):
            self.copies[q, half].wait_recv()
            self.copies[3, half] = push(
                self.part(self.dst.at[q], half),
                self.part(self.dst.at[3], half),
                self.send.at[at],
                self.recv.at[at],
                self.to[across],
            )

    def finish(self):
        for q, half in ((1, 1), (2, 0), (3, 0), (3, 1)):
            self.copies[q, half].wait_recv()
        for copy in self.copies.values():
            copy.wait_send()


class Swap:
    def __init__(self, src, dst, send, recv, d, e):
        self.src, self.dst, self.send, self.recv = src, dst, send, recv
        self.to = group(d, e)
        self.copies = {}

    def start(self, q):
        self.copies[q] = push(
            self.src.at[q], self.dst.at[q], self.send.at[q], self.recv.at[q], self.to[q]
        )

    def finish(self):
        for copy in self.copies.values():
            copy.wait_recv()
        for copy in self.copies.values():
            copy.wait_send()


def gather_weights_kernel(own, full, local, send, recv):
    d, e, z, c = here()
    share = own.shape[0]
    other = 2 * z + 1 - c
    to_x, to_y, to_core = (d, flipped(e, 1)), (d, flipped(e, 2)), (other, e)
    to_z = [None] + [(2 * flipped(z, k) + c, e) for k in (1, 2, 3)]
    meet([to_x, to_y, to_core] + to_z[1:])

    def item(k, q):
        row = (2 * flipped(z, k) + c) * 4 + flipped(e, q)
        return full.at[pl.ds(pl.multiple_of(row * share, share), share)]

    def pass_on(src, k, q, way, at, to):
        return push(src, item(k, q), send.at[way, at], recv.at[way, at], to)

    z_way, x_way, y_way, across_way, core_way = range(5)
    mine = pltpu.make_async_copy(own, item(0, 0), local.at[0])
    mine.start()
    copies = []
    from_z, from_x, from_y, across, from_core = {}, {}, {}, {}, {}
    for k in (1, 2, 3):
        from_z[k] = pass_on(own, 0, 0, z_way, k, to_z[k])
    for k in range(4):
        src = own
        if k:
            from_z[k].wait_recv()
            src = item(k, 0)
        from_x[k] = pass_on(src, k, 0, x_way, k, to_x)
        from_y[k] = pass_on(src, k, 0, y_way, k, to_y)
        from_core[k, 0] = pass_on(src, k, 0, core_way, k, to_core)
    for k in range(4):
        from_x[k].wait_recv()
        from_core[k, 1] = pass_on(item(k, 1), k, 1, core_way, 4 + k, to_core)
        if k % 2 == 0:
            across[k] = pass_on(item(k, 1), k, 1, across_way, k, to_y)
        from_y[k].wait_recv()
        from_core[k, 2] = pass_on(item(k, 2), k, 2, core_way, 8 + k, to_core)
        if k % 2 == 1:
            across[k] = pass_on(item(k, 2), k, 2, across_way, k, to_x)
    for k in range(4):
        across[k].wait_recv()
        from_core[k, 3] = pass_on(item(k, 3), k, 3, core_way, 12 + k, to_core)
    for copy in from_core.values():
        copy.wait_recv()
    for copies in (from_z, from_x, from_y, across, from_core):
        for copy in copies.values():
            copy.wait_send()
    mine.wait()


def gather_weights(own):
    shape = (32 * own.shape[0], own.shape[1])
    return call(
        gather_weights_kernel,
        (jax.ShapeDtypeStruct(shape, BF16),),
        [DMA((1,)), DMA((5, 16)), DMA((5, 16))],
        16 * MB,
        0,
        own,
        stay=(0,),
        land=(0,),
        link=0,
    )[0]


def attention_forward_kernel(experts, *refs):
    fast = len(refs) > 16
    tokens, weights, heads, hot, length = refs[:5]
    refs = refs[5:]
    if fast:
        cotangent, meta = refs[:2]
        refs = refs[2:]
    qkv, attended, probs, resid, normed_two, small = refs[:6]
    normed, diagonals = refs[-2:]
    if fast:
        rows_full, cots_full, meta_full, local, send, recv = refs[6:-2]
        d, e, _, _ = here()
        meet(group(d, e)[1:])
        rows_spread = Spread(normed_two, rows_full, send.at[0], recv.at[0], d, e)
        cots_spread = Spread(cotangent, cots_full, send.at[1], recv.at[1], d, e)
        cots_spread.start()
        meta_copies = [
            push(meta, meta_full.at[q], send.at[2, q], recv.at[2, q], group(d, e)[q])
            for q in (1, 2, 3)
        ]
        own_copies = [
            pltpu.make_async_copy(cotangent, cots_full.at[0], local.at[0]),
            pltpu.make_async_copy(meta, meta_full.at[0], local.at[1]),
        ]
        for copy in own_copies:
            copy.start()
    slots, width = tokens.shape
    small[...] = jnp.transpose(weights[:, 4 * width :].astype(F32))[: small.shape[0], :]
    x = tokens[...].astype(F32)
    inv_one = lax.rsqrt(jnp.mean(x * x, axis=1, keepdims=True) + epsilon)
    normed[...] = (x * inv_one * small[experts : experts + 1, :]).astype(BF16)
    spread_bias = heads[...].astype(F32) * small[experts + 2 : experts + 3, :]
    diagonals[...] = dot(spread_bias.astype(BF16), hot[...])

    @pl.loop(0, 3 * width // 512)
    def _(j):
        qkv[:, columns(j, 512)] = dot(normed[...], weights[:, columns(j, 512)]).astype(BF16)

    lane = lax.broadcasted_iota(jnp.int32, (slots, LANES), 1)
    first = lane < HD
    live = lax.broadcasted_iota(jnp.int32, (slots, slots), 1) < length[0, 0]

    def attend(pair):
        q = qkv[:, columns(pair, LANES)]
        k = qkv[:, columns(PAIRS + pair, LANES)]
        v = qkv[:, columns(2 * PAIRS + pair, LANES)]
        outs = []
        for half in range(2):
            head = 2 * pair + half
            own = first if half == 0 else jnp.logical_not(first)
            row = jnp.broadcast_to(diagonals[pl.ds(head, 1), :], (slots, 2 * slots))
            bias = pltpu.roll(row, 0, 1, stride=1, stride_axis=0)[:, :slots]
            scores = dot_nt(jnp.where(own, q, jnp.zeros_like(q)), k) * SCALE + bias
            scores = jnp.where(live, scores, masked_value)
            exponent = jnp.exp(scores - jnp.max(scores, axis=1, keepdims=True))
            low = (exponent / jnp.sum(exponent, axis=1, keepdims=True)).astype(BF16)
            probs[head] = low
            outs.append(dot(low, v))
        attended[:, columns(pair, LANES)] = jnp.where(first, outs[0], outs[1]).astype(BF16)

    pl.loop(0, PAIRS // 2)(attend)
    if fast:
        cots_spread.forward()
    pl.loop(PAIRS // 2, PAIRS)(attend)

    @pl.loop(0, width // 512)
    def _(j):
        resid[:, columns(j, 512)] = tokens[:, columns(j, 512)].astype(F32) + dot(
            attended[...], weights[:, columns(3 * width // 512 + j, 512)]
        )

    r = resid[...]
    inv_two = lax.rsqrt(jnp.mean(r * r, axis=1, keepdims=True) + epsilon)
    normed_two[...] = (r * inv_two * small[experts + 1 : experts + 2, :]).astype(BF16)
    if fast:
        rows_spread.start()
        own_rows = pltpu.make_async_copy(normed_two, rows_full.at[0], local.at[2])
        own_rows.start()
        rows_spread.forward()
        for copy in own_copies:
            copy.wait()
        for copy in meta_copies:
            copy.wait()
        cots_spread.finish()
        own_rows.wait()
        rows_spread.finish()


def attention_forward(fast, experts, tokens, weights, heads, hot, length, cotangent, meta):
    slots, width = tokens.shape
    small_rows = -(-(experts + 3) // 8) * 8
    shapes = (
        jax.ShapeDtypeStruct((slots, 3 * width), BF16),
        jax.ShapeDtypeStruct((slots, width), BF16),
        jax.ShapeDtypeStruct((HEADS, slots, slots), BF16),
        jax.ShapeDtypeStruct((slots, width), F32),
        jax.ShapeDtypeStruct((slots, width), BF16),
        jax.ShapeDtypeStruct((small_rows, width), F32),
    )
    scratch = [pltpu.VMEM((slots, width), BF16), pltpu.VMEM((HEADS, 2 * slots), F32)]
    args = (tokens, weights, heads, hot, length)
    options = {}
    if fast:
        args = args + (cotangent, meta)
        shapes = shapes + (
            jax.ShapeDtypeStruct((experts, slots, width), BF16),
            jax.ShapeDtypeStruct((experts, slots, width), BF16),
            jax.ShapeDtypeStruct((experts,) + meta.shape, jnp.int32),
        )
        scratch = [DMA((3,)), DMA((3, 6)), DMA((3, 6))] + scratch
        options = dict(stay=(5, 6), land=(6, 7, 8), link=1)
    return call(
        functools.partial(attention_forward_kernel, experts),
        shapes,
        scratch,
        48 * MB,
        2 * slots * width * (4 * width + 2 * slots),
        *args,
        **options,
    )


def pair_gates(logits, route_zero, route_one):
    experts = logits.shape[0]
    which = lax.broadcasted_iota(jnp.int32, logits.shape, 0)
    zero = jnp.sum(jnp.where(which == route_zero, logits, 0.0), axis=0, keepdims=True)
    one = jnp.sum(jnp.where(which == route_one, logits, 0.0), axis=0, keepdims=True)
    top = jnp.maximum(zero, one)
    zero, one = jnp.exp(zero - top), jnp.exp(one - top)
    total = zero + one
    return zero / total, one / total


def dispatch_kernel(
    rows, cots, meta, small, own, buffer, scaled, plain, select, gate_column, acc, acc_cot, rank
):
    blocks, slots = rows.shape[0], rows.shape[1]
    expert = own[0, 0]
    total_zero = jnp.zeros((1, 1), F32)
    acc[...] = jnp.zeros_like(acc)
    acc_cot[...] = jnp.zeros_like(acc_cot)
    gate_column[...] = jnp.zeros_like(gate_column)

    def names(block):
        info = meta[block]
        valid = info[3:4, :] > 0
        zero = jnp.logical_and(valid, info[0:1, :] == expert)
        one = jnp.logical_and(valid, info[1:2, :] == expert)
        return info, zero, one

    row_of = lax.broadcasted_iota(jnp.int32, (16, slots), 0)
    for block in range(blocks):
        _, zero, _ = names(block)
        total_zero = total_zero + jnp.sum(zero.astype(F32), axis=1, keepdims=True)
        rank[block] = jnp.transpose(meta[block].astype(F32))

    for block in range(blocks):
        info, zero, one = names(block)
        mine = info[2:3, :].astype(F32)

        def earlier(other, counts):
            _, other_zero, other_one = names(other)
            marks = jnp.where(row_of == 0, other_zero.astype(F32), 0.0) + jnp.where(
                row_of == 1, other_one.astype(F32), 0.0
            )
            before = (rank[other][:, 2:3] < mine).astype(F32).astype(BF16)
            return counts + dot(marks.astype(BF16), before)

        counts = lax.fori_loop(0, blocks, earlier, jnp.zeros((16, slots), F32))
        place = jnp.where(
            zero, counts[0:1, :], jnp.where(one, counts[1:2, :] + total_zero, -1.0)
        ).astype(jnp.int32)
        hot = lax.broadcasted_iota(jnp.int32, (CAP, slots), 0) == place
        picked = hot.astype(F32).astype(BF16)
        select[block] = picked
        logits = dot_nt(small[...].astype(BF16), rows[block])
        gate_zero, gate_one = pair_gates(logits, info[0:1, :], info[1:2, :])
        gate = jnp.where(zero, gate_zero, jnp.where(one, gate_one, 0.0))
        gate_column[...] += jnp.sum(jnp.where(hot, gate, 0.0), axis=1, keepdims=True)
        acc[...] += dot(picked, rows[block])
        acc_cot[...] += dot(picked, cots[block])

    buffer[...] = acc[...].astype(BF16)
    plain[...] = acc_cot[...].astype(BF16)
    scaled[...] = (acc_cot[...] * gate_column[:, 0:1]).astype(BF16)


def dispatch(rows, cots, meta, small, own):
    blocks, slots, width = rows.shape
    shapes = (
        jax.ShapeDtypeStruct((CAP, width), BF16),
        jax.ShapeDtypeStruct((CAP, width), BF16),
        jax.ShapeDtypeStruct((CAP, width), BF16),
        jax.ShapeDtypeStruct((blocks, CAP, slots), BF16),
        jax.ShapeDtypeStruct((CAP, 128), F32),
    )
    return call(
        dispatch_kernel,
        shapes,
        [
            pltpu.VMEM((CAP, width), F32),
            pltpu.VMEM((CAP, width), F32),
            pltpu.VMEM((blocks, slots, meta.shape[1]), F32),
        ],
        56 * MB,
        4 * CAP * blocks * slots * width,
        rows,
        cots,
        meta,
        small,
        own,
    )


CHUNK = 256
GELU_A = math.sqrt(2.0 / math.pi)
GELU_B = 0.044715


def expert_chunk(buffer, scaled, gate, up, down):
    gate_in, up_in = dot(buffer, gate), dot(buffer, up)
    square = gate_in * gate_in
    wave = jnp.tanh(GELU_A * gate_in * (1.0 + GELU_B * square))
    half = 0.5 * (1.0 + wave)
    activated = gate_in * half
    slope = half + (0.5 * GELU_A) * gate_in * (1.0 - wave * wave) * (1.0 + 3.0 * GELU_B * square)
    hidden = (activated * up_in).astype(BF16)
    grad_hidden = dot_nt(scaled, down)
    grad_gate_in = (grad_hidden * up_in * slope).astype(BF16)
    grad_up_in = (grad_hidden * activated).astype(BF16)
    grad_buffer = dot_nt(grad_gate_in, gate) + dot_nt(grad_up_in, up)
    return (
        dot(hidden, down),
        grad_buffer,
        dot_tn(buffer, grad_gate_in),
        dot_tn(buffer, grad_up_in),
        dot_tn(hidden, scaled),
    )


def expert_kernel(
    buffer,
    scaled,
    plain,
    gate,
    up,
    down,
    out,
    grad_buffer,
    inner,
    grad_gate,
    grad_up,
    grad_down,
    acc_out,
    acc_grad,
):
    step = pl.program_id(0)

    @pl.when(step == 0)
    def _():
        acc_out[...] = jnp.zeros_like(acc_out)
        acc_grad[...] = jnp.zeros_like(acc_grad)

    more_out, more_grad, d_gate, d_up, d_down = expert_chunk(
        buffer[...], scaled[...], gate[...], up[...], down[...]
    )
    acc_out[...] += more_out
    acc_grad[...] += more_grad
    grad_gate[...] = d_gate.astype(BF16)
    grad_up[...] = d_up.astype(BF16)
    grad_down[...] = d_down.astype(BF16)

    @pl.when(step == pl.num_programs(0) - 1)
    def _():
        low = acc_out[...].astype(BF16)
        out[...] = low
        grad_buffer[...] = acc_grad[...].astype(BF16)
        inner[...] = jnp.broadcast_to(
            jnp.sum(low.astype(F32) * plain[...].astype(F32), axis=1, keepdims=True), inner.shape
        )


def experts(buffer, scaled, plain, gate, up, down):
    rows, width = buffer.shape
    hidden = gate.shape[1]
    whole = pl.BlockSpec((rows, width), lambda j: (0, 0))
    tall = pl.BlockSpec((width, CHUNK), lambda j: (0, j))
    wide = pl.BlockSpec((CHUNK, width), lambda j: (j, 0))
    shapes = (
        jax.ShapeDtypeStruct((rows, width), BF16),
        jax.ShapeDtypeStruct((rows, width), BF16),
        jax.ShapeDtypeStruct((rows, 128), F32),
        jax.ShapeDtypeStruct((width, hidden), BF16),
        jax.ShapeDtypeStruct((width, hidden), BF16),
        jax.ShapeDtypeStruct((hidden, width), BF16),
    )
    return pl.pallas_call(
        expert_kernel,
        out_shape=shapes,
        grid=(hidden // CHUNK,),
        in_specs=[whole, whole, whole, tall, tall, wide],
        out_specs=(whole, whole, pl.BlockSpec((rows, 128), lambda j: (0, 0)), tall, tall, wide),
        scratch_shapes=[pltpu.VMEM((rows, width), F32), pltpu.VMEM((rows, width), F32)],
        compiler_params=pltpu.CompilerParams(
            vmem_limit_bytes=48 * MB, dimension_semantics=("arbitrary",)
        ),
        cost_estimate=pl.CostEstimate(
            flops=18 * rows * width * hidden,
            bytes_accessed=12 * width * hidden,
            transcendentals=rows * hidden,
        ),
    )(buffer, scaled, plain, gate, up, down)


def give_back_kernel(fast, select, out, grad_buffer, inner, gate_column, *refs):
    mixed = refs[0]
    grads, inner_rows = refs[-2:]
    blocks = select.shape[0]
    order = range(blocks)
    if fast:
        returned, inner_full, local, send, recv = refs[1:-2]
        d, e, _, _ = here()
        meet(group(d, e)[1:])
        swap = Swap(grads, returned, send.at[0], recv.at[0], d, e)
        inner_swap = Swap(inner_rows, inner_full, send.at[1], recv.at[1], d, e)
        order = (3, 1, 2, 0)
    for block in order:
        row = jnp.sum(select[block].astype(F32) * inner[:, 0:1], axis=0, keepdims=True)
        inner_rows[block] = jnp.broadcast_to(row, inner_rows.shape[1:])
        grads[block] = dot_tn(select[block], grad_buffer[...]).astype(BF16)
        if fast and block:
            inner_swap.start(block)
            swap.start(block)
    if fast:
        own_copies = [
            pltpu.make_async_copy(grads.at[0], returned.at[0], local.at[0]),
            pltpu.make_async_copy(inner_rows.at[0], inner_full.at[0], local.at[1]),
        ]
        for copy in own_copies:
            copy.start()
    weighted = (out[...].astype(F32) * gate_column[:, 0:1]).astype(BF16)
    for block in order:
        mixed[block] = dot_tn(select[block], weighted).astype(BF16)
    if fast:
        for copy in own_copies:
            copy.wait()
        inner_swap.finish()
        swap.finish()


def give_back(fast, select, out, grad_buffer, inner, gate_column):
    blocks, rows, slots = select.shape
    width = out.shape[1]
    wide = (blocks, slots, width)
    thin = (blocks, 8, slots)
    shapes = (
        jax.ShapeDtypeStruct(wide, BF16),
        jax.ShapeDtypeStruct(wide, BF16),
        jax.ShapeDtypeStruct(thin, F32),
    )
    scratch, options = [], {}
    if fast:
        scratch = [DMA((2,)), DMA((2, 4)), DMA((2, 4)), pltpu.VMEM(wide, BF16), pltpu.VMEM(thin, F32)]
        options = dict(land=(1, 2), link=2)
    return call(
        functools.partial(give_back_kernel, fast),
        shapes,
        scratch,
        56 * MB,
        4 * rows * blocks * slots * width,
        select,
        out,
        grad_buffer,
        inner,
        gate_column,
        **options,
    )


def attention_backward_kernel(
    fast,
    experts,
    tokens,
    cotangent,
    weights,
    small,
    heads,
    hot_back,
    length,
    meta,
    own,
    returned,
    inner_rows,
    mixed,
    qkv,
    attended,
    probs,
    resid,
    normed_two,
    output,
    grad_tokens,
    grad_weights,
    grad_small,
    grad_attended,
    grad_qkv,
    branch,
    normed,
    work,
    grad_diagonals,
    *refs,
):
    slots, width = tokens.shape
    blocks = returned.shape[0]
    if fast:
        mixed_full, send, recv = refs
        d, e, _, _ = here()
        meet(group(d, e)[1:])
        swap = Swap(mixed, mixed_full, send, recv, d, e)
        for block in (3, 1, 2):
            swap.start(block)
    router_t = small[...].astype(BF16)
    keep_row = lax.broadcasted_iota(jnp.int32, (slots, 1), 0) < length[0, 0]
    logits = dot_nt(router_t, normed_two[...])
    zero_route, one_route = meta[0:1, :], meta[1:2, :]
    gate_zero, gate_one = pair_gates(logits, zero_route, one_route)
    which = lax.broadcasted_iota(jnp.int32, logits.shape, 0)
    grad_zero = jnp.zeros((1, slots), F32)
    grad_one = jnp.zeros((1, slots), F32)
    for block in range(blocks):
        row = inner_rows[block][0:1, :]
        expert = jnp.bitwise_xor(own[0, 0], block) if fast else block
        grad_zero = grad_zero + jnp.where(zero_route == expert, row, 0.0)
        grad_one = grad_one + jnp.where(one_route == expert, row, 0.0)
    shared = gate_zero * grad_zero + gate_one * grad_one
    grad_zero = gate_zero * (grad_zero - shared)
    grad_one = gate_one * (grad_one - shared)
    grad_logits = jnp.where(which == zero_route, grad_zero, 0.0) + jnp.where(
        which == one_route, grad_one, 0.0
    )
    high, rest = two_halves(grad_logits)
    grad_small[...] = dot(high, normed_two[...]) + dot(rest, normed_two[...])
    grad_normed_two = dot_tn(high, router_t) + dot_tn(rest, router_t)
    for block in range(blocks):
        grad_normed_two = grad_normed_two + returned[block].astype(F32)
    r = resid[...]
    inv_two = lax.rsqrt(jnp.mean(r * r, axis=1, keepdims=True) + epsilon)
    unit_two = r * inv_two
    grad_small[experts + 1 : experts + 2, :] = jnp.sum(
        grad_normed_two * unit_two, axis=0, keepdims=True
    )
    scaled_two = small[experts + 1 : experts + 2, :] * grad_normed_two
    grad_resid = jnp.where(keep_row, cotangent[...].astype(F32), 0.0) + inv_two * (
        scaled_two - unit_two * jnp.mean(scaled_two * unit_two, axis=1, keepdims=True)
    )
    work[...] = grad_resid
    branch[...] = grad_resid.astype(BF16)

    @pl.loop(0, width // 256)
    def _(j):
        grad_weights[:, columns(3 * width // 256 + j, 256)] = dot_tn(
            attended[...], branch[:, columns(j, 256)]
        ).astype(BF16)

    grad_attended[...] = dot_nt(branch[...], weights[:, 3 * width : 4 * width]).astype(BF16)

    lane = lax.broadcasted_iota(jnp.int32, (slots, LANES), 1)
    first = lane < HD
    square = (slots, slots)
    flip = (
        lax.broadcasted_iota(jnp.int32, square, 0) + lax.broadcasted_iota(jnp.int32, square, 1)
        == slots - 1
    )
    flip = flip.astype(F32).astype(BF16)

    @pl.loop(0, PAIRS)
    def _(pair):
        q = qkv[:, columns(pair, LANES)]
        k = qkv[:, columns(PAIRS + pair, LANES)]
        v = qkv[:, columns(2 * PAIRS + pair, LANES)]
        g = grad_attended[:, columns(pair, LANES)]
        dq, dk, dv = [], [], []
        for half in range(2):
            head = 2 * pair + half
            own = first if half == 0 else jnp.logical_not(first)
            low = probs[head]
            p = low.astype(F32)
            grad_probs = dot_nt(jnp.where(own, g, jnp.zeros_like(g)), v)
            ds = p * (grad_probs - jnp.sum(p * grad_probs, axis=1, keepdims=True))
            ds = ds.astype(BF16)
            wide = jnp.concatenate([dot(flip, ds), jnp.zeros((slots, slots), F32)], axis=1)
            skewed = pltpu.roll(wide, 0, 1, stride=1, stride_axis=0)
            grad_diagonals[pl.ds(head, 1), :] = jnp.sum(skewed, axis=0, keepdims=True)
            dq.append(dot(ds, k))
            dk.append(dot_tn(ds, q))
            dv.append(dot_tn(low, g))
        grad_qkv[:, columns(pair, LANES)] = (jnp.where(first, dq[0], dq[1]) * SCALE).astype(BF16)
        grad_qkv[:, columns(PAIRS + pair, LANES)] = (
            jnp.where(first, dk[0], dk[1]) * SCALE
        ).astype(BF16)
        grad_qkv[:, columns(2 * PAIRS + pair, LANES)] = jnp.where(first, dv[0], dv[1]).astype(BF16)

    x = tokens[...].astype(F32)
    inv_one = lax.rsqrt(jnp.mean(x * x, axis=1, keepdims=True) + epsilon)
    unit_one = x * inv_one
    normed[...] = (unit_one * small[experts : experts + 1, :]).astype(BF16)
    high, rest = two_halves(grad_diagonals[...])
    by_lane = dot_nt(high, hot_back[...]) + dot_nt(rest, hot_back[...])
    grad_small[experts + 2 : experts + 3, :] = jnp.sum(
        by_lane * heads[...].astype(F32), axis=0, keepdims=True
    )

    @pl.loop(0, 3 * width // 256)
    def _(j):
        grad_weights[:, columns(j, 256)] = dot_tn(normed[...], grad_qkv[:, columns(j, 256)]).astype(
            BF16
        )

    grad_normed = dot_nt(grad_qkv[...], weights[:, : 3 * width])
    grad_small[experts : experts + 1, :] = jnp.sum(grad_normed * unit_one, axis=0, keepdims=True)
    scaled_one = small[experts : experts + 1, :] * grad_normed
    grad_tokens[...] = work[...] + inv_one * (
        scaled_one - unit_one * jnp.mean(scaled_one * unit_one, axis=1, keepdims=True)
    )
    if fast:
        swap.finish()
    total = resid[...] + mixed[0].astype(F32)
    for block in range(1, blocks):
        total = total + (mixed_full if fast else mixed)[block].astype(F32)
    output[...] = jnp.where(keep_row, total, 0.0).astype(BF16)


def attention_backward(fast, experts, *args):
    tokens, small, mixed = args[0], args[3], args[11]
    slots, width = tokens.shape
    shapes = (
        jax.ShapeDtypeStruct((slots, width), BF16),
        jax.ShapeDtypeStruct((slots, width), F32),
        jax.ShapeDtypeStruct((width, 4 * width), BF16),
        jax.ShapeDtypeStruct(small.shape, F32),
    )
    scratch = [
        pltpu.VMEM((slots, width), BF16),
        pltpu.VMEM((slots, 3 * width), BF16),
        pltpu.VMEM((slots, width), BF16),
        pltpu.VMEM((slots, width), BF16),
        pltpu.VMEM((slots, width), F32),
        pltpu.VMEM((HEADS, 2 * slots), F32),
    ]
    options = {}
    if fast:
        scratch += [pltpu.VMEM(mixed.shape, BF16), DMA((4,)), DMA((4,))]
        options = dict(link=3)
    return call(
        functools.partial(attention_backward_kernel, fast, experts),
        shapes,
        scratch,
        60 * MB,
        4 * slots * width * (4 * width + 2 * slots),
        *args,
        **options,
    )


def add_up_kernel(
    partial,
    small,
    grad_qkv,
    grad_out,
    small_sum,
    mine,
    theirs,
    first_in,
    second_in,
    planes,
    last_in,
    smalls,
    small_in,
    local,
    send,
    recv,
    small_send,
    small_recv,
):
    d, e, z, c = here()
    share = grad_qkv.shape[0]
    quad = 4 * share
    width = grad_out.shape[1]
    other = (2 * z + 1 - c, e)
    to_x, to_y = (d, flipped(e, 1)), (d, flipped(e, 2))
    to_z = [None] + [(2 * flipped(z, k) + c, e) for k in (1, 2, 3)]
    meet([other, to_x, to_y] + to_z[1:])
    turns = (3, 2, 1, 0)

    def block(k, core):
        row = (2 * flipped(z, k) + core) * quad
        return partial.at[pl.ds(pl.multiple_of(row, quad), quad)]

    def piece(k, q):
        row = flipped(e, q) * share
        return mine.at[k, pl.ds(pl.multiple_of(row, share), share)]

    loads, from_core, firsts, seconds, lasts = {}, {}, {}, {}, {}
    for k in turns:
        from_core[k] = push(block(k, 1 - c), theirs.at[k], send.at[0, k], recv.at[0, k], other)
        loads[k] = pltpu.make_async_copy(block(k, c), mine.at[k], local.at[k])
        loads[k].start()

    small_to = [other, to_x, to_y, to_z[1], to_z[2]]
    smalls[0] = small[...]
    small_copies = []

    def small_step():
        at = len(small_copies)
        if at:
            small_copies[at - 1].wait_recv()
            smalls[at] = smalls[at - 1] + small_in[at - 1]
        if at < len(small_to):
            small_copies.append(
                push(
                    smalls.at[at],
                    small_in.at[at],
                    small_send.at[at],
                    small_recv.at[at],
                    small_to[at],
                )
            )

    def stage_one(k):
        loads[k].wait()
        from_core[k].wait_recv()

        @pl.loop(0, 4)
        def _(j):
            at = pl.ds(pl.multiple_of(j * share, share), share)
            mine[k, at] = (mine[k, at].astype(F32) + theirs[k, at].astype(F32)).astype(BF16)

        near, to = (1, to_x) if k % 2 == 0 else (2, to_y)
        firsts[k] = [
            push(piece(k, q), first_in.at[k, slot], send.at[1 + slot, k], recv.at[1 + slot, k], to)
            for slot, q in ((1, 3), (0, near))
        ]

    def stage_two(k):
        far, to = (2, to_y) if k % 2 == 0 else (1, to_x)
        for copy in firsts[k]:
            copy.wait_recv()
        source = piece(k, far)
        source[...] = (source[...].astype(F32) + first_in[k, 1].astype(F32)).astype(BF16)
        seconds[k] = push(source, second_in.at[k], send.at[3, k], recv.at[3, k], to)

    def stage_three(k):
        seconds[k].wait_recv()
        total = piece(k, 0)[...].astype(F32) + first_in[k, 0].astype(F32)
        total = total + second_in[k].astype(F32)
        if k:
            planes[k] = total.astype(BF16)
            lasts[k] = push(planes.at[k], last_in.at[k], send.at[4, k], recv.at[4, k], to_z[k])
        else:
            grad_qkv[...] = total[:, : 3 * width]
            grad_out[...] = total[:, 3 * width :]

    a, b, c_, d_ = turns
    small_step()
    stage_one(a)
    stage_one(b)
    small_step()
    stage_two(a)
    stage_one(c_)
    stage_two(b)
    small_step()
    stage_three(a)
    stage_one(d_)
    stage_two(c_)
    small_step()
    stage_three(b)
    stage_two(d_)
    small_step()
    stage_three(c_)
    stage_three(d_)
    small_step()
    small_sum[...] = smalls[len(small_to)]
    for k in turns[:-1]:
        lasts[k].wait_recv()
    total = last_in[1].astype(F32) + last_in[2].astype(F32) + last_in[3].astype(F32)
    grad_qkv[...] += total[:, : 3 * width]
    grad_out[...] += total[:, 3 * width :]
    for copies in (from_core, seconds, lasts):
        for copy in copies.values():
            copy.wait_send()
    for pair in firsts.values():
        for copy in pair:
            copy.wait_send()
    for copy in small_copies:
        copy.wait_send()


def add_up(partial, small):
    width, wide = partial.shape
    share = width // 32
    return call(
        add_up_kernel,
        (
            jax.ShapeDtypeStruct((share, 3 * width), F32),
            jax.ShapeDtypeStruct((share, width), F32),
            jax.ShapeDtypeStruct(small.shape, F32),
        ),
        [
            pltpu.VMEM((4, 4 * share, wide), BF16),
            pltpu.VMEM((4, 4 * share, wide), BF16),
            pltpu.VMEM((4, 2, share, wide), BF16),
            pltpu.VMEM((4, share, wide), BF16),
            pltpu.VMEM((4, share, wide), BF16),
            pltpu.VMEM((4, share, wide), BF16),
            pltpu.VMEM((6,) + small.shape, F32),
            pltpu.VMEM((5,) + small.shape, F32),
            DMA((4,)),
            DMA((5, 4)),
            DMA((5, 4)),
            DMA((5,)),
            DMA((5,)),
        ],
        40 * MB,
        0,
        partial,
        small,
        stay=(0,),
        link=4,
    )


def on_device(
    fast,
    tokens,
    cotangent,
    qkv_weight,
    out_weight,
    router_weight,
    first_gain,
    second_gain,
    bias_table,
    gate_weight,
    up_weight,
    down_weight,
    lengths,
    routes,
    priority,
):
    both = ("dp", "expert")
    slots, width = tokens.shape
    expert_count = lax.axis_size("expert")
    device_count = lax.axis_size("dp") * expert_count
    share, bias_share = first_gain.shape[0], bias_table.shape[0]
    device = lax.axis_index("dp") * expert_count + lax.axis_index("expert")
    own = lax.axis_index("expert").astype(jnp.int32).reshape(1, 1)
    small_rows = -(-(expert_count + 3) // 8) * 8

    def gathered(value, axes, axis=0, tiled=True):
        return lax.all_gather(value, axes, axis=axis, tiled=tiled)

    def scattered(value, axes):
        return lax.psum_scatter(value, axes, scatter_dimension=0, tiled=True).astype(F32)

    def exchanged(value):
        return lax.all_to_all(value, "expert", split_axis=0, concat_axis=0, tiled=True)

    gate_full, up_full, down_full = (
        gathered(value[0], "dp") for value in (gate_weight, up_weight, down_weight)
    )

    beside = jnp.concatenate(
        [
            router_weight,
            first_gain[:, None],
            second_gain[:, None],
            jnp.pad(bias_table, (0, share - bias_share))[:, None],
            jnp.zeros((share, 128 - expert_count - 3), BF16),
        ],
        axis=1,
    )
    weights_own = jnp.concatenate([qkv_weight, out_weight, beside], axis=1)
    lane = np.arange(width)
    flat = lane // share * bias_share + lane % share
    in_table = lane % share < bias_share
    heads = np.arange(HEADS)[:, None] == np.where(in_table, flat // BUCKETS, -1)[None, :]
    heads = jnp.asarray(heads.astype(np.float32), BF16)
    ahead = np.arange(2 * slots)

    def hot(ahead):
        return jnp.asarray(
            np.where(in_table[:, None], diagonal_onehot(ahead)[flat % BUCKETS], 0.0), BF16
        )

    valid_rows = jnp.arange(slots, dtype=jnp.int32) < lengths[0, 0]
    meta_own = jnp.concatenate(
        [
            routes.T,
            priority,
            valid_rows.astype(jnp.int32)[None, :],
            jnp.zeros((4, slots), jnp.int32),
        ],
        axis=0,
    )

    weights = gather_weights(weights_own) if fast else gathered(weights_own, both)
    qkv, attended, probs, resid, normed_two, small, *spread = attention_forward(
        fast,
        expert_count,
        tokens,
        weights,
        heads,
        hot(np.where(ahead < slots, ahead, ahead - 2 * slots)),
        lengths,
        cotangent,
        meta_own,
    )
    if fast:
        rows, cots, meta = spread
    else:
        rows, cots, meta = (
            gathered(value, "expert", tiled=False) for value in (normed_two, cotangent, meta_own)
        )
    buffer, scaled, plain, select, gate_column = dispatch(rows, cots, meta, small, own)
    expert_out, grad_buffer, inner, grad_gate, grad_up, grad_down = experts(
        buffer, scaled, plain, gate_full, up_full, down_full
    )
    mixed, returned, inner_rows = give_back(
        fast, select, expert_out, grad_buffer, inner, gate_column
    )
    if not fast:
        mixed, returned, inner_rows = exchanged(mixed), exchanged(returned), exchanged(inner_rows)
    output, grad_tokens, grad_weights, grad_small = attention_backward(
        fast,
        expert_count,
        tokens,
        cotangent,
        weights,
        small,
        heads,
        hot(ahead - (slots - 1)),
        lengths,
        meta_own,
        own,
        returned,
        inner_rows,
        mixed,
        qkv,
        attended,
        probs,
        resid,
        normed_two,
    )
    if fast:
        grad_qkv, grad_out, grad_small = add_up(grad_weights, grad_small)
    else:
        grad_weights = scattered(grad_weights, both)
        grad_qkv, grad_out = grad_weights[:, : 3 * width], grad_weights[:, 3 * width :]
        grad_small = lax.psum(grad_small, both)
    grad_small = lax.dynamic_slice(grad_small, (0, device * share), (small_rows, share))
    return (
        output,
        grad_tokens,
        grad_qkv,
        grad_out,
        grad_small[:expert_count].T,
        grad_small[expert_count],
        grad_small[expert_count + 1],
        grad_small[expert_count + 2, :bias_share],
        scattered(grad_gate, "dp")[None],
        scattered(grad_up, "dp")[None],
        scattered(grad_down, "dp")[None],
    )


def solution(mesh):
    fast = dict(mesh.shape) == {"dp": 8, "expert": 4}
    rows = P(("dp", "expert"), None)
    flat = P(("dp", "expert"))
    expert = P("expert", "dp", None)
    grid = P("dp", "expert")
    return jax.shard_map(
        functools.partial(on_device, fast),
        mesh=mesh,
        in_specs=(rows,) * 5 + (flat,) * 3 + (expert,) * 3 + (grid, rows, grid),
        out_specs=(rows,) * 5 + (flat,) * 3 + (expert,) * 3,
        check_vma=False,
    )
```

time: 1100 us -> 486 us (0.44)
  waiting for transfers between devices: 614 us -> 150 us
  Pallas kernels: 0 us -> 289 us
  blocking collectives: 188 us -> 0 us
  matrix products: 111 us -> 0 us
  local copies, waits for them, and re-layouts: 122 us -> 24.8 us
  starting transfers between devices: 19.7 us -> 0.41 us
  other arithmetic: 23.2 us -> 7.07 us
    reduce_scatter x5 -> x3, waiting for transfers between devices: 439 us -> 68.3 us  [scattered(): lax.psum_scatter(value, axes, scatter_dimension=0, tiled=True).astype(F32)]
    pallas_call x0 -> x7, Pallas kernels: none -> 289 us  [the longest x6 250 us: call(): pl.pallas_call(kernel, out_shape=out_shape, in_specs=[ANY_SPEC if i in st...]
    dot_general x25 -> x0, matrix products: 108 us -> none  [the longest x1 12.3 us: on_device(): jnp.dot(grad_expert_out, down_matrix.T, preferred_element_type=jnp.float32)]
    all_gather x3 -> x0, blocking collectives: 100 us -> none  [the longest x1 83.4 us: on_device(): lax.all_gather(router_weight, ('dp', 'expert'), axis=0, tiled=True)]
    unnamed x3 -> x0, blocking collectives: 87.6 us -> none
    all_to_all x5 -> x0, waiting for transfers between devices: 68.4 us -> none  [the longest x1 25.2 us: on_device(): lax.all_to_all(back_slots, 'expert', split_axis=0, concat_axis=0, tiled=T...]
    gather x9 -> x0, local copies, waits for them, and re-layouts: 44.7 us -> none  [the longest x4 16.3 us: take_rows(): return padded[row_index]]
    all_gather x5 -> x3, waiting for transfers between devices: 103 us -> 78.4 us  [gathered(): return lax.all_gather(value, axes, axis=axis, tiled=tiled)]
  transfers between devices with their start and end apart: 16 -> 6, of which waited for: 10 -> 4; matrix products, arithmetic and copies ran while one was open for 20% -> 1% of each run, Pallas kernels for 0% -> 52%
where the time goes in v1:
time: 486 us
  Pallas kernels  289 us (59%)
  waiting for transfers between devices  150 us (31%)
  local copies, waits for them, and re-layouts  24.8 us (5%)
  between operations  15 us (3%)
  other arithmetic  7.07 us (1%)
    pallas_call x6, Pallas kernels, call(): pl.pallas_call(kernel, out_shape=out_shape, in_specs=[ANY_SPEC if i in st...  250 us
    all_gather x3, waiting for transfers between devices, gathered(): return lax.all_gather(value, axes, axis=axis, tiled=tiled)  78.4 us
    reduce_scatter x3, waiting for transfers between devices, scattered(): lax.psum_scatter(value, axes, scatter_dimension=0, tiled=True).astype(F32)  68.3 us
    pallas_call x1, Pallas kernels, experts(): pl.pallas_call(expert_kernel, out_shape=shapes, grid=(hidden // CHUNK,),...  38.5 us
    unnamed x65, local copies, waits for them, and re-layouts  22.6 us
  transfers between devices with their start and end apart: 6, of which 4 were waited for; matrix products, arithmetic and copies ran while one was open for 1% of the time, Pallas kernels for 52%

profile of v1, /device:TPU:0, one launch (start us, length us, event | category | flops | bytes accessed | tf_op | source)
XLA Modules:
  0.0 485.6 jit_solution(12780469011190768571)
XLA Ops:
  7.3 0.7 all-gather.7.cloned.1.call-update
  8.0 0.7 all-gather.9.cloned.1.call-update
  8.8 0.7 all-gather.11.cloned.1.call-update
  10.2 0.1 copy.31
  10.4 0.1 copy.28
  10.5 0.1 copy.29
  10.6 0.1 copy.30
  10.7 0.1 concatenate.6.own
  10.9 58.8 %shard_map.248.refs_1_.weights = bf16[1024,4224]{1,0:T(8,128)(2,1)S(1)} custom-call(bf16[32,4224]{1,0:T(8,128)(2,1)S(1)} %concatenate.6.own), custom_call_target="tpu_custom_call" | custom-call | bytes 270336 | tf_op jit(solution)/shard_map/pallas_call | solution.py:80
  69.6 3.4 copy-done
  73.1 43.4 %shard_map.249 = (bf16[256,3072]{1,0:T(8,128)(2,1)S(1)}, bf16[256,1024]{1,0:T(8,128)(2,1)S(1)}, bf16[16,256,256]{2,1,0:T(8,128)(2,1)}, f32[256,1024]{1,0:T(8,128...) custom-call(bf16[256,1024]{1,0:T(8,128)(2,1)S(1)} %copy-done.2, ...), custom_call_target="tpu_custom_call" | custom-call | flops 2415919104 | bytes 10788868 | tf_op jit(solution)/shard_map/pallas_call | solution.py:80
  116.5 1.2 copy-done.4
  117.8 1.0 copy-done.5
  118.7 0.8 copy-done.7
  119.5 0.8 copy-done.8
  120.3 0.6 copy-done.11
  120.9 0.6 copy-done.13
  121.5 11.2 %shard_map.250 = (bf16[480,1024]{1,0:T(8,128)(2,1)}, bf16[480,1024]{1,0:T(8,128)(2,1)}, bf16[480,1024]{1,0:T(8,128)(2,1)}, bf16[4,480,256]{2,1,0:T(8,128)(2,1)}, f32[480,128]{1,0:T(8,128)}) custom-call(bf16[4,256,1024]{2,1,0:T(8,128)(2,1)} %get-tuple-element.42.rows, bf16[4,256,1024]{2,1,0:T(8,128)(2,1)} %get-tuple-element.43.cots, s32[4,8,256]{2,1,0:T(8,128)} %copy-done.13, ...), custom_call_target="tpu_custom_call" | custom-call | flops 2013265920 | bytes 4259844 | tf_op jit(solution)/shard_map/pallas_call | solution.py:80
  132.7 17.6 %all-gather.9.cloned.1.call-done = bf16[1,1024,2816]{2,1,0:T(8,128)(2,1)} async-done(((bf16[1,128,2816]{2,1,0:T(8,128)(2,1)}), bf16[1,1024,2816]{2,1,0:T(8,128)(2,1)}) %all-gather.9.cloned.1.call-update) | async-done | bytes 5767184 | tf_op jit(solution)/shard_map/all_gather | solution.py:1003
  150.3 60.8 %all-gather.11.cloned.1.call-done = bf16[1,2816,1024]{2,1,0:T(8,128)(2,1)} async-done(((bf16[1,352,1024]{2,1,0:T(8,128)(2,1)}), bf16[1,2816,1024]{2,1,0:T(8,128)(2,1)}) %all-gather.11.cloned.1.call-update) | async-done | bytes 5767184 | tf_op jit(solution)/shard_map/all_gather | solution.py:1003
  211.1 1.2 copy-done.14
  212.3 1.2 copy-done.15
  213.5 1.2 copy-done.16
  214.7 38.5 %shard_map.251 = (bf16[480,1024]{1,0:T(8,128)(2,1)S(1)}, bf16[480,1024]{1,0:T(8,128)(2,1)S(1)}, f32[480,128]{1,0:T(8,128)S(1)}, bf16[1024,2816]{1,0:T(8,128)(2,1...) custom-call(bf16[480,1024]{1,0:T(8,128)(2,1)S(1)} %copy-done.14, bf16[480,1024]{1,0:T(8,128)(2,1)S(1)} %copy-done.15, ...), custom_call_target="tpu_custom_call" | custom-call | flops 24914165760 | bytes 34603008 | tf_op jit(solution)/shard_map/pallas_call | solution.py:542
  253.2 0.9 copy-done.17
  254.1 0.9 copy-done.18
  255.1 0.7 copy-done.19
  255.9 0.5 reduce-scatter.6.cloned.1.call-update
  256.4 0.2 reduce-scatter.4.cloned.1.call-start
  256.6 0.3 reduce-scatter.4.cloned.1.call-update
  257.0 30.6 %shard_map.252 = (bf16[4,256,1024]{2,1,0:T(8,128)(2,1)}, bf16[4,256,1024]{2,1,0:T(8,128)(2,1)}, f32[4,8,256]{2,1,0:T(8,128)}) custom-call(bf16[4,480,256]{2,1,0:T(8,128)(2,1)} %get-tuple-element.45.select, bf16[480,1024]{1,0:T(8,128)(2,1)} %copy-done.17, bf16[480,1024]{1,0:T(8,128)(2,1)} %copy-done.18, f32[480,128]{1,0:T(8,128)} %copy-done.19, ...), custom_call_target="tpu_custom_call" | custom-call | flops 2013265920 | bytes 3440640 | tf_op jit(solution)/shard_map/pallas_call | solution.py:80
  287.6 37.1 %shard_map.253 = (bf16[256,1024]{1,0:T(8,128)(2,1)}, f32[256,1024]{1,0:T(8,128)}, bf16[1024,4096]{1,0:T(8,128)(2,1)}, f32[8,1024]{1,0:T(8,128)}) custom-call(bf16[256,1024]{1,0:T(8,128)(2,1)} %tokens.1, bf16[256,1024]{1,0:T(8,128)(2,1)} %cotangent.1, bf16[1024,4224]{1,0:T(8,128)(2,1)} %copy-done, f32[8,1024]{1,0:T(8,128)} %copy-done.11, ...), custom_call_target="tpu_custom_call" | custom-call | flops 4831838208 | bytes 20815880 | tf_op jit(solution)/shard_map/pallas_call | solution.py:80
  324.7 3.9 copy-done.1
  328.6 0.8 copy-done.12
  329.4 69.2 %shard_map.254 = (f32[32,3072]{1,0:T(8,128)S(1)}, f32[32,1024]{1,0:T(8,128)S(1)}, f32[8,1024]{1,0:T(8,128)S(1)}) custom-call(bf16[1024,4096]{1,0:T(8,128)(2,1)S(1)} %copy-done.1, f32[8,1024]{1,0:T(8,128)S(1)} %copy-done.12), custom_call_target="tpu_custom_call" | custom-call | bytes 8421376 | tf_op jit(solution)/shard_map/pallas_call | solution.py:80
  398.6 0.1 constant_dynamic-slice_fusion
  398.7 0.5 slice_bitcast_fusion.1
  399.2 0.5 slice_bitcast_fusion.2
  399.7 0.6 slice_bitcast_fusion
  400.3 2.4 bitcast_convert_fusion
  402.7 0.5 reduce-scatter.6.cloned.1.call-done
  403.2 2.3 bitcast_convert_fusion.1
  405.5 67.8 %reduce-scatter.4.cloned.1.call-done = bf16[128,2816]{1,0:T(8,128)(2,1)} async-done(((bf16[1024,2816]{1,0:T(8,128)(2,1)}), bf16[128,2816]{1,0:T(8,128)(2,1)}) %reduce-scatter.4.cloned.1.call-update) | async-done | bytes 720912 | tf_op jit(solution)/shard_map/reduce_scatter | solution.py:1006
  473.3 2.3 bitcast_convert_fusion.2
  475.6 0.8 copy.37
  476.4 1.0 copy.38
  477.4 0.7 copy.39
  478.1 0.7 copy.40
  (59 shorter events, 0.5 us)
Async XLA Ops:
  7.2 3.1 copy-start.29
  7.2 3.2 copy-start.25
  7.2 3.3 copy-start.27
  7.2 3.4 copy-start.28
  7.2 3.4 copy-start.23
  7.2 3.4 copy-start.22
  7.2 125.5 %all-gather.7.cloned.1.call-start = ((), (), s32[]{:S(2)}) async-start(), calls=%async_computation.6 | async-start | bytes 6488064 | tf_op jit(solution)/shard_map/all_gather | solution.py:1003
  8.0 142.3 %all-gather.9.cloned.1.call-start = ((), (), s32[]{:S(2)}) async-start(), calls=%async_computation.7 | async-start | bytes 6488064 | tf_op jit(solution)/shard_map/all_gather | solution.py:1003
  8.7 202.4 %all-gather.11.cloned.1.call-start = ((), (), s32[]{:S(2)}) async-start(), calls=%async_computation.8 | async-start | bytes 6488064 | tf_op jit(solution)/shard_map/all_gather | solution.py:1003
  9.5 390.9 %reduce-scatter.8.cloned.1.call-start = ((), (), s32[]{:S(2)}) async-start(), calls=%async_computation.5 | async-start | bytes 6488064 | tf_op jit(solution)/shard_map/reduce_scatter | solution.py:1006
  10.8 62.2 %copy-start.24 = (s32[256,2]{0,1:T(2,128)S(1)}, s32[256,2]{0,1:T(2,128)}, u32[]{:S(2)}) copy-start(s32[256,2]{0,1:T(2,128)} %param.29) | copy-start | bytes 6148
  10.8 62.2 %copy-start.26 = (s32[1,256]{1,0:T(1,128)S(1)}, s32[1,256]{1,0:T(1,128)}, u32[]{:S(2)}) copy-start(s32[1,256]{1,0:T(1,128)} %param.30) | copy-start | bytes 3076
  10.8 62.3 %copy-start.2 = (bf16[256,1024]{1,0:T(8,128)(2,1)S(1)}, bf16[256,1024]{1,0:T(8,128)(2,1)}, u32[]{:S(2)}) copy-start(bf16[256,1024]{1,0:T(8,128)(2,1)} %tokens.1) | copy-start | bytes 1572868
  10.8 62.3 %copy-start.3 = (bf16[256,1024]{1,0:T(8,128)(2,1)S(1)}, bf16[256,1024]{1,0:T(8,128)(2,1)}, u32[]{:S(2)}) copy-start(bf16[256,1024]{1,0:T(8,128)(2,1)} %cotangent.1) | copy-start | bytes 1572868
  10.8 62.3 %copy-start.6 = (bf16[1024,512]{1,0:T(8,128)(2,1)S(1)}, bf16[1024,512]{1,0:T(8,128)(2,1)}, u32[]{:S(2)}) copy-start(bf16[1024,512]{1,0:T(8,128)(2,1)} %constant.28.clone.refs_3_) | copy-start | bytes 3145732
  10.8 62.3 %copy-start.9 = (bf16[16,1024]{1,0:T(8,128)(2,1)S(1)}, bf16[16,1024]{1,0:T(8,128)(2,1)}, u32[]{:S(2)}) copy-start(bf16[16,1024]{1,0:T(8,128)(2,1)} %constant.27.clone.refs_2_.heads) | copy-start | bytes 98308
  69.6 3.4 copy-start
  73.1 43.4 %copy-start.10 = (s32[8,256]{1,0:T(8,128)}, s32[8,256]{1,0:T(8,128)S(1)}, u32[]{:S(2)}) copy-start(s32[8,256]{1,0:T(8,128)S(1)} %add_add_fusion.refs_6_.meta) | copy-start | bytes 24580
  116.5 1.2 copy-start.4
  117.8 1.0 copy-start.5
  118.7 0.8 copy-start.7
  119.5 0.8 copy-start.8
  120.3 0.6 copy-start.11
  120.9 0.6 copy-start.13
  211.1 1.2 copy-start.14
  212.3 1.2 copy-start.15
  213.5 1.2 copy-start.16
  253.2 0.9 copy-start.17
  254.1 0.9 copy-start.18
  255.1 0.7 copy-start.19
  255.8 147.4 %reduce-scatter.6.cloned.1.call-start = ((), (), s32[]{:S(2)}) async-start(), calls=%async_computation.4 | async-start | bytes 6488064 | tf_op jit(solution)/shard_map/reduce_scatter | solution.py:1006
  256.4 216.9 %reduce-scatter.4.cloned.1.call-start = ((), (), s32[]{:S(2)}) async-start(), calls=%async_computation.3 | async-start | bytes 6488064 | tf_op jit(solution)/shard_map/reduce_scatter | solution.py:1006
  324.7 3.9 copy-start.1
  328.6 0.8 copy-start.12
  402.7 72.9 %copy-start.21 = (bf16[256,1024]{1,0:T(8,128)(2,1)S(1)}, bf16[256,1024]{1,0:T(8,128)(2,1)}, u32[]{:S(2)}) copy-start(bf16[256,1024]{1,0:T(8,128)(2,1)} %get-tuple-element.84) | copy-start | bytes 1572868
  405.5 70.9 %copy-start.20 = (f32[256,1024]{1,0:T(8,128)S(1)}, f32[256,1024]{1,0:T(8,128)}, u32[]{:S(2)}) copy-start(f32[256,1024]{1,0:T(8,128)} %get-tuple-element.85) | copy-start | bytes 3145732
Sparse Core Ops, SparseCore 0:
  9.7 78.4 all-gather.6
  89.8 60.4 all-gather.8
  152.0 59.0 all-gather.10
  255.9 63.5 reduce-scatter.7
  321.6 81.4 reduce-scatter.5
  405.3 67.8 reduce-scatter.3

commit v2 on v1

--- a/solution.py
+++ b/solution.py
@@ -243,8 +243,209 @@
     )[0]
 
 
-def attention_forward_kernel(experts, *refs):
-    fast = len(refs) > 16
+class LineSum:
+    def __init__(self, count, source, scratch, load):
+        self.count, self.source, self.load_first = count, source, load
+        scratch = list(scratch)
+        self.theirs, self.landed, self.send, self.recv = scratch[:4]
+        if load:
+            self.loads, self.loaded = scratch[4:]
+        self.d, self.e, self.z, self.core = here()
+        self.other = (2 * self.z + 1 - self.core, self.e)
+        self.to = [None] + [(2 * flipped(self.z, k) + self.core, self.e) for k in (1, 2, 3)]
+        self.end = jnp.logical_or(self.z == 0, self.z == 3)
+        self.middle = jnp.logical_not(self.end)
+
+    @staticmethod
+    def scratch(count, rows, width, load):
+        shape = (count, 4, rows, width)
+        parts = [pltpu.VMEM(shape, BF16), pltpu.VMEM(shape, BF16), DMA((count, 3, 4)), DMA((count, 3, 4))]
+        return parts + ([pltpu.VMEM(shape, BF16), DMA((count, 4))] if load else [])
+
+    def remote(self, i, src, dst, stage, out, into, to):
+        return pltpu.make_async_remote_copy(
+            src_ref=src,
+            dst_ref=dst,
+            send_sem=self.send.at[i, stage, out],
+            recv_sem=self.recv.at[i, stage, into],
+            device_id=to,
+            device_id_type=MESH,
+        )
+
+    def load(self, i, k):
+        return pltpu.make_async_copy(
+            self.source(i, k, self.core), self.loads.at[i, k], self.loaded.at[i, k]
+        )
+
+    def swap(self, i, k):
+        src = self.source(i, k, 1 - self.core)
+        return self.remote(i, src, self.theirs.at[i, k], 0, k, k, self.other)
+
+    def hand(self, i, k):
+        at = 1 if k == 1 else 5 - k
+        return self.remote(i, self.theirs.at[i, k], self.landed.at[i, at], 1, k, at, self.to[1])
+
+    def handed(self, i, at):
+        return self.remote(i, self.theirs.at[i, at], self.landed.at[i, at], 1, at, at, self.to[1])
+
+    def deliver(self, i, k):
+        return self.remote(i, self.theirs.at[i, k], self.landed.at[i, 0], 2, k, 0, self.to[k])
+
+    def add(self, i, k, more):
+        self.theirs[i, k] = (self.theirs[i, k].astype(F32) + more[...].astype(F32)).astype(BF16)
+
+    def begin(self, i):
+        for k in (3, 2, 1, 0):
+            self.swap(i, k).start()
+            if self.load_first:
+                self.load(i, k).start()
+
+    def halve(self, i):
+        for k in (3, 2, 1, 0):
+            if self.load_first:
+                self.load(i, k).wait()
+            self.swap(i, k).wait_recv()
+            self.add(i, k, self.loads.at[i, k] if self.load_first else self.source(i, k, self.core))
+        self.hand(i, 1).start()
+
+        @pl.when(self.end)
+        def _():
+            self.hand(i, 2).start()
+            self.hand(i, 3).start()
+
+    def relay(self, i):
+        @pl.when(self.middle)
+        def _():
+            for k in (3, 2):
+                self.handed(i, k).wait_recv()
+                self.add(i, k, self.landed.at[i, k])
+                self.deliver(i, k).start()
+
+    def finish(self, i):
+        self.handed(i, 1).wait_recv()
+        self.deliver(i, 2).wait_recv()
+        return (
+            self.theirs[i, 0].astype(F32)
+            + self.landed[i, 0].astype(F32)
+            + self.landed[i, 1].astype(F32)
+        )
+
+    def settle(self, i):
+        for k in range(4):
+            self.swap(i, k).wait_send()
+        self.hand(i, 1).wait_send()
+
+        @pl.when(self.end)
+        def _():
+            self.hand(i, 2).wait_send()
+            self.hand(i, 3).wait_send()
+
+        @pl.when(self.middle)
+        def _():
+            self.deliver(i, 2).wait_send()
+            self.deliver(i, 3).wait_send()
+
+
+class LineSpread:
+    def __init__(self, own, place, scratch):
+        self.own, self.place = own, place
+        self.copied, self.send, self.recv = scratch
+        self.d, self.e, self.z, self.core = here()
+        self.other = (2 * self.z + 1 - self.core, self.e)
+        self.to = [None] + [(2 * flipped(self.z, k) + self.core, self.e) for k in (1, 2, 3)]
+        self.end = jnp.logical_or(self.z == 0, self.z == 3)
+        self.middle = jnp.logical_not(self.end)
+
+    @staticmethod
+    def scratch(count):
+        return [DMA((count,)), DMA((count, 8)), DMA((count, 8))]
+
+    def from_chip(self, j, k, core=None):
+        return self.place(j, 2 * flipped(self.z, k) + (self.core if core is None else core))
+
+    def remote(self, j, src, dst, out, into, to):
+        return pltpu.make_async_remote_copy(
+            src_ref=src,
+            dst_ref=dst,
+            send_sem=self.send.at[j, out],
+            recv_sem=self.recv.at[j, into],
+            device_id=to,
+            device_id_type=MESH,
+        )
+
+    def keep(self, j):
+        return pltpu.make_async_copy(self.own(j), self.place(j, self.d), self.copied.at[j])
+
+    def first(self, j, way):
+        out = min(way, 2)
+        into = 4 if way == 0 else way
+        to = self.to[way] if way else self.other
+        return self.remote(j, self.own(j), self.place(j, self.d), out, into, to)
+
+    def share(self, j, k):
+        piece = self.from_chip(j, k)
+        return self.remote(j, piece, piece, 2 + k, 4 + k, self.other)
+
+    def pass_on(self, j, k):
+        piece = self.from_chip(j, k)
+        return self.remote(j, piece, piece, 4 + k, 5 - k, self.to[1])
+
+    def arrival(self, j, k):
+        piece = self.from_chip(j, k)
+        return self.remote(j, piece, piece, k, k, self.to[1])
+
+    def shared(self, j, k):
+        piece = self.from_chip(j, k, 1 - self.core)
+        return self.remote(j, piece, piece, 4 + k if k else 0, 4 + k, self.other)
+
+    def start(self, j):
+        self.first(j, 1).start()
+
+        @pl.when(self.middle)
+        def _():
+            self.first(j, 3).start()
+
+        @pl.when(self.end)
+        def _():
+            self.first(j, 2).start()
+
+        self.first(j, 0).start()
+        self.keep(j).start()
+
+    def relay(self, j):
+        for k in (1, 3, 2):
+            self.arrival(j, k).wait_recv()
+            if k > 1:
+                @pl.when(self.middle)
+                def _():
+                    self.pass_on(j, k).start()
+
+            self.share(j, k).start()
+
+    def complete(self, j):
+        self.keep(j).wait()
+        for k in range(4):
+            self.shared(j, k).wait_recv()
+
+    def settle(self, j):
+        self.first(j, 0).wait_send()
+        self.first(j, 1).wait_send()
+
+        @pl.when(self.middle)
+        def _():
+            self.first(j, 3).wait_send()
+            self.pass_on(j, 2).wait_send()
+            self.pass_on(j, 3).wait_send()
+
+        @pl.when(self.end)
+        def _():
+            self.first(j, 2).wait_send()
+
+        for k in (1, 2, 3):
+            self.share(j, k).wait_send()
+
+
+def attention_forward_kernel(fast, experts, *refs):
     tokens, weights, heads, hot, length = refs[:5]
     refs = refs[5:]
     if fast:
@@ -355,7 +556,7 @@
         scratch = [DMA((3,)), DMA((3, 6)), DMA((3, 6))] + scratch
         options = dict(stay=(5, 6), land=(6, 7, 8), link=1)
     return call(
-        functools.partial(attention_forward_kernel, experts),
+        functools.partial(attention_forward_kernel, fast, experts),
         shapes,
         scratch,
         48 * MB,
@@ -557,60 +758,27 @@
     )(buffer, scaled, plain, gate, up, down)
 
 
-def give_back_kernel(fast, select, out, grad_buffer, inner, gate_column, *refs):
-    mixed = refs[0]
-    grads, inner_rows = refs[-2:]
-    blocks = select.shape[0]
-    order = range(blocks)
-    if fast:
-        returned, inner_full, local, send, recv = refs[1:-2]
-        d, e, _, _ = here()
-        meet(group(d, e)[1:])
-        swap = Swap(grads, returned, send.at[0], recv.at[0], d, e)
-        inner_swap = Swap(inner_rows, inner_full, send.at[1], recv.at[1], d, e)
-        order = (3, 1, 2, 0)
-    for block in order:
+def give_back_kernel(select, out, grad_buffer, inner, gate_column, mixed, grads, inner_rows):
+    weighted = (out[...].astype(F32) * gate_column[:, 0:1]).astype(BF16)
+    for block in range(select.shape[0]):
         row = jnp.sum(select[block].astype(F32) * inner[:, 0:1], axis=0, keepdims=True)
         inner_rows[block] = jnp.broadcast_to(row, inner_rows.shape[1:])
         grads[block] = dot_tn(select[block], grad_buffer[...]).astype(BF16)
-        if fast and block:
-            inner_swap.start(block)
-            swap.start(block)
-    if fast:
-        own_copies = [
-            pltpu.make_async_copy(grads.at[0], returned.at[0], local.at[0]),
-            pltpu.make_async_copy(inner_rows.at[0], inner_full.at[0], local.at[1]),
-        ]
-        for copy in own_copies:
-            copy.start()
-    weighted = (out[...].astype(F32) * gate_column[:, 0:1]).astype(BF16)
-    for block in order:
         mixed[block] = dot_tn(select[block], weighted).astype(BF16)
-    if fast:
-        for copy in own_copies:
-            copy.wait()
-        inner_swap.finish()
-        swap.finish()
-
-
-def give_back(fast, select, out, grad_buffer, inner, gate_column):
+
+
+def give_back(select, out, grad_buffer, inner, gate_column):
     blocks, rows, slots = select.shape
     width = out.shape[1]
     wide = (blocks, slots, width)
-    thin = (blocks, 8, slots)
-    shapes = (
-        jax.ShapeDtypeStruct(wide, BF16),
-        jax.ShapeDtypeStruct(wide, BF16),
-        jax.ShapeDtypeStruct(thin, F32),
-    )
-    scratch, options = [], {}
-    if fast:
-        scratch = [DMA((2,)), DMA((2, 4)), DMA((2, 4)), pltpu.VMEM(wide, BF16), pltpu.VMEM(thin, F32)]
-        options = dict(land=(1, 2), link=2)
     return call(
-        functools.partial(give_back_kernel, fast),
-        shapes,
-        scratch,
+        give_back_kernel,
+        (
+            jax.ShapeDtypeStruct(wide, BF16),
+            jax.ShapeDtypeStruct(wide, BF16),
+            jax.ShapeDtypeStruct((blocks, 8, slots), F32),
+        ),
+        [],
         56 * MB,
         4 * rows * blocks * slots * width,
         select,
@@ -618,51 +786,296 @@
         grad_buffer,
         inner,
         gate_column,
-        **options,
-    )
-
-
-def attention_backward_kernel(
-    fast,
-    experts,
-    tokens,
-    cotangent,
-    weights,
-    small,
-    heads,
-    hot_back,
-    length,
-    meta,
+    )
+
+
+TILE = 2 * CHUNK
+
+
+def sweep_kernel(
+    ready,
+    summed,
+    buffer,
+    scaled,
+    plain,
+    gate_column,
+    select,
     own,
+    early,
+    down_full,
+    sums,
+    rest,
+    grad_down,
+    mixed,
     returned,
+    inner_full,
+    both,
+    down,
+    acc_out,
+    acc_grad,
+    down_stage,
+    grads,
     inner_rows,
-    mixed,
-    qkv,
-    attended,
-    probs,
-    resid,
-    normed_two,
-    output,
-    grad_tokens,
-    grad_weights,
-    grad_small,
-    grad_attended,
-    grad_qkv,
-    branch,
-    normed,
-    work,
-    grad_diagonals,
-    *refs,
+    loaded,
+    stored,
+    local,
+    swap_send,
+    swap_recv,
+    *scratch,
 ):
+    tiles, width = both.shape[0], both.shape[1]
+    share = own.shape[0]
+    coming = tiles - ready
+    d, e, z, c = here()
+
+    def columns_of(tile):
+        return pl.ds(pl.multiple_of(tile * TILE, TILE), TILE)
+
+    def rows_of(device):
+        return pl.ds(pl.multiple_of(device * share, share), share)
+
+    spread = LineSpread(
+        lambda j: own.at[:, columns_of(ready + j)],
+        lambda j, device: both.at[ready + j, rows_of(device)],
+        scratch[:3],
+    )
+    line = LineSum(
+        summed,
+        lambda i, k, core: both.at[i, rows_of(2 * flipped(z, k) + core)],
+        scratch[3:],
+        load=False,
+    )
+    swap = Swap(grads, returned, swap_send.at[0], swap_recv.at[0], d, e)
+    inner_swap = Swap(inner_rows, inner_full, swap_send.at[1], swap_recv.at[1], d, e)
+    meet(group(d, e)[1:] + [line.other] + line.to[1:])
+
+    def early_load(t):
+        return pltpu.make_async_copy(early.at[:, columns_of(t)], both.at[t], loaded.at[t])
+
+    down_load = pltpu.make_async_copy(down_full, down, loaded.at[tiles])
+    for t in range(ready):
+        early_load(t).start()
+        if t == 0:
+            down_load.start()
+    for j in range(min(2, coming)):
+        spread.start(j)
+    acc_out[...] = jnp.zeros_like(acc_out)
+    acc_grad[...] = jnp.zeros_like(acc_grad)
+    down_load.wait()
+
+    def down_rows(t):
+        return pl.ds(pl.multiple_of(t * CHUNK, CHUNK), CHUNK)
+
+    def down_store(t, slot):
+        return pltpu.make_async_copy(
+            down_stage.at[slot], grad_down.at[down_rows(t)], stored.at[tiles + slot]
+        )
+
+    def rest_store(t):
+        return pltpu.make_async_copy(both.at[t], rest.at[t - summed], stored.at[t])
+
+    def between(low, value, high):
+        return jnp.logical_and(value >= low, value < high)
+
+    def tile_step(t, _):
+        @pl.when(t < ready)
+        def _():
+            early_load(t).wait()
+
+        @pl.when(between(0, t - 2, coming))
+        def _():
+            spread.relay(t - 2)
+
+        @pl.when(between(2, t, coming))
+        def _():
+            spread.start(t)
+
+        @pl.when(t >= ready)
+        def _():
+            spread.complete(t - ready)
+
+        @pl.when(between(0, t - 1, summed))
+        def _():
+            line.halve(t - 1)
+
+        @pl.when(between(0, t - LAG, summed))
+        def _():
+            line.relay(t - LAG)
+
+        more_out, more_grad, d_gate, d_up, d_down = expert_chunk(
+            buffer[...], scaled[...], both[t, :, :CHUNK], both[t, :, CHUNK:], down[down_rows(t)]
+        )
+        acc_out[...] += more_out
+        acc_grad[...] += more_grad
+
+        @pl.when(t >= ready)
+        def _():
+            spread.settle(t - ready)
+
+        both[t, :, :CHUNK] = d_gate.astype(BF16)
+        both[t, :, CHUNK:] = d_up.astype(BF16)
+        slot = lax.rem(t, 2)
+
+        @pl.when(t >= 2)
+        def _():
+            down_store(t - 2, slot).wait()
+
+        down_stage[slot] = d_down.astype(BF16)
+        down_store(t, slot).start()
+
+        @pl.when(t < summed)
+        def _():
+            line.begin(t)
+
+        @pl.when(t >= summed)
+        def _():
+            rest_store(t).start()
+
+        return 0
+
+    lax.fori_loop(0, tiles, tile_step, 0)
+
+    low = acc_out[...].astype(BF16)
+    inner = jnp.sum(low.astype(F32) * plain[...].astype(F32), axis=1, keepdims=True)
+    grad_low = acc_grad[...].astype(BF16)
+    order = (3, 1, 2, 0)
+    for block in order:
+        row = jnp.sum(select[block].astype(F32) * inner, axis=0, keepdims=True)
+        inner_rows[block] = jnp.broadcast_to(row, inner_rows.shape[1:])
+        grads[block] = dot_tn(select[block], grad_low).astype(BF16)
+        if block:
+            inner_swap.start(block)
+            swap.start(block)
+    own_copies = [
+        pltpu.make_async_copy(grads.at[0], returned.at[0], local.at[0]),
+        pltpu.make_async_copy(inner_rows.at[0], inner_full.at[0], local.at[1]),
+    ]
+    for copy in own_copies:
+        copy.start()
+    for i in range(tiles - 1, summed):
+        line.halve(i)
+    weighted = (low.astype(F32) * gate_column[:, 0:1]).astype(BF16)
+    for block in order:
+        mixed[block] = dot_tn(select[block], weighted).astype(BF16)
+
+    @pl.loop(max(0, tiles - LAG), summed)
+    def _(i):
+        line.relay(i)
+
+    @pl.loop(0, summed)
+    def _(i):
+        sums[i] = line.finish(i)
+        line.settle(i)
+
+    for t in range(tiles - 2, tiles):
+        down_store(t, t % 2).wait()
+    for t in range(summed, tiles):
+        rest_store(t).wait()
+    for copy in own_copies:
+        copy.wait()
+    inner_swap.finish()
+    swap.finish()
+
+
+LAG = 4
+
+
+def sweep(ready, summed, buffer, scaled, plain, gate_column, select, own, early, down_full):
+    rows, width = buffer.shape
+    tiles = own.shape[1] // TILE
+    share = own.shape[0]
+    block = (select.shape[0], select.shape[2], width)
+    thin = (select.shape[0], 8, select.shape[2])
+    hidden = tiles * CHUNK
+    shapes = (
+        jax.ShapeDtypeStruct((summed, share, TILE), F32),
+        jax.ShapeDtypeStruct((max(1, tiles - summed), width, TILE), BF16),
+        jax.ShapeDtypeStruct(down_full.shape, BF16),
+        jax.ShapeDtypeStruct(block, BF16),
+        jax.ShapeDtypeStruct(block, BF16),
+        jax.ShapeDtypeStruct(thin, F32),
+    )
+    scratch = [
+        pltpu.VMEM((tiles, width, TILE), BF16),
+        pltpu.VMEM(down_full.shape, BF16),
+        pltpu.VMEM((rows, width), F32),
+        pltpu.VMEM((rows, width), F32),
+        pltpu.VMEM((2, CHUNK, width), BF16),
+        pltpu.VMEM(block, BF16),
+        pltpu.VMEM(thin, F32),
+        DMA((tiles + 1,)),
+        DMA((tiles + 2,)),
+        DMA((2,)),
+        DMA((2, 4)),
+        DMA((2, 4)),
+    ]
+    scratch += LineSpread.scratch(tiles - ready) + LineSum.scratch(summed, share, TILE, False)
+    return call(
+        functools.partial(sweep_kernel, ready, summed),
+        shapes,
+        scratch,
+        62 * MB,
+        18 * rows * width * hidden,
+        buffer,
+        scaled,
+        plain,
+        gate_column,
+        select,
+        own,
+        early,
+        down_full,
+        stay=(5, 6, 7),
+        land=(1, 2, 4, 5),
+        link=2,
+    )
+
+
+def down_source(array, z, share):
+    def source(i, k, core):
+        row = pl.multiple_of((2 * flipped(z, k) + core) * share, share)
+        return array.at[pl.ds(row, share), pl.ds(pl.multiple_of(i * CHUNK, CHUNK), CHUNK)]
+
+    return source
+
+
+def attention_backward_kernel(fast, experts, down_units, *refs):
+    refs = list(refs)
+
+    def take(count):
+        taken, refs[:] = refs[:count], refs[count:]
+        return taken
+
+    tokens, cotangent, weights, small, heads, hot_back, length, meta, own = take(9)
+    returned, inner_rows, mixed, qkv, attended, probs, resid, normed_two = take(8)
+    if fast:
+        tail, grad_down = take(2)
+    output, grad_tokens, grad_weights, grad_small = take(4)
+    if fast:
+        rest_sums, down_sums = take(2)
+    grad_attended, grad_qkv, branch, normed, work, grad_diagonals = take(6)
     slots, width = tokens.shape
     blocks = returned.shape[0]
     if fast:
-        mixed_full, send, recv = refs
-        d, e, _, _ = here()
-        meet(group(d, e)[1:])
+        mixed_full, send, recv = take(3)
+        d, e, z, _ = here()
+        share, down_share = width // 8, grad_down.shape[0] // 8
+
+        def rest_source(i, k, core):
+            row = pl.multiple_of((2 * flipped(z, k) + core) * share, share)
+            return tail.at[i, pl.ds(row, share)]
+
+        rest_line = LineSum(tail.shape[0], rest_source, take(6), True)
+        down_line = LineSum(down_units, down_source(grad_down, z, down_share), take(6), True)
+        lines = [(rest_line, i) for i in range(tail.shape[0])]
+        lines += [(down_line, i) for i in range(down_units)]
+        meet(group(d, e)[1:] + [rest_line.other] + rest_line.to[1:])
+        for line, i in lines:
+            line.begin(i)
         swap = Swap(mixed, mixed_full, send, recv, d, e)
         for block in (3, 1, 2):
             swap.start(block)
+        for line, i in lines:
+            line.halve(i)
     router_t = small[...].astype(BF16)
     keep_row = lax.broadcasted_iota(jnp.int32, (slots, 1), 0) < length[0, 0]
     logits = dot_nt(router_t, normed_two[...])
@@ -717,8 +1130,7 @@
     )
     flip = flip.astype(F32).astype(BF16)
 
-    @pl.loop(0, PAIRS)
-    def _(pair):
+    def attend_back(pair):
         q = qkv[:, columns(pair, LANES)]
         k = qkv[:, columns(PAIRS + pair, LANES)]
         v = qkv[:, columns(2 * PAIRS + pair, LANES)]
@@ -744,6 +1156,15 @@
         ).astype(BF16)
         grad_qkv[:, columns(2 * PAIRS + pair, LANES)] = jnp.where(first, dv[0], dv[1]).astype(BF16)
 
+    pl.loop(0, PAIRS // 2)(attend_back)
+    if fast:
+        for line, i in lines[: len(lines) // 2]:
+            line.relay(i)
+    pl.loop(PAIRS // 2, PAIRS)(attend_back)
+    if fast:
+        for line, i in lines[len(lines) // 2 :]:
+            line.relay(i)
+
     x = tokens[...].astype(F32)
     inv_one = lax.rsqrt(jnp.mean(x * x, axis=1, keepdims=True) + epsilon)
     unit_one = x * inv_one
@@ -767,6 +1188,9 @@
         scaled_one - unit_one * jnp.mean(scaled_one * unit_one, axis=1, keepdims=True)
     )
     if fast:
+        for line, i in lines:
+            (rest_sums if line is rest_line else down_sums)[i] = line.finish(i)
+            line.settle(i)
         swap.finish()
     total = resid[...] + mixed[0].astype(F32)
     for block in range(1, blocks):
@@ -774,7 +1198,7 @@
     output[...] = jnp.where(keep_row, total, 0.0).astype(BF16)
 
 
-def attention_backward(fast, experts, *args):
+def attention_backward(fast, experts, down_units, *args):
     tokens, small, mixed = args[0], args[3], args[11]
     slots, width = tokens.shape
     shapes = (
@@ -793,13 +1217,21 @@
     ]
     options = {}
     if fast:
+        rest, grad_down = args[-2:]
+        share, down_share = width // 8, grad_down.shape[0] // 8
+        shapes += (
+            jax.ShapeDtypeStruct((rest.shape[0], share, TILE), F32),
+            jax.ShapeDtypeStruct((down_units, down_share, CHUNK), F32),
+        )
         scratch += [pltpu.VMEM(mixed.shape, BF16), DMA((4,)), DMA((4,))]
-        options = dict(link=3)
+        scratch += LineSum.scratch(rest.shape[0], share, TILE, True)
+        scratch += LineSum.scratch(down_units, down_share, CHUNK, True)
+        options = dict(link=3, stay=(len(args) - 2, len(args) - 1))
     return call(
-        functools.partial(attention_backward_kernel, fast, experts),
+        functools.partial(attention_backward_kernel, fast, experts, down_units),
         shapes,
         scratch,
-        60 * MB,
+        62 * MB,
         4 * slots * width * (4 * width + 2 * slots),
         *args,
         **options,
@@ -807,11 +1239,14 @@
 
 
 def add_up_kernel(
+    done,
     partial,
     small,
+    grad_down,
     grad_qkv,
     grad_out,
     small_sum,
+    down_sums,
     mine,
     theirs,
     first_in,
@@ -825,9 +1260,16 @@
     recv,
     small_send,
     small_recv,
+    *scratch,
 ):
     d, e, z, c = here()
     share = grad_qkv.shape[0]
+    down_share = grad_down.shape[0] // 8
+    whole = down_source(grad_down, z, down_share)
+    line = LineSum(
+        down_sums.shape[0], lambda i, k, core: whole(done + i, k, core), scratch, True
+    )
+    units = range(down_sums.shape[0])
     quad = 4 * share
     width = grad_out.shape[1]
     other = (2 * z + 1 - c, e)
@@ -844,6 +1286,8 @@
         row = flipped(e, q) * share
         return mine.at[k, pl.ds(pl.multiple_of(row, share), share)]
 
+    for i in units:
+        line.begin(i)
     loads, from_core, firsts, seconds, lasts = {}, {}, {}, {}, {}
     for k in turns:
         from_core[k] = push(block(k, 1 - c), theirs.at[k], send.at[0, k], recv.at[0, k], other)
@@ -906,6 +1350,8 @@
 
     a, b, c_, d_ = turns
     small_step()
+    for i in units:
+        line.halve(i)
     stage_one(a)
     stage_one(b)
     small_step()
@@ -914,12 +1360,16 @@
     stage_two(b)
     small_step()
     stage_three(a)
+    for i in units[:1]:
+        line.relay(i)
     stage_one(d_)
     stage_two(c_)
     small_step()
     stage_three(b)
     stage_two(d_)
     small_step()
+    for i in units[1:]:
+        line.relay(i)
     stage_three(c_)
     stage_three(d_)
     small_step()
@@ -929,6 +1379,9 @@
     total = last_in[1].astype(F32) + last_in[2].astype(F32) + last_in[3].astype(F32)
     grad_qkv[...] += total[:, : 3 * width]
     grad_out[...] += total[:, 3 * width :]
+    for i in units:
+        down_sums[i] = line.finish(i)
+        line.settle(i)
     for copies in (from_core, seconds, lasts):
         for copy in copies.values():
             copy.wait_send()
@@ -939,15 +1392,18 @@
         copy.wait_send()
 
 
-def add_up(partial, small):
+def add_up(done, partial, small, grad_down):
     width, wide = partial.shape
     share = width // 32
+    down_share = grad_down.shape[0] // 8
+    left = width // CHUNK - done
     return call(
-        add_up_kernel,
+        functools.partial(add_up_kernel, done),
         (
             jax.ShapeDtypeStruct((share, 3 * width), F32),
             jax.ShapeDtypeStruct((share, width), F32),
             jax.ShapeDtypeStruct(small.shape, F32),
+            jax.ShapeDtypeStruct((left, down_share, CHUNK), F32),
         ),
         [
             pltpu.VMEM((4, 4 * share, wide), BF16),
@@ -963,14 +1419,21 @@
             DMA((5, 4)),
             DMA((5,)),
             DMA((5,)),
+            *LineSum.scratch(left, down_share, CHUNK, True),
         ],
-        40 * MB,
+        56 * MB,
         0,
         partial,
         small,
-        stay=(0,),
+        grad_down,
+        stay=(0, 2),
         link=4,
     )
+
+
+READY = 4
+SUMMED = 9
+DOWN_EARLY = 1
 
 
 def on_device(
@@ -1008,9 +1471,16 @@
     def exchanged(value):
         return lax.all_to_all(value, "expert", split_axis=0, concat_axis=0, tiled=True)
 
-    gate_full, up_full, down_full = (
-        gathered(value[0], "dp") for value in (gate_weight, up_weight, down_weight)
-    )
+    rows_own, hidden = gate_weight.shape[1:]
+    down_full = gathered(down_weight[0], "dp")
+    if fast:
+        tiles = (rows_own, hidden // CHUNK, 1, CHUNK)
+        both_own = jnp.concatenate(
+            [gate_weight.reshape(tiles), up_weight.reshape(tiles)], axis=2
+        ).reshape(rows_own, 2 * hidden)
+        early = gathered(both_own[:, : READY * TILE], "dp")
+    else:
+        gate_full, up_full = (gathered(value[0], "dp") for value in (gate_weight, up_weight))
 
     beside = jnp.concatenate(
         [
@@ -1065,17 +1535,34 @@
             gathered(value, "expert", tiled=False) for value in (normed_two, cotangent, meta_own)
         )
     buffer, scaled, plain, select, gate_column = dispatch(rows, cots, meta, small, own)
-    expert_out, grad_buffer, inner, grad_gate, grad_up, grad_down = experts(
-        buffer, scaled, plain, gate_full, up_full, down_full
-    )
-    mixed, returned, inner_rows = give_back(
-        fast, select, expert_out, grad_buffer, inner, gate_column
-    )
-    if not fast:
-        mixed, returned, inner_rows = exchanged(mixed), exchanged(returned), exchanged(inner_rows)
-    output, grad_tokens, grad_weights, grad_small = attention_backward(
+    if fast:
+        sums, rest, grad_down, mixed, returned, inner_rows = sweep(
+            READY,
+            SUMMED,
+            buffer,
+            scaled,
+            plain,
+            gate_column,
+            select,
+            both_own,
+            early,
+            down_full,
+        )
+        left = [rest, grad_down]
+    else:
+        expert_out, grad_buffer, inner, *grad_experts = experts(
+            buffer, scaled, plain, gate_full, up_full, down_full
+        )
+        mixed, returned, inner_rows = (
+            exchanged(value)
+            for value in give_back(select, expert_out, grad_buffer, inner, gate_column)
+        )
+        grad_gate, grad_up, grad_down = (scattered(value, "dp")[None] for value in grad_experts)
+        left = []
+    output, grad_tokens, grad_weights, grad_small, *more = attention_backward(
         fast,
         expert_count,
+        DOWN_EARLY,
         tokens,
         cotangent,
         weights,
@@ -1093,9 +1580,22 @@
         probs,
         resid,
         normed_two,
+        *left,
     )
     if fast:
-        grad_qkv, grad_out, grad_small = add_up(grad_weights, grad_small)
+        grad_qkv, grad_out, grad_small, down_late = add_up(
+            DOWN_EARLY, grad_weights, grad_small, grad_down
+        )
+        rest_sums, down_early = more
+        tiles = jnp.concatenate([sums, rest_sums], axis=0)
+        grad_gate, grad_up = (
+            jnp.transpose(tiles[:, :, i * CHUNK : (i + 1) * CHUNK], (1, 0, 2)).reshape(
+                1, rows_own, hidden
+            )
+            for i in range(2)
+        )
+        tiles = jnp.concatenate([down_early, down_late], axis=0)
+        grad_down = jnp.transpose(tiles, (1, 0, 2)).reshape((1,) + down_weight.shape[1:])
     else:
         grad_weights = scattered(grad_weights, both)
         grad_qkv, grad_out = grad_weights[:, : 3 * width], grad_weights[:, 3 * width :]
@@ -1110,9 +1610,9 @@
         grad_small[expert_count],
         grad_small[expert_count + 1],
         grad_small[expert_count + 2, :bias_share],
-        scattered(grad_gate, "dp")[None],
-        scattered(grad_up, "dp")[None],
-        scattered(grad_down, "dp")[None],
+        grad_gate,
+        grad_up,
+        grad_down,
     )
 
 

time: 486 us -> 451 us (0.928)
  waiting for transfers between devices: 150 us -> 3.73 us
  Pallas kernels: 289 us -> 399 us
  local copies, waits for them, and re-layouts: 24.8 us -> 31.7 us
  other arithmetic: 7.07 us -> 1.55 us
    pallas_call x6, Pallas kernels: 250 us -> 399 us  [call(): pl.pallas_call(kernel, out_shape=out_shape, in_specs=[ANY_SPEC if i in st...]
    all_gather x3 -> x2, waiting for transfers between devices: 78.4 us -> 3.02 us  [gathered(): return lax.all_gather(value, axes, axis=axis, tiled=tiled)]
    reduce_scatter x3 -> x0, waiting for transfers between devices: 68.3 us -> none  [scattered(): lax.psum_scatter(value, axes, scatter_dimension=0, tiled=True).astype(F32)]
    pallas_call x1 -> x0, Pallas kernels: 38.5 us -> none  [experts(): pl.pallas_call(expert_kernel, out_shape=shapes, grid=(hidden // CHUNK,),...]
    broadcast_in_dim x3 -> x0, other arithmetic: 6.99 us -> none  [the longest x1 2.39 us: on_device(): scattered(grad_down, 'dp')[None]]
    unnamed x65 -> x66, local copies, waits for them, and re-layouts: 22.6 us -> 18.6 us
  transfers between devices with their start and end apart: 6 -> 2, of which waited for: 4 -> 1; matrix products, arithmetic and copies ran while one was open for 1% -> 0% of each run, Pallas kernels for 52% -> 26%
where the time goes in v2:
time: 451 us
  Pallas kernels  399 us (88%)
  local copies, waits for them, and re-layouts  31.7 us (7%)
  between operations  15.1 us (3%)
    pallas_call x6, Pallas kernels, call(): pl.pallas_call(kernel, out_shape=out_shape, in_specs=[ANY_SPEC if i in st...  399 us
    unnamed x66, local copies, waits for them, and re-layouts  18.6 us
  transfers between devices with their start and end apart: 2, of which 1 were waited for; matrix products, arithmetic and copies ran while one was open for 0% of the time, Pallas kernels for 26%

profile of v2, /device:TPU:0, one launch (start us, length us, event | category | flops | bytes accessed | tf_op | source)
XLA Modules:
  0.0 450.6 jit_solution(5695741778101357992)
XLA Ops:
  7.2 0.0 all-gather.4.cloned.1.call-start
  7.2 1.5 copy.38
  8.8 0.3 copy.39
  9.1 0.1 pad_maximum_fusion
  9.3 2.0 copy.40
  11.3 1.0 reshape.56.own
  12.4 0.8 slice.28
  13.2 0.0 all-gather.4.cloned.1.call-update
  13.2 0.0 all-gather.6.cloned.1.call-start
  13.3 0.7 all-gather.6.cloned.1.call-update
  14.6 0.1 pad.12.clone
  14.7 0.1 copy.37
  14.8 0.1 copy.34
  14.9 0.1 copy.35
  15.0 0.1 copy.36
  15.2 0.1 concatenate.15.own
  15.3 60.4 %shard_map.248.refs_1_.refs_2_ = bf16[1024,4224]{1,0:T(8,128)(2,1)S(1)} custom-call(bf16[32,4224]{1,0:T(8,128)(2,1)S(1)} %concatenate.15.own), custom_call_target="tpu_custom_call" | custom-call | bytes 270336 | tf_op jit(solution)/shard_map/pallas_call | solution.py:80
  75.8 3.4 copy-done
  79.2 0.1 add_add_fusion.refs_6_.refs_7_
  79.3 43.7 %shard_map.249 = (bf16[256,3072]{1,0:T(8,128)(2,1)S(1)}, bf16[256,1024]{1,0:T(8,128)(2,1)S(1)}, bf16[16,256,256]{2,1,0:T(8,128)(2,1)}, f32[256,1024]{1,0:T(8,128...) custom-call(bf16[256,1024]{1,0:T(8,128)(2,1)S(1)} %copy-done.1, ...), custom_call_target="tpu_custom_call" | custom-call | flops 2415919104 | bytes 10788868 | tf_op jit(solution)/shard_map/pallas_call | solution.py:80
  123.0 1.1 copy-done.3
  124.1 1.0 copy-done.5
  125.1 0.8 copy-done.6
  125.9 0.8 copy-done.7
  126.7 0.6 copy-done.10
  127.3 0.6 copy-done.11
  127.9 11.1 %shard_map.250 = (bf16[480,1024]{1,0:T(8,128)(2,1)}, bf16[480,1024]{1,0:T(8,128)(2,1)}, bf16[480,1024]{1,0:T(8,128)(2,1)}, bf16[4,480,256]{2,1,0:T(8,128)(2,1)}, f32[480,128]{1,0:T(8,128)}) custom-call(bf16[4,256,1024]{2,1,0:T(8,128)(2,1)} %get-tuple-element.42.rows, bf16[4,256,1024]{2,1,0:T(8,128)(2,1)} %get-tuple-element.43.cots, s32[4,8,256]{2,1,0:T(8,128)} %copy-done.11, ...), custom_call_target="tpu_custom_call" | custom-call | flops 2013265920 | bytes 4259844 | tf_op jit(solution)/shard_map/pallas_call | solution.py:80
  139.1 3.0 all-gather.6.cloned.1.call-done
  142.1 149.0 %shard_map.251 = (f32[9,128,512]{2,1,0:T(8,128)}, bf16[2,1024,512]{2,1,0:T(8,128)(2,1)}, bf16[2816,1024]{1,0:T(8,128)(2,1)}, bf16[4,256,1024]{2,1,0:T(8,128)(2,1...) custom-call(bf16[480,1024]{1,0:T(8,128)(2,1)} %get-tuple-element.45.buffer, ...), custom_call_target="tpu_custom_call" | custom-call | flops 24914165760 | bytes 15581184 | tf_op jit(solution)/shard_map/pallas_call | solution.py:80
  291.1 52.7 %shard_map.252 = (bf16[256,1024]{1,0:T(8,128)(2,1)}, f32[256,1024]{1,0:T(8,128)}, bf16[1024,4096]{1,0:T(8,128)(2,1)}, f32[8,1024]{1,0:T(8,128)}, f32[2,128,512]{2,1,0:T(8,128)}, /*index=5*/f32[1,352,256]{2,1,0:T(8,128)}) custom-call(bf16[256,1024]{1,0:T(8,128)(2,1)} %refs_0_.3, bf16[256,1024]{1,0:T(8,128)(2,1)} %refs_1_.1, bf16[1024,4224]{1,0:T(8,128)(2,1)} %copy-done, ...), custom_call_target="tpu_custom_call" | custom-call | flops 4831838208 | bytes 28680200 | tf_op jit(solution)/shard_map/pallas_call | solution.py:80
  343.8 81.6 %shard_map.253 = (f32[32,3072]{1,0:T(8,128)}, f32[32,1024]{1,0:T(8,128)}, f32[8,1024]{1,0:T(8,128)}, f32[3,352,256]{2,1,0:T(8,128)}) custom-call(bf16[1024,4096]{1,0:T(8,128)(2,1)} %get-tuple-element.62.partial, f32[8,1024]{1,0:T(8,128)} %get-tuple-element.63.small, bf16[2816,1024]{1,0:T(8,128)(2,1)} %get-tuple-element.59.refs_18_.grad_down), custom_call_target="tpu_custom_call" | custom-call | bytes 14188544 | tf_op jit(solution)/shard_map/pallas_call | solution.py:80
  425.4 0.7 constant_dynamic-slice_fusion
  426.1 0.5 slice_bitcast_fusion.3
  426.6 0.5 slice_bitcast_fusion.4
  427.2 0.6 slice_bitcast_fusion.2
  427.7 1.3 maximum_bitcast_fusion
  429.1 0.9 copy.43
  430.0 1.8 reshape.59
  431.9 1.9 constant_dynamic-update-slice_fusion.1
  433.9 1.4 slice_bitcast_fusion
  435.3 1.8 copy.42
  437.1 1.5 copy.45
  438.6 0.4 copy.41
  439.1 1.5 copy.44
  440.6 0.8 copy.52
  441.4 1.0 copy.53
  442.4 0.7 copy.54
  443.1 0.7 copy.55
  (55 shorter events, 0.2 us)
Async XLA Ops:
  7.2 1.6 copy-start.14
  7.2 131.9 %all-gather.4.cloned.1.call-start = ((), (), s32[]{:S(2)}) async-start(), calls=%async_computation | async-start | bytes 4718592 | tf_op jit(solution)/shard_map/all_gather | solution.py:1466
  12.3 2.9 copy-start.12
  12.3 2.4 copy-start.27
  12.3 2.5 copy-start.23
  12.3 2.6 copy-start.25
  12.3 2.7 copy-start.26
  12.3 2.8 copy-start.19
  12.3 2.8 copy-start.21
  13.2 128.9 %all-gather.6.cloned.1.call-start = ((), (), s32[]{:S(2)}) async-start(), calls=%async_computation.1 | async-start | bytes 6488064 | tf_op jit(solution)/shard_map/all_gather | solution.py:1466
  15.3 63.9 %copy-start.22 = (s32[256,2]{0,1:T(2,128)S(1)}, s32[256,2]{0,1:T(2,128)}, u32[]{:S(2)}) copy-start(s32[256,2]{0,1:T(2,128)} %param.29) | copy-start | bytes 6148
  15.3 63.9 %copy-start.24 = (s32[1,256]{1,0:T(1,128)S(1)}, s32[1,256]{1,0:T(1,128)}, u32[]{:S(2)}) copy-start(s32[1,256]{1,0:T(1,128)} %param.30) | copy-start | bytes 3076
  15.3 64.0 %copy-start.1 = (bf16[256,1024]{1,0:T(8,128)(2,1)S(1)}, bf16[256,1024]{1,0:T(8,128)(2,1)}, u32[]{:S(2)}) copy-start(bf16[256,1024]{1,0:T(8,128)(2,1)} %refs_0_.3) | copy-start | bytes 1572868
  15.3 63.9 %copy-start.2 = (bf16[256,1024]{1,0:T(8,128)(2,1)S(1)}, bf16[256,1024]{1,0:T(8,128)(2,1)}, u32[]{:S(2)}) copy-start(bf16[256,1024]{1,0:T(8,128)(2,1)} %refs_1_.1) | copy-start | bytes 1572868
  15.3 63.9 %copy-start.4 = (bf16[1024,512]{1,0:T(8,128)(2,1)S(1)}, bf16[1024,512]{1,0:T(8,128)(2,1)}, u32[]{:S(2)}) copy-start(bf16[1024,512]{1,0:T(8,128)(2,1)} %constant.28.clone.refs_3_) | copy-start | bytes 3145732
  15.3 63.9 %copy-start.8 = (bf16[16,1024]{1,0:T(8,128)(2,1)S(1)}, bf16[16,1024]{1,0:T(8,128)(2,1)}, u32[]{:S(2)}) copy-start(bf16[16,1024]{1,0:T(8,128)(2,1)} %constant.27.clone.refs_2_.refs_4_) | copy-start | bytes 98308
  75.8 3.4 copy-start
  79.3 43.7 %copy-start.9 = (s32[8,256]{1,0:T(8,128)}, s32[8,256]{1,0:T(8,128)S(1)}, u32[]{:S(2)}) copy-start(s32[8,256]{1,0:T(8,128)S(1)} %add_add_fusion.refs_6_.refs_7_) | copy-start | bytes 24580
  123.0 1.1 copy-start.3
  124.1 1.0 copy-start.5
  125.1 0.8 copy-start.6
  125.9 0.8 copy-start.7
  126.7 0.6 copy-start.10
  127.3 0.6 copy-start.11
  343.8 84.0 %copy-start.18 = (f32[1,352,256]{2,1,0:T(8,128)S(1)}, f32[1,352,256]{2,1,0:T(8,128)}, u32[]{:S(2)}) copy-start(f32[1,352,256]{2,1,0:T(8,128)} %get-tuple-element.69) | copy-start | bytes 1081348
  431.9 1.9 copy-start.16
  439.1 1.6 copy-start.15
  439.1 2.3 copy-start.13
  440.6 1.8 copy-start.17
  441.4 1.7 copy-start.20
Sparse Core Ops, SparseCore 0:
  13.3 66.5 all-gather.3
  81.6 60.4 all-gather.5

commit v3 on v2

v3 whole, which is shorter than its diff:
```python
import functools
import math

import jax
import jax.numpy as jnp
import numpy as np
from jax import lax
from jax.experimental import pallas as pl
from jax.experimental.pallas import tpu as pltpu
from jax.sharding import PartitionSpec as P

HEADS = 16
HD = 64
BUCKETS = 32
CAP = 480
PAIRS = HEADS // 2
LANES = 2 * HD

epsilon = 1e-06
masked_value = -1e30
max_distance = 128.0
SCALE = 1.0 / math.sqrt(HD)
MB = 1 << 20
F32 = jnp.float32
BF16 = jnp.bfloat16


def bucket_of(offset, bucket_count):
    halfway = bucket_count // 2
    exact_span = bucket_count // 4
    distance = np.abs(offset)
    log_part = np.log(np.maximum(distance, 1) / float(exact_span)) / np.log(
        max_distance / exact_span
    )
    far_bucket = np.minimum(
        exact_span + np.floor(log_part * exact_span).astype(np.int64), halfway - 1
    )
    inside = np.where(distance < exact_span, distance, far_bucket)
    return np.where(offset < 0, halfway, 0) + inside


def diagonal_onehot(ahead):
    return (bucket_of(-ahead, BUCKETS)[None, :] == np.arange(BUCKETS)[:, None]).astype(np.float32)


def dot(a, b):
    return jnp.dot(a, b, preferred_element_type=F32)


def dot_nt(a, b):
    return lax.dot_general(a, b, (((1,), (1,)), ((), ())), preferred_element_type=F32)


def dot_tn(a, b):
    return lax.dot_general(a, b, (((0,), (0,)), ((), ())), preferred_element_type=F32)


def two_halves(value):
    high = value.astype(BF16)
    return high, (value - high.astype(F32)).astype(BF16)


def columns(index, width):
    return pl.ds(pl.multiple_of(index * width, width), width)


VMEM_SPEC = pl.BlockSpec(memory_space=pltpu.VMEM)


ANY_SPEC = pl.BlockSpec(memory_space=pl.ANY)
MESH = pl.DeviceIdType.MESH
DMA = pltpu.SemaphoreType.DMA


def call(kernel, out_shape, scratch, vmem, flops, *args, stay=(), land=(), link=None, aliases=None):
    nbytes = sum(a.size * a.dtype.itemsize for a in args)
    params = dict(vmem_limit_bytes=vmem)
    if link is not None:
        params.update(collective_id=link, has_side_effects=True)
    return pl.pallas_call(
        kernel,
        out_shape=out_shape,
        in_specs=[ANY_SPEC if i in stay else VMEM_SPEC for i in range(len(args))],
        out_specs=tuple(ANY_SPEC if i in land else VMEM_SPEC for i in range(len(out_shape))),
        scratch_shapes=scratch,
        input_output_aliases=aliases or {},
        compiler_params=pltpu.CompilerParams(**params),
        cost_estimate=pl.CostEstimate(flops=flops, bytes_accessed=nbytes, transcendentals=0),
    )(*args)


def here():
    d, e = lax.axis_index("dp"), lax.axis_index("expert")
    return d, e, d // 2, lax.rem(d, 2)


def flipped(value, bits):
    low, high = lax.rem(value, 2), value // 2
    low = 1 - low if bits & 1 else low
    high = 1 - high if bits & 2 else high
    return 2 * high + low


def meet(partners):
    barrier = pltpu.get_barrier_semaphore()
    for partner in partners:
        pl.semaphore_signal(barrier, inc=1, device_id=partner, device_id_type=MESH)
    pl.semaphore_wait(barrier, len(partners))


def push(src, dst, send, recv, to):
    copy = pltpu.make_async_remote_copy(
        src_ref=src, dst_ref=dst, send_sem=send, recv_sem=recv, device_id=to, device_id_type=MESH
    )
    copy.start()
    return copy


def group(d, e):
    return [None] + [(d, flipped(e, q)) for q in (1, 2, 3)]


class Spread:
    def __init__(self, src, dst, send, recv, d, e):
        self.src, self.dst, self.send, self.recv = src, dst, send, recv
        self.to = group(d, e)
        self.half = src.shape[0] // 2
        self.copies = {}

    def part(self, ref, half):
        return ref.at[pl.ds(half * self.half, self.half)]

    def start(self):
        for turn in range(2):
            for q in (1, 2):
                half = turn if q == 1 else 1 - turn
                at = 2 * (q - 1) + half
                self.copies[q, half] = push(
                    self.part(self.src, half),
                    self.part(self.dst.at[q], half),
                    self.send.at[at],
                    self.recv.at[at],
                    self.to[q],
                )

    def forward(self):
        for q, half, across, at in ((1, 0, 2, 4), (2, 1, 1, 5)):
            self.copies[q, half].wait_recv()
            self.copies[3, half] = push(
                self.part(self.dst.at[q], half),
                self.part(self.dst.at[3], half),
                self.send.at[at],
                self.recv.at[at],
                self.to[across],
            )

    def arrived(self, q):
        for half in {1: (1,), 2: (0,), 3: (0, 1)}[q]:
            self.copies[q, half].wait_recv()

    def sent(self):
        for copy in self.copies.values():
            copy.wait_send()

    def finish(self):
        for q in (1, 2, 3):
            self.arrived(q)
        self.sent()


class Swap:
    def __init__(self, src, dst, send, recv, d, e):
        self.src, self.dst, self.send, self.recv = src, dst, send, recv
        self.to = group(d, e)
        self.copies = {}

    def start(self, q):
        self.copies[q] = push(
            self.src.at[q], self.dst.at[q], self.send.at[q], self.recv.at[q], self.to[q]
        )

    def finish(self):
        for copy in self.copies.values():
            copy.wait_recv()
        for copy in self.copies.values():
            copy.wait_send()


class DeviceGather:
    WAYS = 5

    def __init__(self, full, share, send, recv):
        self.full, self.share, self.send, self.recv = full, share, send, recv
        self.d, self.e, self.z, self.core = d, e, z, c = here()
        self.to_x, self.to_y = (d, flipped(e, 1)), (d, flipped(e, 2))
        self.other = (2 * z + 1 - c, e)
        self.to_z = [None] + [(2 * flipped(z, k) + c, e) for k in (1, 2, 3)]
        self.end = jnp.logical_or(z == 0, z == 3)
        self.middle = jnp.logical_not(self.end)

    def item(self, k, q, core=None):
        device = 2 * flipped(self.z, k) + (self.core if core is None else core)
        row = (device * 4 + flipped(self.e, q)) * self.share
        return self.full.at[pl.ds(pl.multiple_of(row, self.share), self.share)]

    def pass_on(self, k, q, way, at, to, into=None):
        piece = self.item(k, q)
        return pltpu.make_async_remote_copy(
            src_ref=piece,
            dst_ref=piece,
            send_sem=self.send.at[way, at],
            recv_sem=self.recv.at[way, at if into is None else into],
            device_id=to,
            device_id_type=MESH,
        )

    def along_z(self, k):
        return self.pass_on(0, 0, 0, k, self.to_z[k])

    def relay_z(self, k):
        return self.pass_on(k, 0, 0, 2 + k, self.to_z[1], 5 - k)

    def along_x(self, k):
        return self.pass_on(k, 0, 1, k, self.to_x)

    def along_y(self, k):
        return self.pass_on(k, 0, 2, k, self.to_y)

    def across(self, k):
        return self.pass_on(k, 1, 3, k, self.to_y) if k % 2 == 0 else self.pass_on(k, 2, 3, k, self.to_x)

    def over(self, k, q):
        return self.pass_on(k, q, 4, 4 * q + k, self.other)

    def start(self):
        self.along_z(1).start()

        @pl.when(self.middle)
        def _():
            self.along_z(3).start()

        @pl.when(self.end)
        def _():
            self.along_z(2).start()

        self.spread_out(0)

    def spread_out(self, k):
        self.along_x(k).start()
        self.along_y(k).start()
        self.over(k, 0).start()

    def from_z(self, k):
        self.along_z(k).wait_recv()
        if k > 1:

            @pl.when(self.middle)
            def _():
                self.relay_z(k).start()

        self.spread_out(k)

    def from_neighbours(self, k):
        self.along_x(k).wait_recv()
        if k % 2 == 0:
            self.across(k).start()
        self.over(k, 1).start()
        self.along_y(k).wait_recv()
        if k % 2 == 1:
            self.across(k).start()
        self.over(k, 2).start()

    def from_across(self, k):
        self.across(k).wait_recv()
        self.over(k, 3).start()

    def complete(self):
        for q in range(4):
            for k in range(4):
                self.over(k, q).wait_recv()

    def settle(self):
        self.along_z(1).wait_send()

        @pl.when(self.middle)
        def _():
            self.along_z(3).wait_send()
            self.relay_z(2).wait_send()
            self.relay_z(3).wait_send()

        @pl.when(self.end)
        def _():
            self.along_z(2).wait_send()

        for k in range(4):
            self.along_x(k).wait_send()
            self.along_y(k).wait_send()
            self.across(k).wait_send()
            for q in range(4):
                self.over(k, q).wait_send()


class LineSum:
    def __init__(self, count, source, scratch, load):
        self.count, self.source, self.load_first = count, source, load
        scratch = list(scratch)
        self.theirs, self.landed, self.send, self.recv = scratch[:4]
        if load:
            self.loads, self.loaded = scratch[4:]
        self.d, self.e, self.z, self.core = here()
        self.other = (2 * self.z + 1 - self.core, self.e)
        self.to = [None] + [(2 * flipped(self.z, k) + self.core, self.e) for k in (1, 2, 3)]
        self.end = jnp.logical_or(self.z == 0, self.z == 3)
        self.middle = jnp.logical_not(self.end)

    @staticmethod
    def scratch(count, rows, width, load):
        part = (rows, width)
        parts = [
            pltpu.VMEM((count, 4) + part, BF16),
            pltpu.VMEM((count, 5) + part, BF16),
            DMA((count, 3, 5)),
            DMA((count, 3, 5)),
        ]
        return parts + ([pltpu.VMEM((count, 4) + part, BF16), DMA((count, 4))] if load else [])

    def remote(self, i, src, dst, stage, out, into, to):
        return pltpu.make_async_remote_copy(
            src_ref=src,
            dst_ref=dst,
            send_sem=self.send.at[i, stage, out],
            recv_sem=self.recv.at[i, stage, into],
            device_id=to,
            device_id_type=MESH,
        )

    def load(self, i, k):
        return pltpu.make_async_copy(
            self.source(i, k, self.core), self.loads.at[i, k], self.loaded.at[i, k]
        )

    def swap(self, i, k):
        src = self.source(i, k, 1 - self.core)
        return self.remote(i, src, self.theirs.at[i, k], 0, k, k, self.other)

    def hand(self, i, k):
        at = 1 if k == 1 else 5 - k
        return self.remote(i, self.theirs.at[i, k], self.landed.at[i, at], 1, k, at, self.to[1])

    def handed(self, i, at):
        return self.remote(i, self.theirs.at[i, at], self.landed.at[i, at], 1, at, at, self.to[1])

    def deliver(self, i, k):
        at = 0 if k == 3 else 4
        return self.remote(i, self.theirs.at[i, k], self.landed.at[i, at], 2, k, at, self.to[3])

    def for_partner(self, i):
        return self.remote(i, self.theirs.at[i, 0], self.landed.at[i, 4], 2, 4, 4, self.to[3])

    def last(self, i):
        return self.remote(i, self.theirs.at[i, 1], self.landed.at[i, 0], 2, 0, 0, self.to[1])

    def add(self, i, k, more):
        self.theirs[i, k] = (self.theirs[i, k].astype(F32) + more[...].astype(F32)).astype(BF16)

    def begin(self, i):
        for k in (3, 2, 1, 0):
            self.swap(i, k).start()
            if self.load_first:
                self.load(i, k).start()

    def halve(self, i):
        for k in (3, 2, 1, 0):
            if self.load_first:
                self.load(i, k).wait()
            self.swap(i, k).wait_recv()
            self.add(i, k, self.loads.at[i, k] if self.load_first else self.source(i, k, self.core))
        self.hand_over(i)

    def hand_over(self, i):
        @pl.when(self.end)
        def _():
            for k in (3, 2, 1):
                self.hand(i, k).start()

    def relay(self, i):
        @pl.when(self.middle)
        def _():
            for k in (2, 3):
                self.handed(i, k).wait_recv()
                self.add(i, k, self.landed.at[i, k])
                self.deliver(i, k).start()

    def pass_on(self, i):
        @pl.when(self.middle)
        def _():
            self.for_partner(i).wait_recv()
            self.add(i, 1, self.landed.at[i, 4])
            self.last(i).start()

    def finish(self, i, out):
        self.last(i).wait_recv()
        out[...] = self.theirs[i, 0].astype(F32) + self.landed[i, 0].astype(F32)
        if self.source is not None:
            for k in range(4):
                self.swap(i, k).wait_send()

        @pl.when(self.end)
        def _():
            for k in (3, 2, 1):
                self.hand(i, k).wait_send()

        @pl.when(self.middle)
        def _():
            self.handed(i, 1).wait_recv()
            out[...] += self.landed[i, 1].astype(F32)
            self.deliver(i, 2).wait_send()
            self.deliver(i, 3).wait_send()
            self.last(i).wait_send()


class LineSpread:
    def __init__(self, halves, place, scratch):
        self.halves, self.place = halves, place
        self.copied, self.send, self.recv = scratch
        self.d, self.e, self.z, self.core = here()
        self.other = (2 * self.z + 1 - self.core, self.e)
        self.to = [None] + [(2 * flipped(self.z, k) + self.core, self.e) for k in (1, 2, 3)]
        self.end = jnp.logical_or(self.z == 0, self.z == 3)
        self.middle = jnp.logical_not(self.end)

    @staticmethod
    def scratch(count):
        return [DMA((count,)), DMA((count, 9)), DMA((count, 8))]

    def from_chip(self, j, k, core=None):
        return self.place(j, 2 * flipped(self.z, k) + (self.core if core is None else core))

    def remote(self, j, src, dst, out, into, to):
        return pltpu.make_async_remote_copy(
            src_ref=src,
            dst_ref=dst,
            send_sem=self.send.at[j, out],
            recv_sem=self.recv.at[j, into],
            device_id=to,
            device_id_type=MESH,
        )

    def parts(self, j):
        piece = self.place(j, self.d)
        width = piece.shape[1] // 2
        for i, half in enumerate(self.halves(j)):
            yield half, piece.at[:, i * width : (i + 1) * width]

    def keep(self, j):
        piece = self.place(j, self.d)
        return pltpu.make_async_copy(piece, piece, self.copied.at[j])

    def first(self, j, way):
        piece = self.place(j, self.d)
        return self.remote(j, piece, piece, *self.way(way))

    def way(self, way):
        return min(way, 2), 4 if way == 0 else way, self.to[way] if way else self.other

    def send_own(self, j, way):
        for src, dst in self.parts(j):
            self.remote(j, src, dst, *self.way(way)).start()

    def share(self, j, k):
        piece = self.from_chip(j, k)
        return self.remote(j, piece, piece, 2 + k, 4 + k, self.other)

    def pass_on(self, j, k):
        piece = self.from_chip(j, k)
        return self.remote(j, piece, piece, 4 + k, 5 - k, self.to[1])

    def arrival(self, j, k):
        piece = self.from_chip(j, k)
        return self.remote(j, piece, piece, k, k, self.to[1])

    def shared(self, j, k):
        piece = self.from_chip(j, k, 1 - self.core)
        return self.remote(j, piece, piece, 4 + k if k else 0, 4 + k, self.other)

    def across(self, j):
        piece = self.from_chip(j, 1)
        return self.remote(j, piece, piece, 8, 2, self.to[3])

    def start(self, j):
        self.send_own(j, 1)

        @pl.when(self.middle)
        def _():
            self.send_own(j, 3)

        self.send_own(j, 0)
        for src, dst in self.parts(j):
            pltpu.make_async_copy(src, dst, self.copied.at[j]).start()

    def relay_near(self, j):
        self.arrival(j, 1).wait_recv()

        @pl.when(self.middle)
        def _():
            self.across(j).start()

        self.share(j, 1).start()

    def relay_far(self, j):
        for k in (3, 2):
            self.arrival(j, k).wait_recv()

            @pl.when(self.middle)
            def _():
                self.pass_on(j, k).start()

            self.share(j, k).start()

    def complete(self, j):
        self.keep(j).wait()
        for k in range(4):
            self.shared(j, k).wait_recv()

    def settle(self, j):
        self.first(j, 0).wait_send()
        self.first(j, 1).wait_send()

        @pl.when(self.middle)
        def _():
            self.first(j, 3).wait_send()
            self.across(j).wait_send()
            self.pass_on(j, 2).wait_send()
            self.pass_on(j, 3).wait_send()

        for k in (1, 2, 3):
            self.share(j, k).wait_send()


def pair_gates(logits, route_zero, route_one):
    experts = logits.shape[0]
    which = lax.broadcasted_iota(jnp.int32, logits.shape, 0)
    zero = jnp.sum(jnp.where(which == route_zero, logits, 0.0), axis=0, keepdims=True)
    one = jnp.sum(jnp.where(which == route_one, logits, 0.0), axis=0, keepdims=True)
    top = jnp.maximum(zero, one)
    zero, one = jnp.exp(zero - top), jnp.exp(one - top)
    total = zero + one
    return zero / total, one / total


class Dispatch:
    def __init__(self, expert, meta, rank, places):
        self.expert, self.meta, self.rank, self.places = expert, meta, rank, places
        self.blocks, _, self.slots = meta.shape

    def names(self, block):
        info = self.meta[block]
        valid = info[3:4, :] > 0
        zero = jnp.logical_and(valid, info[0:1, :] == self.expert)
        one = jnp.logical_and(valid, info[1:2, :] == self.expert)
        return info, zero, one

    def find_places(self):
        row_of = lax.broadcasted_iota(jnp.int32, (16, self.slots), 0)
        total_zero = jnp.zeros((1, 1), F32)
        for block in range(self.blocks):
            _, zero, _ = self.names(block)
            total_zero = total_zero + jnp.sum(zero.astype(F32), axis=1, keepdims=True)
            self.rank[block] = jnp.transpose(self.meta[block].astype(F32))

        def block_places(block, _):
            info, zero, one = self.names(block)
            mine = info[2:3, :].astype(F32)

            def earlier(other, counts):
                _, other_zero, other_one = self.names(other)
                marks = jnp.where(row_of == 0, other_zero.astype(F32), 0.0) + jnp.where(
                    row_of == 1, other_one.astype(F32), 0.0
                )
                before = (self.rank[other][:, 2:3] < mine).astype(F32).astype(BF16)
                return counts + dot(marks.astype(BF16), before)

            counts = lax.fori_loop(0, self.blocks, earlier, jnp.zeros((16, self.slots), F32))
            place = jnp.where(
                zero, counts[0:1, :], jnp.where(one, counts[1:2, :] + total_zero, -1.0)
            ).astype(jnp.int32)
            self.places[block] = jnp.broadcast_to(place, self.places.shape[1:])
            return 0

        lax.fori_loop(0, self.blocks, block_places, 0)

    def hot(self, block):
        return lax.broadcasted_iota(jnp.int32, (CAP, self.slots), 0) == self.places[block][0:1, :]

    def gates(self, block, rows, router_t):
        info, zero, one = self.names(block)
        gate_zero, gate_one = pair_gates(dot_nt(router_t, rows), info[0:1, :], info[1:2, :])
        gate = jnp.where(zero, gate_zero, jnp.where(one, gate_one, 0.0))
        return jnp.sum(jnp.where(self.hot(block), gate, 0.0), axis=1, keepdims=True)


def attend_forward(experts, tokens, weights, heads, hot, length, out, between):
    qkv, attended, probs, resid, normed_two, small, normed, diagonals = out
    slots, width = tokens.shape
    small[...] = jnp.transpose(weights[:, 4 * width :].astype(F32))[: small.shape[0], :]
    x = tokens[...].astype(F32)
    inv_one = lax.rsqrt(jnp.mean(x * x, axis=1, keepdims=True) + epsilon)
    normed[...] = (x * inv_one * small[experts : experts + 1, :]).astype(BF16)
    spread_bias = heads[...].astype(F32) * small[experts + 2 : experts + 3, :]
    diagonals[...] = dot(spread_bias.astype(BF16), hot[...])

    @pl.loop(0, 3 * width // 512)
    def _(j):
        qkv[:, columns(j, 512)] = dot(normed[...], weights[:, columns(j, 512)]).astype(BF16)

    lane = lax.broadcasted_iota(jnp.int32, (slots, LANES), 1)
    first = lane < HD
    live = lax.broadcasted_iota(jnp.int32, (slots, slots), 1) < length[0, 0]

    def attend(pair):
        q = qkv[:, columns(pair, LANES)]
        k = qkv[:, columns(PAIRS + pair, LANES)]
        v = qkv[:, columns(2 * PAIRS + pair, LANES)]
        outs = []
        for half in range(2):
            head = 2 * pair + half
            own = first if half == 0 else jnp.logical_not(first)
            row = jnp.broadcast_to(diagonals[pl.ds(head, 1), :], (slots, 2 * slots))
            bias = pltpu.roll(row, 0, 1, stride=1, stride_axis=0)[:, :slots]
            scores = dot_nt(jnp.where(own, q, jnp.zeros_like(q)), k) * SCALE + bias
            scores = jnp.where(live, scores, masked_value)
            exponent = jnp.exp(scores - jnp.max(scores, axis=1, keepdims=True))
            low = (exponent / jnp.sum(exponent, axis=1, keepdims=True)).astype(BF16)
            probs[head] = low
            outs.append(dot(low, v))
        attended[:, columns(pair, LANES)] = jnp.where(first, outs[0], outs[1]).astype(BF16)

    pl.loop(0, PAIRS // 2)(attend)
    between()
    pl.loop(PAIRS // 2, PAIRS)(attend)

    @pl.loop(0, width // 512)
    def _(j):
        resid[:, columns(j, 512)] = tokens[:, columns(j, 512)].astype(F32) + dot(
            attended[...], weights[:, columns(3 * width // 512 + j, 512)]
        )

    r = resid[...]
    inv_two = lax.rsqrt(jnp.mean(r * r, axis=1, keepdims=True) + epsilon)
    normed_two[...] = (r * inv_two * small[experts + 1 : experts + 2, :]).astype(BF16)


def attention_forward_kernel(
    experts,
    tokens,
    weights,
    heads,
    hot,
    length,
    qkv,
    attended,
    probs,
    resid,
    normed_two,
    small,
    *scratch,
):
    out = (qkv, attended, probs, resid, normed_two, small) + scratch
    attend_forward(experts, tokens, weights, heads, hot, length, out, lambda: None)


def attention_shapes(experts, tokens):
    slots, width = tokens.shape
    return (
        jax.ShapeDtypeStruct((slots, 3 * width), BF16),
        jax.ShapeDtypeStruct((slots, width), BF16),
        jax.ShapeDtypeStruct((HEADS, slots, slots), BF16),
        jax.ShapeDtypeStruct((slots, width), F32),
        jax.ShapeDtypeStruct((slots, width), BF16),
        jax.ShapeDtypeStruct((-(-(experts + 3) // 8) * 8, width), F32),
    )


def attention_forward(experts, tokens, weights, heads, hot, length):
    slots, width = tokens.shape
    return call(
        functools.partial(attention_forward_kernel, experts),
        attention_shapes(experts, tokens),
        [pltpu.VMEM((slots, width), BF16), pltpu.VMEM((HEADS, 2 * slots), F32)],
        48 * MB,
        2 * slots * width * (4 * width + 2 * slots),
        tokens,
        weights,
        heads,
        hot,
        length,
    )


def dispatch_kernel(
    rows, cots, meta, small, own, buffer, scaled, plain, select, gate_column, acc, acc_cot, rank, places
):
    work = Dispatch(own[0, 0], meta, rank, places)
    work.find_places()
    acc[...] = jnp.zeros_like(acc)
    acc_cot[...] = jnp.zeros_like(acc_cot)
    gate_column[...] = jnp.zeros_like(gate_column)
    router_t = small[...].astype(BF16)
    for block in range(work.blocks):
        picked = work.hot(block).astype(F32).astype(BF16)
        select[block] = picked
        gate_column[...] += work.gates(block, rows[block], router_t)
        acc[...] += dot(picked, rows[block])
        acc_cot[...] += dot(picked, cots[block])
    buffer[...] = acc[...].astype(BF16)
    plain[...] = acc_cot[...].astype(BF16)
    scaled[...] = (acc_cot[...] * gate_column[:, 0:1]).astype(BF16)


def dispatch_shapes(blocks, slots, width):
    return (
        jax.ShapeDtypeStruct((CAP, width), BF16),
        jax.ShapeDtypeStruct((CAP, width), BF16),
        jax.ShapeDtypeStruct((CAP, width), BF16),
        jax.ShapeDtypeStruct((blocks, CAP, slots), BF16),
        jax.ShapeDtypeStruct((CAP, 128), F32),
    )


def dispatch_scratch(blocks, slots, width):
    return [
        pltpu.VMEM((CAP, width), F32),
        pltpu.VMEM((CAP, width), F32),
        pltpu.VMEM((blocks, slots, 8), F32),
        pltpu.VMEM((blocks, 8, slots), jnp.int32),
    ]


def dispatch(rows, cots, meta, small, own):
    blocks, slots, width = rows.shape
    return call(
        dispatch_kernel,
        dispatch_shapes(blocks, slots, width),
        dispatch_scratch(blocks, slots, width),
        60 * MB,
        4 * CAP * blocks * slots * width,
        rows,
        cots,
        meta,
        small,
        own,
    )


def forward_kernel(
    experts,
    tokens,
    heads,
    hot,
    length,
    cotangent,
    meta,
    qkv_own,
    out_own,
    beside,
    qkv,
    attended,
    probs,
    resid,
    normed_two,
    small,
    buffer,
    scaled,
    plain,
    select,
    gate_column,
    kept,
    acc,
    acc_cot,
    rank,
    places,
    weights,
    rows,
    cots,
    metas,
    normed,
    diagonals,
    local,
    send,
    recv,
    gather_send,
    gather_recv,
):
    d, e, z, c = here()
    slots, width = tokens.shape
    share = qkv_own.shape[0]
    gather = DeviceGather(weights, share, gather_send, gather_recv)
    rows_spread = Spread(normed_two, rows, send.at[0], recv.at[0], d, e)
    cots_spread = Spread(cotangent, cots, send.at[1], recv.at[1], d, e)
    work = Dispatch(e, metas, rank, places)

    mine = gather.item(0, 0)
    own_parts = [
        pltpu.make_async_copy(part, mine.at[:, start : start + part.shape[1]], local.at[i])
        for i, (part, start) in enumerate(((qkv_own, 0), (out_own, 3 * width), (beside, 4 * width)))
    ]
    own_cots = pltpu.make_async_copy(cotangent, cots.at[0], local.at[3])
    for copy in own_parts:
        copy.start()
    meet(group(d, e)[1:] + [gather.other] + gather.to_z[1:])
    meta_copies = [
        push(meta, metas.at[q], send.at[2, q], recv.at[2, q], group(d, e)[q]) for q in (1, 2, 3)
    ]
    for copy in own_parts:
        copy.wait()
    gather.start()
    own_cots.start()
    metas[0] = meta[...]
    for copy in meta_copies:
        copy.wait_recv()
    work.find_places()
    for k in (1, 3, 2):
        gather.from_z(k)
        if k == 3:
            gather.from_neighbours(0)
    for k in (1, 3, 2):
        gather.from_neighbours(k)
    cots_spread.start()
    for k in (0, 1, 3, 2):
        gather.from_across(k)
    gather.complete()
    keep = pltpu.make_async_copy(weights, kept, local.at[4])
    keep.start()

    out = (qkv, attended, probs, resid, normed_two, small, normed, diagonals)
    attend_forward(experts, tokens, weights, heads, hot, length, out, cots_spread.forward)

    rows_spread.start()
    own_cots.wait()
    cots_spread.finish()
    router_t = small[...].astype(BF16)

    def take_cots(block):
        picked = work.hot(block).astype(F32).astype(BF16)
        select[block] = picked
        more = dot(picked, cots[block])
        if block:
            acc_cot[...] += more
        else:
            acc_cot[...] = more

    def take_rows(block, ref):
        gate = work.gates(block, ref[...], router_t)
        more = dot(select[block], ref[...])
        if block:
            gate_column[...] += gate
            acc[...] += more
        else:
            gate_column[...] = jnp.broadcast_to(gate, gate_column.shape)
            acc[...] = more

    take_cots(0)
    take_cots(1)
    rows_spread.forward()
    take_cots(2)
    take_cots(3)
    plain[...] = acc_cot[...].astype(BF16)
    take_rows(0, normed_two)
    rows_spread.arrived(1)
    take_rows(1, rows.at[1])
    rows_spread.arrived(2)
    take_rows(2, rows.at[2])
    rows_spread.arrived(3)
    take_rows(3, rows.at[3])
    buffer[...] = acc[...].astype(BF16)
    scaled[...] = (acc_cot[...] * gate_column[:, 0:1]).astype(BF16)
    rows_spread.sent()
    gather.settle()
    for copy in meta_copies:
        copy.wait_send()
    keep.wait()


def forward(experts, tokens, heads, hot, length, cotangent, meta, qkv_own, out_own, beside):
    slots, width = tokens.shape
    full = (32 * qkv_own.shape[0], 4 * width + beside.shape[1])
    block = (experts, slots, width)
    scratch = dispatch_scratch(*block) + [
        pltpu.VMEM(full, BF16),
        pltpu.VMEM(block, BF16),
        pltpu.VMEM(block, BF16),
        pltpu.VMEM((experts,) + meta.shape, jnp.int32),
        pltpu.VMEM((slots, width), BF16),
        pltpu.VMEM((HEADS, 2 * slots), F32),
        DMA((5,)),
        DMA((3, 6)),
        DMA((3, 6)),
        DMA((5, 16)),
        DMA((5, 16)),
    ]
    shapes = attention_shapes(experts, tokens) + dispatch_shapes(*block)
    return call(
        functools.partial(forward_kernel, experts),
        shapes + (jax.ShapeDtypeStruct(full, BF16),),
        scratch,
        60 * MB,
        2 * slots * width * (4 * width + 2 * slots),
        tokens,
        heads,
        hot,
        length,
        cotangent,
        meta,
        qkv_own,
        out_own,
        beside,
        stay=(4, 6, 7, 8),
        land=(len(shapes),),
        link=0,
    )


CHUNK = 256
GELU_A = math.sqrt(2.0 / math.pi)
GELU_B = 0.044715


def expert_chunk(buffer, scaled, gate, up, down):
    gate_in, up_in = dot(buffer, gate), dot(buffer, up)
    square = gate_in * gate_in
    wave = jnp.tanh(GELU_A * gate_in * (1.0 + GELU_B * square))
    half = 0.5 * (1.0 + wave)
    activated = gate_in * half
    slope = half + (0.5 * GELU_A) * gate_in * (1.0 - wave * wave) * (1.0 + 3.0 * GELU_B * square)
    hidden = (activated * up_in).astype(BF16)
    grad_hidden = dot_nt(scaled, down)
    grad_gate_in = (grad_hidden * up_in * slope).astype(BF16)
    grad_up_in = (grad_hidden * activated).astype(BF16)
    grad_buffer = dot_nt(grad_gate_in, gate) + dot_nt(grad_up_in, up)
    return (
        dot(hidden, down),
        grad_buffer,
        dot_tn(buffer, grad_gate_in),
        dot_tn(buffer, grad_up_in),
        dot_tn(hidden, scaled),
    )


def expert_kernel(
    buffer,
    scaled,
    plain,
    gate,
    up,
    down,
    out,
    grad_buffer,
    inner,
    grad_gate,
    grad_up,
    grad_down,
    acc_out,
    acc_grad,
):
    step = pl.program_id(0)

    @pl.when(step == 0)
    def _():
        acc_out[...] = jnp.zeros_like(acc_out)
        acc_grad[...] = jnp.zeros_like(acc_grad)

    more_out, more_grad, d_gate, d_up, d_down = expert_chunk(
        buffer[...], scaled[...], gate[...], up[...], down[...]
    )
    acc_out[...] += more_out
    acc_grad[...] += more_grad
    grad_gate[...] = d_gate.astype(BF16)
    grad_up[...] = d_up.astype(BF16)
    grad_down[...] = d_down.astype(BF16)

    @pl.when(step == pl.num_programs(0) - 1)
    def _():
        low = acc_out[...].astype(BF16)
        out[...] = low
        grad_buffer[...] = acc_grad[...].astype(BF16)
        inner[...] = jnp.broadcast_to(
            jnp.sum(low.astype(F32) * plain[...].astype(F32), axis=1, keepdims=True), inner.shape
        )


def experts(buffer, scaled, plain, gate, up, down):
    rows, width = buffer.shape
    hidden = gate.shape[1]
    whole = pl.BlockSpec((rows, width), lambda j: (0, 0))
    tall = pl.BlockSpec((width, CHUNK), lambda j: (0, j))
    wide = pl.BlockSpec((CHUNK, width), lambda j: (j, 0))
    shapes = (
        jax.ShapeDtypeStruct((rows, width), BF16),
        jax.ShapeDtypeStruct((rows, width), BF16),
        jax.ShapeDtypeStruct((rows, 128), F32),
        jax.ShapeDtypeStruct((width, hidden), BF16),
        jax.ShapeDtypeStruct((width, hidden), BF16),
        jax.ShapeDtypeStruct((hidden, width), BF16),
    )
    return pl.pallas_call(
        expert_kernel,
        out_shape=shapes,
        grid=(hidden // CHUNK,),
        in_specs=[whole, whole, whole, tall, tall, wide],
        out_specs=(whole, whole, pl.BlockSpec((rows, 128), lambda j: (0, 0)), tall, tall, wide),
        scratch_shapes=[pltpu.VMEM((rows, width), F32), pltpu.VMEM((rows, width), F32)],
        compiler_params=pltpu.CompilerParams(
            vmem_limit_bytes=48 * MB, dimension_semantics=("arbitrary",)
        ),
        cost_estimate=pl.CostEstimate(
            flops=18 * rows * width * hidden,
            bytes_accessed=12 * width * hidden,
            transcendentals=rows * hidden,
        ),
    )(buffer, scaled, plain, gate, up, down)


def give_back_kernel(select, out, grad_buffer, inner, gate_column, mixed, grads, inner_rows):
    weighted = (out[...].astype(F32) * gate_column[:, 0:1]).astype(BF16)
    for block in range(select.shape[0]):
        row = jnp.sum(select[block].astype(F32) * inner[:, 0:1], axis=0, keepdims=True)
        inner_rows[block] = jnp.broadcast_to(row, inner_rows.shape[1:])
        grads[block] = dot_tn(select[block], grad_buffer[...]).astype(BF16)
        mixed[block] = dot_tn(select[block], weighted).astype(BF16)


def give_back(select, out, grad_buffer, inner, gate_column):
    blocks, rows, slots = select.shape
    width = out.shape[1]
    wide = (blocks, slots, width)
    return call(
        give_back_kernel,
        (
            jax.ShapeDtypeStruct(wide, BF16),
            jax.ShapeDtypeStruct(wide, BF16),
            jax.ShapeDtypeStruct((blocks, 8, slots), F32),
        ),
        [],
        56 * MB,
        4 * rows * blocks * slots * width,
        select,
        out,
        grad_buffer,
        inner,
        gate_column,
    )


TILE = 2 * CHUNK


def sweep_kernel(
    ready,
    buffer,
    scaled,
    plain,
    gate_column,
    select,
    gate_own,
    up_own,
    early,
    down_full,
    gate_sum,
    up_sum,
    grad_down,
    mixed,
    returned,
    inner_full,
    sums,
    both,
    down,
    acc_out,
    acc_grad,
    down_stage,
    grads,
    inner_rows,
    loaded,
    stored,
    local,
    swap_send,
    swap_recv,
    *scratch,
):
    tiles, width = both.shape[0], both.shape[1]
    share = gate_own.shape[0]
    coming = tiles - ready
    d, e, z, c = here()

    def columns_of(tile):
        return pl.ds(pl.multiple_of(tile * TILE, TILE), TILE)

    def rows_of(device):
        return pl.ds(pl.multiple_of(device * share, share), share)

    spread = LineSpread(
        lambda j: [own.at[:, columns(ready + j, CHUNK)] for own in (gate_own, up_own)],
        lambda j, device: both.at[ready + j, rows_of(device)],
        scratch[:3],
    )
    line = LineSum(
        tiles,
        lambda i, k, core: both.at[i, rows_of(2 * flipped(z, k) + core)],
        scratch[3:],
        load=False,
    )
    swap = Swap(grads, returned, swap_send.at[0], swap_recv.at[0], d, e)
    inner_swap = Swap(inner_rows, inner_full, swap_send.at[1], swap_recv.at[1], d, e)
    meet(group(d, e)[1:] + [line.other] + line.to[1:])

    def early_load(t):
        return pltpu.make_async_copy(early.at[:, columns_of(t)], both.at[t], loaded.at[t])

    down_load = pltpu.make_async_copy(down_full, down, loaded.at[tiles])
    for t in range(ready):
        early_load(t).start()
        if t == 0:
            down_load.start()
    for j in range(min(DEPTH, coming)):
        spread.start(j)
    acc_out[...] = jnp.zeros_like(acc_out)
    acc_grad[...] = jnp.zeros_like(acc_grad)
    down_load.wait()

    def down_rows(t):
        return pl.ds(pl.multiple_of(t * CHUNK, CHUNK), CHUNK)

    def down_store(t, slot):
        return pltpu.make_async_copy(
            down_stage.at[slot], grad_down.at[down_rows(t)], stored.at[slot]
        )

    def between(low, value, high):
        return jnp.logical_and(value >= low, value < high)

    def tile_step(t, _):
        @pl.when(t < ready)
        def _():
            early_load(t).wait()

        near = t - ready + NEAR

        @pl.when(between(0, near, coming))
        def _():
            spread.relay_near(near)

        @pl.when(between(0, near - 1, coming))
        def _():
            spread.relay_far(near - 1)

        @pl.when(between(DEPTH, near - 1 + DEPTH, coming))
        def _():
            spread.start(near - 1 + DEPTH)

        @pl.when(t >= ready)
        def _():
            spread.complete(t - ready)

        @pl.when(t >= 1)
        def _():
            line.halve(t - 1)

        @pl.when(t >= LAG)
        def _():
            line.relay(t - LAG)

        @pl.when(t >= LAG + 1)
        def _():
            line.pass_on(t - LAG - 1)

        more_out, more_grad, d_gate, d_up, d_down = expert_chunk(
            buffer[...], scaled[...], both[t, :, :CHUNK], both[t, :, CHUNK:], down[down_rows(t)]
        )
        acc_out[...] += more_out
        acc_grad[...] += more_grad

        @pl.when(t >= ready)
        def _():
            spread.settle(t - ready)

        both[t, :, :CHUNK] = d_gate.astype(BF16)
        both[t, :, CHUNK:] = d_up.astype(BF16)
        slot = lax.rem(t, 2)

        @pl.when(t >= 2)
        def _():
            down_store(t - 2, slot).wait()

        down_stage[slot] = d_down.astype(BF16)
        down_store(t, slot).start()
        line.begin(t)
        return 0

    lax.fori_loop(0, tiles, tile_step, 0)

    low = acc_out[...].astype(BF16)
    inner = jnp.sum(low.astype(F32) * plain[...].astype(F32), axis=1, keepdims=True)
    grad_low = acc_grad[...].astype(BF16)
    order = (3, 1, 2, 0)
    for block in order:
        row = jnp.sum(select[block].astype(F32) * inner, axis=0, keepdims=True)
        inner_rows[block] = jnp.broadcast_to(row, inner_rows.shape[1:])
        grads[block] = dot_tn(select[block], grad_low).astype(BF16)
        if block:
            inner_swap.start(block)
            swap.start(block)
    own_copies = [
        pltpu.make_async_copy(grads.at[0], returned.at[0], local.at[0]),
        pltpu.make_async_copy(inner_rows.at[0], inner_full.at[0], local.at[1]),
    ]
    for copy in own_copies:
        copy.start()
    line.halve(tiles - 1)
    weighted = (low.astype(F32) * gate_column[:, 0:1]).astype(BF16)
    for block in order:
        mixed[block] = dot_tn(select[block], weighted).astype(BF16)

    @pl.loop(tiles - LAG, tiles + 1)
    def _(i):
        @pl.when(i < tiles)
        def _():
            line.relay(i)

        line.pass_on(i - 1)

    @pl.loop(0, tiles)
    def _(i):
        line.finish(i, sums.at[i])
        for copy in result_stores(sums.at[i], gate_sum, up_sum, i, local.at[2]):
            copy.start()

    @pl.loop(0, tiles)
    def _(i):
        for copy in result_stores(sums.at[i], gate_sum, up_sum, i, local.at[2]):
            copy.wait()

    for t in range(tiles - 2, tiles):
        down_store(t, t % 2).wait()
    for copy in own_copies:
        copy.wait()
    inner_swap.finish()
    swap.finish()


def result_stores(value, gate_sum, up_sum, tile, sem):
    return [
        pltpu.make_async_copy(
            value.at[:, i * CHUNK : (i + 1) * CHUNK], array.at[:, columns(tile, CHUNK)], sem
        )
        for i, array in enumerate((gate_sum, up_sum))
    ]


LAG = 5

DEPTH = 6
NEAR = 2


def sweep(ready, buffer, scaled, plain, gate_column, select, gate_own, up_own, early, down_full):
    rows, width = buffer.shape
    tiles = gate_own.shape[1] // CHUNK
    share = gate_own.shape[0]
    block = (select.shape[0], select.shape[2], width)
    thin = (select.shape[0], 8, select.shape[2])
    hidden = tiles * CHUNK
    shapes = (
        jax.ShapeDtypeStruct(gate_own.shape, F32),
        jax.ShapeDtypeStruct(gate_own.shape, F32),
        jax.ShapeDtypeStruct(down_full.shape, BF16),
        jax.ShapeDtypeStruct(block, BF16),
        jax.ShapeDtypeStruct(block, BF16),
        jax.ShapeDtypeStruct(thin, F32),
    )
    scratch = [
        pltpu.VMEM((tiles, share, TILE), F32),
        pltpu.VMEM((tiles, width, TILE), BF16),
        pltpu.VMEM(down_full.shape, BF16),
        pltpu.VMEM((rows, width), F32),
        pltpu.VMEM((rows, width), F32),
        pltpu.VMEM((2, CHUNK, width), BF16),
        pltpu.VMEM(block, BF16),
        pltpu.VMEM(thin, F32),
        DMA((tiles + 1,)),
        DMA((2,)),
        DMA((3,)),
        DMA((2, 4)),
        DMA((2, 4)),
    ]
    scratch += LineSpread.scratch(tiles - ready) + LineSum.scratch(tiles, share, TILE, False)
    return call(
        functools.partial(sweep_kernel, ready),
        shapes,
        scratch,
        62 * MB,
        18 * rows * width * hidden,
        buffer,
        scaled,
        plain,
        gate_column,
        select,
        gate_own,
        up_own,
        early,
        down_full,
        stay=(5, 6, 7, 8),
        land=(0, 1, 2, 4, 5),
        link=2,
    )


PARTS = 4


def backward_layer(experts, relative, ins, outs, work, reached):
    tokens, cotangent, weights, small, heads, hot_back, length, meta, own = ins[:9]
    returned, inner_rows, qkv, attended, probs, resid, normed_two = ins[9:]
    grad_tokens, grad_small, grad_out, *grad_halves = outs
    grad_attended, grad_qkv, branch, normed, grad_resid, grad_diagonals = work
    slots, width = tokens.shape
    blocks = returned.shape[0]
    router_t = small[...].astype(BF16)
    keep_row = lax.broadcasted_iota(jnp.int32, (slots, 1), 0) < length[0, 0]
    logits = dot_nt(router_t, normed_two[...])
    zero_route, one_route = meta[0:1, :], meta[1:2, :]
    gate_zero, gate_one = pair_gates(logits, zero_route, one_route)
    which = lax.broadcasted_iota(jnp.int32, logits.shape, 0)
    grad_zero = jnp.zeros((1, slots), F32)
    grad_one = jnp.zeros((1, slots), F32)
    for block in range(blocks):
        row = inner_rows[block][0:1, :]
        expert = jnp.bitwise_xor(own[0, 0], block) if relative else block
        grad_zero = grad_zero + jnp.where(zero_route == expert, row, 0.0)
        grad_one = grad_one + jnp.where(one_route == expert, row, 0.0)
    shared = gate_zero * grad_zero + gate_one * grad_one
    grad_zero = gate_zero * (grad_zero - shared)
    grad_one = gate_one * (grad_one - shared)
    grad_logits = jnp.where(which == zero_route, grad_zero, 0.0) + jnp.where(
        which == one_route, grad_one, 0.0
    )
    high, low = two_halves(grad_logits)
    grad_small[...] = dot(high, normed_two[...]) + dot(low, normed_two[...])
    grad_normed_two = dot_tn(high, router_t) + dot_tn(low, router_t)
    for block in range(blocks):
        grad_normed_two = grad_normed_two + returned[block].astype(F32)
    r = resid[...]
    inv_two = lax.rsqrt(jnp.mean(r * r, axis=1, keepdims=True) + epsilon)
    unit_two = r * inv_two
    grad_small[experts + 1 : experts + 2, :] = jnp.sum(
        grad_normed_two * unit_two, axis=0, keepdims=True
    )
    scaled_two = small[experts + 1 : experts + 2, :] * grad_normed_two
    grad_resid[...] = jnp.where(keep_row, cotangent[...].astype(F32), 0.0) + inv_two * (
        scaled_two - unit_two * jnp.mean(scaled_two * unit_two, axis=1, keepdims=True)
    )
    branch[...] = grad_resid[...].astype(BF16)
    reached("branch")

    @pl.loop(0, width // 256)
    def _(j):
        grad_out[:, columns(j, 256)] = dot_tn(attended[...], branch[:, columns(j, 256)]).astype(
            BF16
        )

    reached("out")
    grad_attended[...] = dot_nt(branch[...], weights[:, 3 * width : 4 * width]).astype(BF16)
    x = tokens[...].astype(F32)
    inv_one = lax.rsqrt(jnp.mean(x * x, axis=1, keepdims=True) + epsilon)
    normed[...] = (x * inv_one * small[experts : experts + 1, :]).astype(BF16)
    reached("attended")

    lane = lax.broadcasted_iota(jnp.int32, (slots, LANES), 1)
    first = lane < HD
    square = (slots, slots)
    flip = (
        lax.broadcasted_iota(jnp.int32, square, 0) + lax.broadcasted_iota(jnp.int32, square, 1)
        == slots - 1
    )
    flip = flip.astype(F32).astype(BF16)

    def attend_back(pair):
        q = qkv[:, columns(pair, LANES)]
        k = qkv[:, columns(PAIRS + pair, LANES)]
        v = qkv[:, columns(2 * PAIRS + pair, LANES)]
        g = grad_attended[:, columns(pair, LANES)]
        dq, dk, dv = [], [], []
        for half in range(2):
            head = 2 * pair + half
            mine = first if half == 0 else jnp.logical_not(first)
            low = probs[head]
            p = low.astype(F32)
            grad_probs = dot_nt(jnp.where(mine, g, jnp.zeros_like(g)), v)
            ds = p * (grad_probs - jnp.sum(p * grad_probs, axis=1, keepdims=True))
            ds = ds.astype(BF16)
            wide = jnp.concatenate([dot(flip, ds), jnp.zeros((slots, slots), F32)], axis=1)
            skewed = pltpu.roll(wide, 0, 1, stride=1, stride_axis=0)
            grad_diagonals[pl.ds(head, 1), :] = jnp.sum(skewed, axis=0, keepdims=True)
            dq.append(dot(ds, k))
            dk.append(dot_tn(ds, q))
            dv.append(dot_tn(low, g))
        grad_qkv[:, columns(pair, LANES)] = (jnp.where(first, dq[0], dq[1]) * SCALE).astype(BF16)
        grad_qkv[:, columns(PAIRS + pair, LANES)] = (
            jnp.where(first, dk[0], dk[1]) * SCALE
        ).astype(BF16)
        grad_qkv[:, columns(2 * PAIRS + pair, LANES)] = jnp.where(first, dv[0], dv[1]).astype(BF16)

    for part in range(PARTS):
        pl.loop(part * PAIRS // PARTS, (part + 1) * PAIRS // PARTS)(attend_back)
        reached(f"part{part}")
        if part % 2 == 1:
            half, wide = part // 2, width // 2
            for i in range(3):
                for j in range(wide // 256):
                    source = i * width + half * wide + j * 256
                    at = i * wide + j * 256
                    grad_halves[half][:, at : at + 256] = dot_tn(
                        normed[...], grad_qkv[:, source : source + 256]
                    ).astype(BF16)
            reached(f"half{half}")

    high, low = two_halves(grad_diagonals[...])
    by_lane = dot_nt(high, hot_back[...]) + dot_nt(low, hot_back[...])
    grad_small[experts + 2 : experts + 3, :] = jnp.sum(
        by_lane * heads[...].astype(F32), axis=0, keepdims=True
    )
    grad_normed = dot_nt(grad_qkv[...], weights[:, : 3 * width])
    x = tokens[...].astype(F32)
    inv_one = lax.rsqrt(jnp.mean(x * x, axis=1, keepdims=True) + epsilon)
    unit_one = x * inv_one
    grad_small[experts : experts + 1, :] = jnp.sum(grad_normed * unit_one, axis=0, keepdims=True)
    scaled_one = small[experts : experts + 1, :] * grad_normed
    grad_tokens[...] = grad_resid[...] + inv_one * (
        scaled_one - unit_one * jnp.mean(scaled_one * unit_one, axis=1, keepdims=True)
    )
    reached("tokens")


def backward_scratch(slots, width):
    return [
        pltpu.VMEM((slots, width), BF16),
        pltpu.VMEM((slots, 3 * width), BF16),
        pltpu.VMEM((slots, width), BF16),
        pltpu.VMEM((slots, width), BF16),
        pltpu.VMEM((slots, width), F32),
        pltpu.VMEM((HEADS, 2 * slots), F32),
    ]


def add_mixed(output, resid, length, parts):
    keep_row = lax.broadcasted_iota(jnp.int32, (resid.shape[0], 1), 0) < length[0, 0]
    total = resid[...]
    for part in parts:
        total = total + part[...].astype(F32)
    output[...] = jnp.where(keep_row, total, 0.0).astype(BF16)


def local_backward_kernel(experts, *refs):
    ins, mixed, output, outs, work = refs[:16], refs[16], refs[17], refs[18:23], refs[23:]
    backward_layer(experts, False, ins, outs, work, lambda name: None)
    add_mixed(output, ins[14], ins[6], [mixed.at[block] for block in range(mixed.shape[0])])


def local_backward(experts, *args):
    tokens, small = args[0], args[3]
    slots, width = tokens.shape
    return call(
        functools.partial(local_backward_kernel, experts),
        (
            jax.ShapeDtypeStruct((slots, width), BF16),
            jax.ShapeDtypeStruct((slots, width), F32),
            jax.ShapeDtypeStruct(small.shape, F32),
            jax.ShapeDtypeStruct((width, width), BF16),
            jax.ShapeDtypeStruct((width, 3 * width // 2), BF16),
            jax.ShapeDtypeStruct((width, 3 * width // 2), BF16),
        ),
        backward_scratch(slots, width),
        62 * MB,
        4 * slots * width * (4 * width + 2 * slots),
        *args,
    )


class DeviceSum:
    @staticmethod
    def scratch(share, width):
        return [
            pltpu.VMEM((4, 4 * share, width), BF16),
            pltpu.VMEM((4, 2, share, width), BF16),
            pltpu.VMEM((4, share, width), BF16),
            DMA((4, 4)),
            DMA((4, 4)),
        ] + LineSum.scratch(1, share, width, False)

    def __init__(self, partial, scratch):
        self.partial = partial
        self.theirs, self.first_in, self.second_in, self.send, self.recv = scratch[:5]
        self.line = LineSum(1, None, scratch[5:], False)
        self.share = self.second_in.shape[1]
        self.d, self.e, self.z, self.core = here()
        self.other = (2 * self.z + 1 - self.core, self.e)
        self.to_x, self.to_y = (self.d, flipped(self.e, 1)), (self.d, flipped(self.e, 2))

    def rows(self, k, core, start, count):
        row = (2 * flipped(self.z, k) + core) * 4 * self.share + start
        return self.partial.at[pl.ds(pl.multiple_of(row, self.share), count)]

    def piece(self, k, q):
        return self.rows(k, self.core, flipped(self.e, q) * self.share, self.share)

    def remote(self, src, dst, stage, k, to):
        return pltpu.make_async_remote_copy(
            src_ref=src,
            dst_ref=dst,
            send_sem=self.send.at[stage, k],
            recv_sem=self.recv.at[stage, k],
            device_id=to,
            device_id_type=MESH,
        )

    def swap(self, k):
        src = self.rows(k, 1 - self.core, 0, 4 * self.share)
        return self.remote(src, self.theirs.at[k], 0, k, self.other)

    def first(self, k, slot):
        near, to = (1, self.to_x) if k % 2 == 0 else (2, self.to_y)
        return self.remote(
            self.piece(k, 3 if slot else near), self.first_in.at[k, slot], 1 + slot, k, to
        )

    def far(self, k):
        return 2 if k % 2 == 0 else 1

    def second(self, k):
        to = self.to_y if k % 2 == 0 else self.to_x
        return self.remote(self.piece(k, self.far(k)), self.second_in.at[k], 3, k, to)

    def begin(self):
        for k in (3, 2, 1, 0):
            self.swap(k).start()

    def stage_one(self):
        for k in (3, 2, 1, 0):
            self.swap(k).wait_recv()

            @pl.loop(0, 4)
            def _(j):
                start = pl.multiple_of(j * self.share, self.share)
                mine = self.rows(k, self.core, start, self.share)
                mine[...] = (
                    mine[...].astype(F32) + self.theirs[k, pl.ds(start, self.share)].astype(F32)
                ).astype(BF16)

            self.first(k, 1).start()
            self.first(k, 0).start()

    def stage_two(self):
        for k in (3, 2, 1, 0):
            self.first(k, 1).wait_recv()
            source = self.piece(k, self.far(k))
            source[...] = (source[...].astype(F32) + self.first_in[k, 1].astype(F32)).astype(BF16)
            self.second(k).start()

    def stage_three(self):
        for k in (3, 2, 1, 0):
            self.first(k, 0).wait_recv()
            self.second(k).wait_recv()
            total = self.piece(k, 0)[...].astype(F32) + self.first_in[k, 0].astype(F32)
            self.line.theirs[0, k] = (total + self.second_in[k].astype(F32)).astype(BF16)
        self.line.hand_over(0)

    def settle(self):
        for k in range(4):
            self.swap(k).wait_send()
            self.first(k, 0).wait_send()
            self.first(k, 1).wait_send()
            self.second(k).wait_send()


class EverySum:
    @staticmethod
    def scratch(shape):
        return [
            pltpu.VMEM((6,) + shape, F32),
            pltpu.VMEM((5,) + shape, F32),
            DMA((5,)),
            DMA((5,)),
        ]

    def __init__(self, scratch):
        self.sums, self.landed, self.send, self.recv = scratch
        d, e, z, c = here()
        near = [(2 * flipped(z, k) + c, e) for k in (1, 2)]
        self.to = [(2 * z + 1 - c, e), (d, flipped(e, 1)), (d, flipped(e, 2))] + near

    def copy(self, at):
        return pltpu.make_async_remote_copy(
            src_ref=self.sums.at[at],
            dst_ref=self.landed.at[at],
            send_sem=self.send.at[at],
            recv_sem=self.recv.at[at],
            device_id=self.to[at],
            device_id_type=MESH,
        )

    def start(self, value):
        self.sums[0] = value
        self.copy(0).start()

    def step(self, at):
        self.copy(at).wait_recv()
        self.sums[at + 1] = self.sums[at] + self.landed[at]
        if at + 1 < len(self.to):
            self.copy(at + 1).start()

    def settle(self):
        for at in range(len(self.to)):
            self.copy(at).wait_send()


def down_source(array, z, share):
    def source(i, k, core):
        row = pl.multiple_of((2 * flipped(z, k) + core) * share, share)
        return array.at[pl.ds(row, share), pl.ds(pl.multiple_of(i * CHUNK, CHUNK), CHUNK)]

    return source


def backward_kernel(experts, *refs):
    refs = list(refs)

    def take(count):
        taken, refs[:] = refs[:count], refs[count:]
        return taken

    ins = take(16)
    mixed, grad_down = take(2)
    output, grad_tokens, qkv_sum, out_sum, small_sum, down_sum = take(6)
    grad_small, grad_out, *grad_halves = take(4)
    work = take(6)
    (half_sums,) = take(1)
    mixed_full, mixed_send, mixed_recv = take(3)
    d, e, z, _ = here()
    width = out_sum.shape[1]
    down = LineSum(width // CHUNK, down_source(grad_down, z, down_sum.shape[0]), take(6), True)
    out = DeviceSum(grad_out, take(9))
    halves = [DeviceSum(grad_half, take(9)) for grad_half in grad_halves]
    every = EverySum(take(4))
    swap = Swap(mixed, mixed_full, mixed_send, mixed_recv, d, e)
    meet(group(d, e)[1:] + [down.other] + down.to[1:])
    for i in range(down.count):
        down.begin(i)
    down.halve(0)

    def reached(name):
        if name == "branch":
            down.halve(1)
        elif name == "out":
            out.begin()
        elif name == "attended":
            down.halve(2)
        elif name == "part0":
            out.stage_one()
            down.relay(0)
        elif name == "part1":
            out.stage_two()
        elif name == "half0":
            halves[0].begin()
            down.pass_on(0)
            down.relay(1)
        elif name == "part2":
            halves[0].stage_one()
            out.stage_three()
            down.halve(3)
        elif name == "part3":
            halves[0].stage_two()
            down.pass_on(1)
        elif name == "half1":
            halves[1].begin()
            down.relay(2)
        elif name == "tokens":
            every.start(grad_small[...])
            halves[1].stage_one()
            for block in (3, 1, 2):
                swap.start(block)

    outs = [grad_tokens, grad_small, grad_out] + grad_halves
    backward_layer(experts, True, ins, outs, work, reached)
    halves[0].stage_three()
    every.step(0)
    halves[1].stage_two()
    out.line.relay(0)
    every.step(1)
    down.pass_on(2)
    down.relay(3)
    out.line.pass_on(0)
    halves[1].stage_three()
    every.step(2)
    halves[0].line.relay(0)
    down.pass_on(3)
    every.step(3)
    halves[0].line.pass_on(0)
    halves[1].line.relay(0)
    every.step(4)
    small_sum[...] = every.sums[5]
    for i in range(down.count):
        down.finish(i, down_sum.at[:, i * CHUNK : (i + 1) * CHUNK])
    halves[1].line.pass_on(0)
    swap.finish()
    add_mixed(output, ins[14], ins[6], [mixed.at[0]] + [mixed_full.at[q] for q in (1, 2, 3)])
    out.line.finish(0, out_sum)
    wide = width // 2
    for half, sums in enumerate(halves):
        sums.line.finish(0, half_sums.at[half])
        for i in range(3):
            at = i * width + half * wide
            qkv_sum[:, at : at + wide] = half_sums[half, :, i * wide : (i + 1) * wide]
    for sums in [out] + halves:
        sums.settle()
    every.settle()


def backward(experts, *args):
    tokens, small, mixed, grad_down = args[0], args[3], args[16], args[17]
    slots, width = tokens.shape
    share, down_share = width // 32, grad_down.shape[0] // 8
    half = 3 * width // 2
    scratch = [
        pltpu.VMEM(small.shape, F32),
        pltpu.VMEM((width, width), BF16),
        pltpu.VMEM((width, half), BF16),
        pltpu.VMEM((width, half), BF16),
        *backward_scratch(slots, width),
        pltpu.VMEM((2, share, half), F32),
        pltpu.VMEM(mixed.shape, BF16),
        DMA((4,)),
        DMA((4,)),
        *LineSum.scratch(width // CHUNK, down_share, CHUNK, True),
        *DeviceSum.scratch(share, width),
        *DeviceSum.scratch(share, half),
        *DeviceSum.scratch(share, half),
        *EverySum.scratch(small.shape),
    ]
    return call(
        functools.partial(backward_kernel, experts),
        (
            jax.ShapeDtypeStruct((slots, width), BF16),
            jax.ShapeDtypeStruct((slots, width), F32),
            jax.ShapeDtypeStruct((share, 3 * width), F32),
            jax.ShapeDtypeStruct((share, width), F32),
            jax.ShapeDtypeStruct(small.shape, F32),
            jax.ShapeDtypeStruct((down_share, width), F32),
        ),
        scratch,
        63 * MB,
        4 * slots * width * (4 * width + 2 * slots),
        *args,
        stay=(17,),
        link=3,
    )


READY = 2


def on_device(
    fast,
    tokens,
    cotangent,
    qkv_weight,
    out_weight,
    router_weight,
    first_gain,
    second_gain,
    bias_table,
    gate_weight,
    up_weight,
    down_weight,
    lengths,
    routes,
    priority,
):
    both = ("dp", "expert")
    slots, width = tokens.shape
    expert_count = lax.axis_size("expert")
    device_count = lax.axis_size("dp") * expert_count
    share, bias_share = first_gain.shape[0], bias_table.shape[0]
    device = lax.axis_index("dp") * expert_count + lax.axis_index("expert")
    own = lax.axis_index("expert").astype(jnp.int32).reshape(1, 1)
    small_rows = -(-(expert_count + 3) // 8) * 8

    def gathered(value, axes, axis=0, tiled=True):
        return lax.all_gather(value, axes, axis=axis, tiled=tiled)

    def scattered(value, axes):
        return lax.psum_scatter(value, axes, scatter_dimension=0, tiled=True).astype(F32)

    def exchanged(value):
        return lax.all_to_all(value, "expert", split_axis=0, concat_axis=0, tiled=True)

    rows_own, hidden = gate_weight.shape[1:]
    down_full = gathered(down_weight[0], "dp")
    if fast:
        cut = (rows_own, READY, 1, CHUNK)
        early = jnp.concatenate(
            [value[0, :, : READY * CHUNK].reshape(cut) for value in (gate_weight, up_weight)],
            axis=2,
        ).reshape(rows_own, READY * TILE)
        early = gathered(early, "dp")
    else:
        gate_full, up_full = (gathered(value[0], "dp") for value in (gate_weight, up_weight))

    beside = jnp.concatenate(
        [
            router_weight,
            first_gain[:, None],
            second_gain[:, None],
            jnp.pad(bias_table, (0, share - bias_share))[:, None],
            jnp.zeros((share, 128 - expert_count - 3), BF16),
        ],
        axis=1,
    )
    lane = np.arange(width)
    flat = lane // share * bias_share + lane % share
    in_table = lane % share < bias_share
    heads = np.arange(HEADS)[:, None] == np.where(in_table, flat // BUCKETS, -1)[None, :]
    heads = jnp.asarray(heads.astype(np.float32), BF16)
    ahead = np.arange(2 * slots)

    def hot(ahead):
        return jnp.asarray(
            np.where(in_table[:, None], diagonal_onehot(ahead)[flat % BUCKETS], 0.0), BF16
        )

    valid_rows = jnp.arange(slots, dtype=jnp.int32) < lengths[0, 0]
    meta_own = jnp.concatenate(
        [
            routes.T,
            priority,
            valid_rows.astype(jnp.int32)[None, :],
            jnp.zeros((4, slots), jnp.int32),
        ],
        axis=0,
    )

    diagonals_hot = hot(np.where(ahead < slots, ahead, ahead - 2 * slots))
    if fast:
        *kept, buffer, scaled, plain, select, gate_column, weights = forward(
            expert_count,
            tokens,
            heads,
            diagonals_hot,
            lengths,
            cotangent,
            meta_own,
            qkv_weight,
            out_weight,
            beside,
        )
    else:
        weights = gathered(jnp.concatenate([qkv_weight, out_weight, beside], axis=1), both)
        kept = attention_forward(expert_count, tokens, weights, heads, diagonals_hot, lengths)
        rows, cots, meta = (
            gathered(value, "expert", tiled=False) for value in (kept[4], cotangent, meta_own)
        )
        buffer, scaled, plain, select, gate_column = dispatch(rows, cots, meta, kept[5], own)
    qkv, attended, probs, resid, normed_two, small = kept
    if fast:
        grad_gate, grad_up, grad_down, mixed, returned, inner_rows = sweep(
            READY,
            buffer,
            scaled,
            plain,
            gate_column,
            select,
            gate_weight[0],
            up_weight[0],
            early,
            down_full,
        )
    else:
        expert_out, grad_buffer, inner, *grad_experts = experts(
            buffer, scaled, plain, gate_full, up_full, down_full
        )
        mixed, returned, inner_rows = (
            exchanged(value)
            for value in give_back(select, expert_out, grad_buffer, inner, gate_column)
        )
        grad_gate, grad_up, grad_down = (scattered(value, "dp")[None] for value in grad_experts)
    layer = (
        tokens,
        cotangent,
        weights,
        small,
        heads,
        hot(ahead - (slots - 1)),
        lengths,
        meta_own,
        own,
        returned,
        inner_rows,
        qkv,
        attended,
        probs,
        resid,
        normed_two,
        mixed,
    )
    if fast:
        output, grad_tokens, grad_qkv, grad_out, grad_small, grad_down = backward(
            expert_count, *layer, grad_down
        )
        grad_gate, grad_up, grad_down = grad_gate[None], grad_up[None], grad_down[None]
    else:
        output, grad_tokens, grad_small, *grad_weights = local_backward(expert_count, *layer)
        grad_out, *halves = (scattered(value, both) for value in grad_weights)
        grad_qkv = jnp.stack([half.reshape(share, 3, width // 2) for half in halves], axis=2)
        grad_qkv = grad_qkv.reshape(share, 3 * width)
        grad_small = lax.psum(grad_small, both)
    grad_small = lax.dynamic_slice(grad_small, (0, device * share), (small_rows, share))
    return (
        output,
        grad_tokens,
        grad_qkv,
        grad_out,
        grad_small[:expert_count].T,
        grad_small[expert_count],
        grad_small[expert_count + 1],
        grad_small[expert_count + 2, :bias_share],
        grad_gate,
        grad_up,
        grad_down,
    )


def solution(mesh):
    fast = dict(mesh.shape) == {"dp": 8, "expert": 4}
    rows = P(("dp", "expert"), None)
    flat = P(("dp", "expert"))
    expert = P("expert", "dp", None)
    grid = P("dp", "expert")
    return jax.shard_map(
        functools.partial(on_device, fast),
        mesh=mesh,
        in_specs=(rows,) * 5 + (flat,) * 3 + (expert,) * 3 + (grid, rows, grid),
        out_specs=(rows,) * 5 + (flat,) * 3 + (expert,) * 3,
        check_vma=False,
    )
```

time: 451 us -> 391 us (0.87)
  Pallas kernels: 399 us -> 357 us
  local copies, waits for them, and re-layouts: 31.7 us -> 16.2 us
    pallas_call x6 -> x3, Pallas kernels: 399 us -> 357 us  [call(): pl.pallas_call(kernel, out_shape=out_shape, in_specs=[ANY_SPEC if i in st...]
    unnamed x66 -> x30, local copies, waits for them, and re-layouts: 18.6 us -> 9.91 us
    transpose x4 -> x0, local copies, waits for them, and re-layouts: 4.58 us -> none  [the longest x3 3.65 us: on_device(): jnp.transpose(tiles[:, :, i * CHUNK:(i + 1) * CHUNK], (1, 0, 2))]
  transfers between devices with their start and end apart: 2 -> 2, of which waited for: 1 -> 0; matrix products, arithmetic and copies ran while one was open for 0% -> 0% of each run, Pallas kernels for 26% -> 27%
where the time goes in v3:
time: 391 us; the launch traced here: 390 us
  Pallas kernels  357 us (91%)
  local copies, waits for them, and re-layouts  16.2 us (4%)
  between operations  14.9 us (4%)
    pallas_call x3, Pallas kernels, call(): pl.pallas_call(kernel, out_shape=out_shape, in_specs=[ANY_SPEC if i in st...  357 us
    unnamed x30, local copies, waits for them, and re-layouts  9.91 us
  transfers between devices with their start and end apart: 2, of which 0 were waited for; matrix products, arithmetic and copies ran while one was open for 0% of the time, Pallas kernels for 27%

profile of v3, /device:TPU:0, one launch (start us, length us, event | category | flops | bytes accessed | tf_op | source)
XLA Modules:
  0.0 390.3 jit_solution(4593476151506938149)
XLA Ops:
  7.2 0.0 copy-start.10
  7.2 0.0 copy-start.6
  7.2 0.0 copy-start.8
  7.2 0.0 copy-start.9
  7.2 0.0 copy-start.5
  7.2 0.0 copy-start.7
  7.2 0.0 all-gather.4.cloned.1.call-start
  7.3 0.9 slice.18
  8.2 0.1 reshape_squeeze.8
  8.3 0.9 slice.19
  9.2 0.1 reshape_squeeze.9
  9.3 0.6 pad_maximum_fusion
  9.9 0.9 reshape.39
  10.7 0.0 all-gather.4.cloned.1.call-update
  10.8 0.0 all-gather.6.cloned.1.call-start
  10.8 0.7 all-gather.6.cloned.1.call-update
  12.2 0.1 pad.10.clone
  12.3 0.0 copy-done.10
  12.3 0.1 copy.31
  12.4 0.0 copy-done.6
  12.4 0.1 copy.28
  12.5 0.0 copy-done.8
  12.5 0.1 copy.29
  12.6 0.0 copy-done.9
  12.6 0.1 copy.30
  12.7 0.7 concatenate.10.beside
  13.4 0.0 copy-done.5
  13.4 0.0 copy-done.7
  13.4 0.7 add_add_fusion.meta.refs_7_
  14.1 106.6 %shard_map.248 = (bf16[256,3072]{1,0:T(8,128)(2,1)}, bf16[256,1024]{1,0:T(8,128)(2,1)}, bf16[16,256,256]{2,1,0:T(8,128)(2,1)}, f32[256,1024]{1,0:T(8,128)}, bf16...) custom-call(bf16[256,1024]{1,0:T(8,128)(2,1)} %refs_0_.1, ...), custom_call_target="tpu_custom_call" | custom-call | flops 2415919104 | bytes 2408452 | tf_op jit(solution)/shard_map/pallas_call | solution.py:80
  120.6 0.0 all-gather.4.cloned.1.call-done.early
  120.7 0.0 all-gather.6.cloned.1.call-done
  120.7 143.0 %shard_map.249 = (f32[128,2816]{1,0:T(8,128)}, f32[128,2816]{1,0:T(8,128)}, bf16[2816,1024]{1,0:T(8,128)(2,1)}, bf16[4,256,1024]{2,1,0:T(8,128)(2,1)}, bf16[4,25...) custom-call(bf16[480,1024]{1,0:T(8,128)(2,1)} %get-tuple-element.37.buffer, bf16[480,1024]{1,0:T(8,128)(2,1)} %get-tuple-element.38.scaled, ...), custom_call_target="tpu_custom_call" | custom-call | flops 24914165760 | bytes 13484032 | tf_op jit(solution)/shard_map/pallas_call | solution.py:80
  263.7 107.5 %shard_map.250 = (bf16[256,1024]{1,0:T(8,128)(2,1)}, f32[256,1024]{1,0:T(8,128)}, f32[32,3072]{1,0:T(8,128)}, f32[32,1024]{1,0:T(8,128)}, f32[8,1024]{1,0:T(8,128)}, /*index=5*/f32[352,1024]{1,0:T(8,128)}) custom-call(bf16[256,1024]{1,0:T(8,128)(2,1)} %refs_0_.1, bf16[256,1024]{1,0:T(8,128)(2,1)} %refs_1_.1, bf16[1024,4224]{1,0:T(8,128)(2,1)} %get-tuple-element.35.refs_2_, ...), custom_call_target="tpu_custom_call" | custom-call | flops 4831838208 | bytes 26583048 | tf_op jit(solution)/shard_map/pallas_call | solution.py:80
  371.3 0.0 copy-start.3
  371.3 0.8 constant_dynamic-slice_fusion
  372.1 0.6 slice_bitcast_fusion
  372.7 0.5 slice_bitcast_fusion.2
  373.2 0.5 slice_bitcast_fusion.1
  373.7 2.0 copy.42
  375.7 2.3 copy.43
  378.0 0.0 copy-done.3
  378.0 0.7 copy.44
  378.7 0.7 copy.45
  379.4 1.1 copy.46
  380.5 1.1 copy.47
  381.6 0.8 copy-done.2
  382.4 1.1 copy.48
  (11 shorter events, 0.0 us)
Async XLA Ops:
  7.2 5.1 %copy-start.10 = (bf16[16]{0:T(256)(128)(2,1)S(1)}, bf16[16]{0:T(256)(128)(2,1)}, u32[]{:S(2)}) copy-start(bf16[16]{0:T(256)(128)(2,1)} %param.24) | copy-start | bytes 100
  7.2 5.2 %copy-start.6 = (bf16[32,4]{0,1:T(4,128)(2,1)S(1)}, bf16[32,4]{0,1:T(4,128)(2,1)}, u32[]{:S(2)}) copy-start(bf16[32,4]{0,1:T(4,128)(2,1)} %param.21) | copy-start | bytes 772
  7.2 5.3 %copy-start.8 = (bf16[32]{0:T(256)(128)(2,1)S(1)}, bf16[32]{0:T(256)(128)(2,1)}, u32[]{:S(2)}) copy-start(bf16[32]{0:T(256)(128)(2,1)} %param.22) | copy-start | bytes 196
  7.2 5.4 %copy-start.9 = (bf16[32]{0:T(256)(128)(2,1)S(1)}, bf16[32]{0:T(256)(128)(2,1)}, u32[]{:S(2)}) copy-start(bf16[32]{0:T(256)(128)(2,1)} %param.23) | copy-start | bytes 196
  7.2 6.2 %copy-start.5 = (s32[256,2]{0,1:T(2,128)S(1)}, s32[256,2]{0,1:T(2,128)}, u32[]{:S(2)}) copy-start(s32[256,2]{0,1:T(2,128)} %param.29) | copy-start | bytes 6148
  7.2 6.2 %copy-start.7 = (s32[1,256]{1,0:T(1,128)S(1)}, s32[1,256]{1,0:T(1,128)}, u32[]{:S(2)}) copy-start(s32[1,256]{1,0:T(1,128)} %param.30) | copy-start | bytes 3076
  7.2 113.4 %all-gather.4.cloned.1.call-start = ((), (), s32[]{:S(2)}) async-start(), calls=%async_computation | async-start | bytes 2359296 | tf_op jit(solution)/shard_map/all_gather | solution.py:1796
  10.8 109.9 %all-gather.6.cloned.1.call-start = ((), (), s32[]{:S(2)}) async-start(), calls=%async_computation.1 | async-start | bytes 6488064 | tf_op jit(solution)/shard_map/all_gather | solution.py:1796
  371.3 6.7 %copy-start.3 = (f32[32,3072]{1,0:T(8,128)S(1)}, f32[32,3072]{1,0:T(8,128)}, u32[]{:S(2)}) copy-start(f32[32,3072]{1,0:T(8,128)} %get-tuple-element.74) | copy-start | bytes 1179652
  371.3 7.5 %copy-start.4 = (f32[32,1024]{1,0:T(8,128)S(1)}, f32[32,1024]{1,0:T(8,128)}, u32[]{:S(2)}) copy-start(f32[32,1024]{1,0:T(8,128)} %get-tuple-element.75) | copy-start | bytes 393220
  373.7 5.7 %copy-start.1 = (f32[128,2816]{1,0:T(8,128)S(1)}, f32[128,2816]{1,0:T(8,128)}, u32[]{:S(2)}) copy-start(f32[128,2816]{1,0:T(8,128)} %get-tuple-element.56) | copy-start | bytes 4325380
  378.0 2.5 copy-start
  380.5 1.9 copy-start.2
Sparse Core Ops, SparseCore 0:
  10.9 41.4 all-gather.3
  54.0 58.9 all-gather.5

commit v4 on v3

--- a/solution.py
+++ b/solution.py
@@ -15,6 +15,7 @@
 CAP = 480
 PAIRS = HEADS // 2
 LANES = 2 * HD
+PARTS = 4
 
 epsilon = 1e-06
 masked_value = -1e30
@@ -243,8 +244,6 @@
         def _():
             self.along_z(2).start()
 
-        self.spread_out(0)
-
     def spread_out(self, k):
         self.along_x(k).start()
         self.along_y(k).start()
@@ -599,10 +598,10 @@
         return jnp.sum(jnp.where(self.hot(block), gate, 0.0), axis=1, keepdims=True)
 
 
-def attend_forward(experts, tokens, weights, heads, hot, length, out, between):
+def attend_forward(experts, tokens, weights, out_weight, heads, hot, length, out, between):
     qkv, attended, probs, resid, normed_two, small, normed, diagonals = out
     slots, width = tokens.shape
-    small[...] = jnp.transpose(weights[:, 4 * width :].astype(F32))[: small.shape[0], :]
+    small[...] = jnp.transpose(weights[:, 3 * width :].astype(F32))[: small.shape[0], :]
     x = tokens[...].astype(F32)
     inv_one = lax.rsqrt(jnp.mean(x * x, axis=1, keepdims=True) + epsilon)
     normed[...] = (x * inv_one * small[experts : experts + 1, :]).astype(BF16)
@@ -635,14 +634,14 @@
             outs.append(dot(low, v))
         attended[:, columns(pair, LANES)] = jnp.where(first, outs[0], outs[1]).astype(BF16)
 
-    pl.loop(0, PAIRS // 2)(attend)
-    between()
-    pl.loop(PAIRS // 2, PAIRS)(attend)
+    for part in range(PARTS):
+        pl.loop(part * PAIRS // PARTS, (part + 1) * PAIRS // PARTS)(attend)
+        between(part)
 
     @pl.loop(0, width // 512)
     def _(j):
         resid[:, columns(j, 512)] = tokens[:, columns(j, 512)].astype(F32) + dot(
-            attended[...], weights[:, columns(3 * width // 512 + j, 512)]
+            attended[...], out_weight[:, columns(j, 512)]
         )
 
     r = resid[...]
@@ -654,6 +653,7 @@
     experts,
     tokens,
     weights,
+    out_weight,
     heads,
     hot,
     length,
@@ -666,7 +666,9 @@
     *scratch,
 ):
     out = (qkv, attended, probs, resid, normed_two, small) + scratch
-    attend_forward(experts, tokens, weights, heads, hot, length, out, lambda: None)
+    attend_forward(
+        experts, tokens, weights, out_weight, heads, hot, length, out, lambda part: None
+    )
 
 
 def attention_shapes(experts, tokens):
@@ -681,7 +683,7 @@
     )
 
 
-def attention_forward(experts, tokens, weights, heads, hot, length):
+def attention_forward(experts, tokens, weights, out_weight, heads, hot, length):
     slots, width = tokens.shape
     return call(
         functools.partial(attention_forward_kernel, experts),
@@ -691,6 +693,7 @@
         2 * slots * width * (4 * width + 2 * slots),
         tokens,
         weights,
+        out_weight,
         heads,
         hot,
         length,
@@ -799,10 +802,12 @@
     cots_spread = Spread(cotangent, cots, send.at[1], recv.at[1], d, e)
     work = Dispatch(e, metas, rank, places)
 
+    cut = 3 * width + beside.shape[1]
     mine = gather.item(0, 0)
     own_parts = [
-        pltpu.make_async_copy(part, mine.at[:, start : start + part.shape[1]], local.at[i])
-        for i, (part, start) in enumerate(((qkv_own, 0), (out_own, 3 * width), (beside, 4 * width)))
+        pltpu.make_async_copy(qkv_own, mine.at[:, : 3 * width], local.at[0]),
+        pltpu.make_async_copy(beside, mine.at[:, 3 * width : cut], local.at[1]),
+        pltpu.make_async_copy(out_own, mine.at[:, cut:], local.at[2]),
     ]
     own_cots = pltpu.make_async_copy(cotangent, cots.at[0], local.at[3])
     for copy in own_parts:
@@ -814,15 +819,16 @@
     for copy in own_parts:
         copy.wait()
     gather.start()
+    gather.spread_out(0)
     own_cots.start()
     metas[0] = meta[...]
     for copy in meta_copies:
         copy.wait_recv()
     work.find_places()
-    for k in (1, 3, 2):
-        gather.from_z(k)
-        if k == 3:
-            gather.from_neighbours(0)
+    gather.from_z(1)
+    gather.from_neighbours(0)
+    gather.from_z(3)
+    gather.from_z(2)
     for k in (1, 3, 2):
         gather.from_neighbours(k)
     cots_spread.start()
@@ -832,8 +838,13 @@
     keep = pltpu.make_async_copy(weights, kept, local.at[4])
     keep.start()
 
+    def between(part):
+        if part == 1:
+            cots_spread.forward()
+
     out = (qkv, attended, probs, resid, normed_two, small, normed, diagonals)
-    attend_forward(experts, tokens, weights, heads, hot, length, out, cots_spread.forward)
+    projections, out_weight = weights.at[:, :cut], weights.at[:, cut:]
+    attend_forward(experts, tokens, projections, out_weight, heads, hot, length, out, between)
 
     rows_spread.start()
     own_cots.wait()
@@ -1313,12 +1324,9 @@
     )
 
 
-PARTS = 4
-
-
 def backward_layer(experts, relative, ins, outs, work, reached):
-    tokens, cotangent, weights, small, heads, hot_back, length, meta, own = ins[:9]
-    returned, inner_rows, qkv, attended, probs, resid, normed_two = ins[9:]
+    tokens, cotangent, weights, out_weight, small, heads, hot_back, length, meta, own = ins[:10]
+    returned, inner_rows, qkv, attended, probs, resid, normed_two = ins[10:]
     grad_tokens, grad_small, grad_out, *grad_halves = outs
     grad_attended, grad_qkv, branch, normed, grad_resid, grad_diagonals = work
     slots, width = tokens.shape
@@ -1367,7 +1375,7 @@
         )
 
     reached("out")
-    grad_attended[...] = dot_nt(branch[...], weights[:, 3 * width : 4 * width]).astype(BF16)
+    grad_attended[...] = dot_nt(branch[...], out_weight[...]).astype(BF16)
     x = tokens[...].astype(F32)
     inv_one = lax.rsqrt(jnp.mean(x * x, axis=1, keepdims=True) + epsilon)
     normed[...] = (x * inv_one * small[experts : experts + 1, :]).astype(BF16)
@@ -1459,13 +1467,13 @@
 
 
 def local_backward_kernel(experts, *refs):
-    ins, mixed, output, outs, work = refs[:16], refs[16], refs[17], refs[18:23], refs[23:]
+    ins, mixed, output, outs, work = refs[:17], refs[17], refs[18], refs[19:24], refs[24:]
     backward_layer(experts, False, ins, outs, work, lambda name: None)
-    add_mixed(output, ins[14], ins[6], [mixed.at[block] for block in range(mixed.shape[0])])
+    add_mixed(output, ins[15], ins[7], [mixed.at[block] for block in range(mixed.shape[0])])
 
 
 def local_backward(experts, *args):
-    tokens, small = args[0], args[3]
+    tokens, small = args[0], args[4]
     slots, width = tokens.shape
     return call(
         functools.partial(local_backward_kernel, experts),
@@ -1636,12 +1644,19 @@
         taken, refs[:] = refs[:count], refs[count:]
         return taken
 
-    ins = take(16)
+    ins = take(17)
     mixed, grad_down = take(2)
     output, grad_tokens, qkv_sum, out_sum, small_sum, down_sum = take(6)
     grad_small, grad_out, *grad_halves = take(4)
     work = take(6)
-    (half_sums,) = take(1)
+    half_sums, *brought, fetched = take(6)
+    cut = brought[0].shape[1]
+    ins[2], ins[3] = ins[2].at[:, :cut], ins[3].at[:, cut:]
+    fetches = []
+    for i, (at, ref) in enumerate(zip(FETCHED, brought)):
+        fetches.append(pltpu.make_async_copy(ins[at], ref, fetched.at[i]))
+        fetches[-1].start()
+        ins[at] = ref
     mixed_full, mixed_send, mixed_recv = take(3)
     d, e, z, _ = here()
     width = out_sum.shape[1]
@@ -1651,6 +1666,8 @@
     every = EverySum(take(4))
     swap = Swap(mixed, mixed_full, mixed_send, mixed_recv, d, e)
     meet(group(d, e)[1:] + [down.other] + down.to[1:])
+    for block in (3, 1, 2):
+        swap.start(block)
     for i in range(down.count):
         down.begin(i)
     down.halve(0)
@@ -1660,6 +1677,8 @@
             down.halve(1)
         elif name == "out":
             out.begin()
+            for copy in fetches:
+                copy.wait()
         elif name == "attended":
             down.halve(2)
         elif name == "part0":
@@ -1684,8 +1703,6 @@
         elif name == "tokens":
             every.start(grad_small[...])
             halves[1].stage_one()
-            for block in (3, 1, 2):
-                swap.start(block)
 
     outs = [grad_tokens, grad_small, grad_out] + grad_halves
     backward_layer(experts, True, ins, outs, work, reached)
@@ -1710,7 +1727,7 @@
         down.finish(i, down_sum.at[:, i * CHUNK : (i + 1) * CHUNK])
     halves[1].line.pass_on(0)
     swap.finish()
-    add_mixed(output, ins[14], ins[6], [mixed.at[0]] + [mixed_full.at[q] for q in (1, 2, 3)])
+    add_mixed(output, ins[15], ins[7], [mixed.at[0]] + [mixed_full.at[q] for q in (1, 2, 3)])
     out.line.finish(0, out_sum)
     wide = width // 2
     for half, sums in enumerate(halves):
@@ -1723,8 +1740,11 @@
     every.settle()
 
 
+FETCHED = (2, 3, 12, 14)
+
+
 def backward(experts, *args):
-    tokens, small, mixed, grad_down = args[0], args[3], args[16], args[17]
+    tokens, small, mixed, grad_down = args[0], args[4], args[17], args[18]
     slots, width = tokens.shape
     share, down_share = width // 32, grad_down.shape[0] // 8
     half = 3 * width // 2
@@ -1735,6 +1755,10 @@
         pltpu.VMEM((width, half), BF16),
         *backward_scratch(slots, width),
         pltpu.VMEM((2, share, half), F32),
+        pltpu.VMEM((width, args[2].shape[1] - width), BF16),
+        pltpu.VMEM((width, width), BF16),
+        *[pltpu.VMEM(args[i].shape, BF16) for i in FETCHED[2:]],
+        DMA((len(FETCHED),)),
         pltpu.VMEM(mixed.shape, BF16),
         DMA((4,)),
         DMA((4,)),
@@ -1758,12 +1782,40 @@
         63 * MB,
         4 * slots * width * (4 * width + 2 * slots),
         *args,
-        stay=(17,),
+        stay=(18,) + FETCHED,
         link=3,
     )
 
 
-READY = 2
+def publish_kernel(*refs):
+    count = (len(refs) - 2) // 3
+    ins, outs, held = refs[:count], refs[count : 2 * count], refs[2 * count : 3 * count]
+    loads = [pltpu.make_async_copy(ins[i], held[i], refs[-2].at[i]) for i in range(count)]
+    stores = [pltpu.make_async_copy(held[i], outs[i], refs[-1].at[i]) for i in range(count)]
+    for copy in loads:
+        copy.start()
+    for load, store in zip(loads, stores):
+        load.wait()
+        store.start()
+    for copy in stores:
+        copy.wait()
+
+
+def publish(*values):
+    count = len(values)
+    return call(
+        publish_kernel,
+        tuple(jax.ShapeDtypeStruct(value.shape, value.dtype) for value in values),
+        [pltpu.VMEM(value.shape, value.dtype) for value in values] + [DMA((count,)), DMA((count,))],
+        60 * MB,
+        0,
+        *values,
+        stay=tuple(range(count)),
+        land=tuple(range(count)),
+    )
+
+
+READY = 3
 
 
 def on_device(
@@ -1860,9 +1912,13 @@
             out_weight,
             beside,
         )
+        out_full = weights
     else:
-        weights = gathered(jnp.concatenate([qkv_weight, out_weight, beside], axis=1), both)
-        kept = attention_forward(expert_count, tokens, weights, heads, diagonals_hot, lengths)
+        weights = gathered(jnp.concatenate([qkv_weight, beside], axis=1), both)
+        out_full = gathered(out_weight, both)
+        kept = attention_forward(
+            expert_count, tokens, weights, out_full, heads, diagonals_hot, lengths
+        )
         rows, cots, meta = (
             gathered(value, "expert", tiled=False) for value in (kept[4], cotangent, meta_own)
         )
@@ -1894,6 +1950,7 @@
         tokens,
         cotangent,
         weights,
+        out_full,
         small,
         heads,
         hot(ahead - (slots - 1)),
@@ -1912,6 +1969,9 @@
     if fast:
         output, grad_tokens, grad_qkv, grad_out, grad_small, grad_down = backward(
             expert_count, *layer, grad_down
+        )
+        output, grad_tokens, grad_qkv, grad_out, grad_gate, grad_up, grad_down = publish(
+            output, grad_tokens, grad_qkv, grad_out, grad_gate, grad_up, grad_down
         )
         grad_gate, grad_up, grad_down = grad_gate[None], grad_up[None], grad_down[None]
     else:

time: 391 us -> 365 us (0.934)
  Pallas kernels: 357 us -> 341 us
  local copies, waits for them, and re-layouts: 16.2 us -> 7.45 us
    pallas_call x3 -> x4, Pallas kernels: 357 us -> 341 us  [call(): pl.pallas_call(kernel, out_shape=out_shape, in_specs=[ANY_SPEC if i in st...]
    unnamed x30 -> x15, local copies, waits for them, and re-layouts: 9.91 us -> 0.46 us
  transfers between devices with their start and end apart: 2 -> 2, of which waited for: 0 -> 0; matrix products, arithmetic and copies ran while one was open for 0% -> 1% of each run, Pallas kernels for 27% -> 31%
where the time goes in v4:
time: 365 us
  Pallas kernels  341 us (93%)
  between operations  14.9 us (4%)
  local copies, waits for them, and re-layouts  7.45 us (2%)
    pallas_call x4, Pallas kernels, call(): pl.pallas_call(kernel, out_shape=out_shape, in_specs=[ANY_SPEC if i in st...  341 us
  transfers between devices with their start and end apart: 2, of which 0 were waited for; matrix products, arithmetic and copies ran while one was open for 1% of the time, Pallas kernels for 31%

profile of v4, /device:TPU:0, one launch (start us, length us, event | category | flops | bytes accessed | tf_op | source)
XLA Modules:
  0.0 364.6 jit_solution(3255091930192985461)
XLA Ops:
  7.2 0.0 all-gather.4.cloned.1.call-start
  7.2 0.9 slice.18
  8.2 0.2 copy.41
  8.3 0.0 copy-start.5
  8.3 0.0 copy-start.1
  8.4 0.0 copy-start.3
  8.4 0.0 copy-start.4
  8.4 1.0 slice.19
  9.3 0.0 copy-start
  9.4 0.0 copy-start.2
  9.4 0.2 copy.42
  9.6 0.6 copy.40
  10.2 1.0 reshape.39
  11.2 0.0 all-gather.4.cloned.1.call-update
  11.2 0.0 all-gather.6.cloned.1.call-start
  11.3 0.7 all-gather.6.cloned.1.call-update
  12.7 0.1 pad.10.clone
  12.7 0.0 copy-done.5
  12.7 0.1 copy.37
  12.8 0.0 copy-done.1
  12.8 0.1 copy.34
  13.0 0.0 copy-done.3
  13.0 0.1 copy.35
  13.1 0.0 copy-done.4
  13.1 0.1 copy.36
  13.2 0.7 concatenate.10.beside
  13.9 0.0 copy-done
  13.9 0.0 copy-done.2
  13.9 0.7 add_add_fusion.meta.refs_8_
  14.5 114.6 %shard_map.248 = (bf16[256,3072]{1,0:T(8,128)(2,1)}, bf16[256,1024]{1,0:T(8,128)(2,1)}, bf16[16,256,256]{2,1,0:T(8,128)(2,1)}, f32[256,1024]{1,0:T(8,128)}, bf16...) custom-call(bf16[256,1024]{1,0:T(8,128)(2,1)} %refs_0_.1, ...), custom_call_target="tpu_custom_call" | custom-call | flops 2415919104 | bytes 2408452 | tf_op jit(solution)/shard_map/pallas_call | solution.py:81
  129.1 0.0 all-gather.4.cloned.1.call-done.early
  129.2 0.0 all-gather.6.cloned.1.call-done
  129.2 132.8 %shard_map.249 = (f32[128,2816]{1,0:T(8,128)}, f32[128,2816]{1,0:T(8,128)}, bf16[2816,1024]{1,0:T(8,128)(2,1)}, bf16[4,256,1024]{2,1,0:T(8,128)(2,1)}, bf16[4,25...) custom-call(bf16[480,1024]{1,0:T(8,128)(2,1)} %get-tuple-element.44.buffer, bf16[480,1024]{1,0:T(8,128)(2,1)} %get-tuple-element.45.scaled, ...), custom_call_target="tpu_custom_call" | custom-call | flops 24914165760 | bytes 14532608 | tf_op jit(solution)/shard_map/pallas_call | solution.py:81
  261.9 88.0 %shard_map.250 = (bf16[256,1024]{1,0:T(8,128)(2,1)}, f32[256,1024]{1,0:T(8,128)}, f32[32,3072]{1,0:T(8,128)}, f32[32,1024]{1,0:T(8,128)}, f32[8,1024]{1,0:T(8,128)}, /*index=5*/f32[352,1024]{1,0:T(8,128)}) custom-call(bf16[256,1024]{1,0:T(8,128)(2,1)} %refs_0_.1, bf16[256,1024]{1,0:T(8,128)(2,1)} %refs_1_.1, ...), custom_call_target="tpu_custom_call" | custom-call | flops 4831838208 | bytes 35233800 | tf_op jit(solution)/shard_map/pallas_call | solution.py:81
  350.0 0.8 constant_dynamic-slice_fusion
  350.7 0.6 slice_bitcast_fusion
  351.3 0.5 slice_bitcast_fusion.2
  351.8 0.5 slice_bitcast_fusion.1
  352.3 5.4 %shard_map.251 = (bf16[256,1024]{1,0:T(8,128)(2,1)}, f32[256,1024]{1,0:T(8,128)}, f32[32,3072]{1,0:T(8,128)}, f32[32,1024]{1,0:T(8,128)}, f32[128,2816]{1,0:T(8,...) custom-call(bf16[256,1024]{1,0:T(8,128)(2,1)} %get-tuple-element.58.refs_0_, f32[256,1024]{1,0:T(8,128)} %get-tuple-element.59.refs_1_, ...), custom_call_target="tpu_custom_call" | custom-call | bytes 6422528 | tf_op jit(solution)/shard_map/pallas_call | solution.py:81
  (5 shorter events, 0.1 us)
Async XLA Ops:
  7.2 122.0 %all-gather.4.cloned.1.call-start = ((), (), s32[]{:S(2)}) async-start(), calls=%async_computation | async-start | bytes 3538944 | tf_op jit(solution)/shard_map/all_gather | solution.py:1848
  8.3 4.4 %copy-start.5 = (bf16[16]{0:T(256)(128)(2,1)S(1)}, bf16[16]{0:T(256)(128)(2,1)}, u32[]{:S(2)}) copy-start(bf16[16]{0:T(256)(128)(2,1)} %param.24) | copy-start | bytes 100
  8.3 4.5 %copy-start.1 = (bf16[32,4]{0,1:T(4,128)(2,1)S(1)}, bf16[32,4]{0,1:T(4,128)(2,1)}, u32[]{:S(2)}) copy-start(bf16[32,4]{0,1:T(4,128)(2,1)} %param.21) | copy-start | bytes 772
  8.4 4.6 %copy-start.3 = (bf16[32]{0:T(256)(128)(2,1)S(1)}, bf16[32]{0:T(256)(128)(2,1)}, u32[]{:S(2)}) copy-start(bf16[32]{0:T(256)(128)(2,1)} %param.22) | copy-start | bytes 196
  8.4 4.7 %copy-start.4 = (bf16[32]{0:T(256)(128)(2,1)S(1)}, bf16[32]{0:T(256)(128)(2,1)}, u32[]{:S(2)}) copy-start(bf16[32]{0:T(256)(128)(2,1)} %param.23) | copy-start | bytes 196
  9.3 4.5 %copy-start = (s32[256,2]{0,1:T(2,128)S(1)}, s32[256,2]{0,1:T(2,128)}, u32[]{:S(2)}) copy-start(s32[256,2]{0,1:T(2,128)} %param.29) | copy-start | bytes 6148
  9.4 4.5 %copy-start.2 = (s32[1,256]{1,0:T(1,128)S(1)}, s32[1,256]{1,0:T(1,128)}, u32[]{:S(2)}) copy-start(s32[1,256]{1,0:T(1,128)} %param.30) | copy-start | bytes 3076
  11.2 117.9 %all-gather.6.cloned.1.call-start = ((), (), s32[]{:S(2)}) async-start(), calls=%async_computation.1 | async-start | bytes 6488064 | tf_op jit(solution)/shard_map/all_gather | solution.py:1848
Sparse Core Ops, SparseCore 0:
  11.4 51.5 all-gather.3
  64.6 59.1 all-gather.5

commit v5 on v4

--- a/solution.py
+++ b/solution.py
@@ -16,6 +16,8 @@
 PAIRS = HEADS // 2
 LANES = 2 * HD
 PARTS = 4
+CHUNK = 256
+TILE = 2 * CHUNK
 
 epsilon = 1e-06
 masked_value = -1e30
@@ -446,9 +448,9 @@
         )
 
     def parts(self, j):
-        piece = self.place(j, self.d)
-        width = piece.shape[1] // 2
-        for i, half in enumerate(self.halves(j)):
+        piece, halves = self.place(j, self.d), self.halves(j)
+        width = piece.shape[1] // len(halves)
+        for i, half in enumerate(halves):
             yield half, piece.at[:, i * width : (i + 1) * width]
 
     def keep(self, j):
@@ -762,10 +764,17 @@
     hot,
     length,
     cotangent,
-    meta,
+    routes,
+    priority,
+    router,
+    first_gain,
+    second_gain,
+    bias,
     qkv_own,
     out_own,
-    beside,
+    gate_own,
+    up_own,
+    down_own,
     qkv,
     attended,
     probs,
@@ -777,7 +786,12 @@
     plain,
     select,
     gate_column,
+    meta,
     kept,
+    early_kept,
+    down_kept,
+    early,
+    down,
     acc,
     acc_cot,
     rank,
@@ -793,6 +807,9 @@
     recv,
     gather_send,
     gather_recv,
+    piece_stored,
+    own_small,
+    *scratch,
 ):
     d, e, z, c = here()
     slots, width = tokens.shape
@@ -801,17 +818,70 @@
     rows_spread = Spread(normed_two, rows, send.at[0], recv.at[0], d, e)
     cots_spread = Spread(cotangent, cots, send.at[1], recv.at[1], d, e)
     work = Dispatch(e, metas, rank, places)
-
-    cut = 3 * width + beside.shape[1]
+    tile_share, down_share = gate_own.shape[0], down_own.shape[0]
+    tile_spread = LineSpread(
+        lambda j: [own.at[:, j * CHUNK : (j + 1) * CHUNK] for own in (gate_own, up_own)],
+        lambda j, device: early.at[
+            j, pl.ds(pl.multiple_of(device * tile_share, tile_share), tile_share)
+        ],
+        scratch[:3],
+    )
+    down_spread = LineSpread(
+        lambda j: [down_own.at[:, j * CHUNK : (j + 1) * CHUNK]],
+        lambda j, device: down.at[
+            pl.ds(pl.multiple_of(device * down_share, down_share), down_share),
+            j * CHUNK : (j + 1) * CHUNK,
+        ],
+        scratch[3:],
+    )
+    pieces = [(tile_spread, j) for j in range(early.shape[0])]
+    pieces += [(down_spread, j) for j in range(width // CHUNK)]
+
+    def near(i):
+        if 0 <= i < len(pieces):
+            pieces[i][0].relay_near(pieces[i][1])
+
+    def far(i):
+        if 0 <= i < len(pieces):
+            pieces[i][0].relay_far(pieces[i][1])
+        begin(i + AHEAD)
+
+    def begin(i):
+        if i < len(pieces):
+            pieces[i][0].start(pieces[i][1])
+
+    def store(i):
+        spread, j = pieces[i]
+        if spread is tile_spread:
+            src, dst = early.at[j], early_kept.at[j]
+        else:
+            at = slice(j * CHUNK, (j + 1) * CHUNK)
+            src, dst = down.at[:, at], down_kept.at[:, at]
+        return pltpu.make_async_copy(src, dst, piece_stored.at[i])
+
+    cut = weights.shape[1] - width
     mine = gather.item(0, 0)
     own_parts = [
         pltpu.make_async_copy(qkv_own, mine.at[:, : 3 * width], local.at[0]),
-        pltpu.make_async_copy(beside, mine.at[:, 3 * width : cut], local.at[1]),
-        pltpu.make_async_copy(out_own, mine.at[:, cut:], local.at[2]),
+        pltpu.make_async_copy(out_own, mine.at[:, cut:], local.at[1]),
     ]
     own_cots = pltpu.make_async_copy(cotangent, cots.at[0], local.at[3])
     for copy in own_parts:
         copy.start()
+    meta[0:2, :] = routes[...]
+    meta[2:3, :] = priority[...]
+    slot = lax.broadcasted_iota(jnp.int32, (1, slots), 1)
+    meta[3:4, :] = (slot < length[0, 0]).astype(jnp.int32)
+    meta[4:8, :] = jnp.zeros((4, slots), jnp.int32)
+    own_small[...] = jnp.zeros_like(own_small)
+    row = 0
+    for part in (router, first_gain, second_gain, bias):
+        own_small[row : row + part.shape[0], : part.shape[1]] = part[...].astype(F32)
+        row += part.shape[0]
+    mine[:, 3 * width : cut] = jnp.zeros((share, cut - 3 * width), BF16)
+    mine[:, 3 * width : 3 * width + own_small.shape[0]] = jnp.transpose(own_small[...])[
+        :share, :
+    ].astype(BF16)
     meet(group(d, e)[1:] + [gather.other] + gather.to_z[1:])
     meta_copies = [
         push(meta, metas.at[q], send.at[2, q], recv.at[2, q], group(d, e)[q]) for q in (1, 2, 3)
@@ -829,18 +899,34 @@
     gather.from_neighbours(0)
     gather.from_z(3)
     gather.from_z(2)
-    for k in (1, 3, 2):
-        gather.from_neighbours(k)
+    for i in range(AHEAD):
+        begin(i)
+    gather.from_neighbours(1)
+    near(0)
+    gather.from_neighbours(3)
+    near(1)
+    far(0)
+    gather.from_neighbours(2)
     cots_spread.start()
+    far(1)
     for k in (0, 1, 3, 2):
         gather.from_across(k)
+    near(2)
     gather.complete()
+    far(2)
     keep = pltpu.make_async_copy(weights, kept, local.at[4])
     keep.start()
 
     def between(part):
-        if part == 1:
+        if part == 0:
+            near(3)
+        elif part == 1:
             cots_spread.forward()
+            far(3)
+        elif part == 2:
+            near(4)
+        else:
+            far(4)
 
     out = (qkv, attended, probs, resid, normed_two, small, normed, diagonals)
     projections, out_weight = weights.at[:, :cut], weights.at[:, cut:]
@@ -874,9 +960,12 @@
     take_cots(1)
     rows_spread.forward()
     take_cots(2)
+    near(5)
     take_cots(3)
     plain[...] = acc_cot[...].astype(BF16)
     take_rows(0, normed_two)
+    far(5)
+    near(6)
     rows_spread.arrived(1)
     take_rows(1, rows.at[1])
     rows_spread.arrived(2)
@@ -885,22 +974,37 @@
     take_rows(3, rows.at[3])
     buffer[...] = acc[...].astype(BF16)
     scaled[...] = (acc_cot[...] * gate_column[:, 0:1]).astype(BF16)
+    far(6)
+    for i, (spread, j) in enumerate(pieces):
+        spread.complete(j)
+        store(i).start()
     rows_spread.sent()
     gather.settle()
+    for i, (spread, j) in enumerate(pieces):
+        spread.settle(j)
+        store(i).wait()
     for copy in meta_copies:
         copy.wait_send()
     keep.wait()
 
 
-def forward(experts, tokens, heads, hot, length, cotangent, meta, qkv_own, out_own, beside):
+AHEAD = 3
+
+
+def forward(ready, experts, *args):
+    tokens, cotangent, qkv_own, gate_own, down_own = args[0], args[4], args[11], args[13], args[15]
     slots, width = tokens.shape
-    full = (32 * qkv_own.shape[0], 4 * width + beside.shape[1])
+    full = (32 * qkv_own.shape[0], 4 * width + 128)
+    meta = jax.ShapeDtypeStruct((8, slots), jnp.int32)
     block = (experts, slots, width)
-    scratch = dispatch_scratch(*block) + [
+    tiles, down_full = (ready, width, TILE), (8 * down_own.shape[0], width)
+    pieces = ready + width // CHUNK
+    scratch = [pltpu.VMEM(tiles, BF16), pltpu.VMEM(down_full, BF16)]
+    scratch += dispatch_scratch(*block) + [
         pltpu.VMEM(full, BF16),
         pltpu.VMEM(block, BF16),
         pltpu.VMEM(block, BF16),
-        pltpu.VMEM((experts,) + meta.shape, jnp.int32),
+        pltpu.VMEM((experts,) + meta.shape, meta.dtype),
         pltpu.VMEM((slots, width), BF16),
         pltpu.VMEM((HEADS, 2 * slots), F32),
         DMA((5,)),
@@ -908,30 +1012,26 @@
         DMA((3, 6)),
         DMA((5, 16)),
         DMA((5, 16)),
+        DMA((pieces,)),
+        pltpu.VMEM((8, 128), F32),
+        *LineSpread.scratch(ready),
+        *LineSpread.scratch(width // CHUNK),
     ]
-    shapes = attention_shapes(experts, tokens) + dispatch_shapes(*block)
+    shapes = attention_shapes(experts, tokens) + dispatch_shapes(*block) + (meta,)
     return call(
         functools.partial(forward_kernel, experts),
-        shapes + (jax.ShapeDtypeStruct(full, BF16),),
+        shapes
+        + tuple(jax.ShapeDtypeStruct(shape, BF16) for shape in (full, tiles, down_full)),
         scratch,
-        60 * MB,
+        62 * MB,
         2 * slots * width * (4 * width + 2 * slots),
-        tokens,
-        heads,
-        hot,
-        length,
-        cotangent,
-        meta,
-        qkv_own,
-        out_own,
-        beside,
-        stay=(4, 6, 7, 8),
-        land=(len(shapes),),
+        *args,
+        stay=(4, 11, 12, 13, 14, 15),
+        land=tuple(len(shapes) + i for i in range(3)),
         link=0,
     )
 
 
-CHUNK = 256
 GELU_A = math.sqrt(2.0 / math.pi)
 GELU_B = 0.044715
 
@@ -1060,9 +1160,6 @@
         inner,
         gate_column,
     )
-
-
-TILE = 2 * CHUNK
 
 
 def sweep_kernel(
@@ -1102,9 +1199,6 @@
     coming = tiles - ready
     d, e, z, c = here()
 
-    def columns_of(tile):
-        return pl.ds(pl.multiple_of(tile * TILE, TILE), TILE)
-
     def rows_of(device):
         return pl.ds(pl.multiple_of(device * share, share), share)
 
@@ -1124,7 +1218,7 @@
     meet(group(d, e)[1:] + [line.other] + line.to[1:])
 
     def early_load(t):
-        return pltpu.make_async_copy(early.at[:, columns_of(t)], both.at[t], loaded.at[t])
+        return pltpu.make_async_copy(early.at[t], both.at[t], loaded.at[t])
 
     down_load = pltpu.make_async_copy(down_full, down, loaded.at[tiles])
     for t in range(ready):
@@ -1787,13 +1881,22 @@
     )
 
 
-def publish_kernel(*refs):
-    count = (len(refs) - 2) // 3
-    ins, outs, held = refs[:count], refs[count : 2 * count], refs[2 * count : 3 * count]
+def publish_kernel(experts, small, *refs):
+    count = (len(refs) - 6) // 3
+    ins, refs = refs[:count], refs[count:]
+    router, first, second, bias, *refs = refs
+    outs, held = refs[:count], refs[count : 2 * count]
     loads = [pltpu.make_async_copy(ins[i], held[i], refs[-2].at[i]) for i in range(count)]
     stores = [pltpu.make_async_copy(held[i], outs[i], refs[-1].at[i]) for i in range(count)]
     for copy in loads:
         copy.start()
+    width, share = small.shape[1], first.shape[1]
+    device = lax.axis_index("dp") * experts + lax.axis_index("expert")
+    turned = pltpu.roll(small[...], lax.rem(width - device * share, width), 1)
+    router[...] = turned[:experts, :share]
+    first[...] = turned[experts : experts + 1, :share]
+    second[...] = turned[experts + 1 : experts + 2, :share]
+    bias[...] = turned[experts + 2 : experts + 3, : bias.shape[1]]
     for load, store in zip(loads, stores):
         load.wait()
         store.start()
@@ -1801,21 +1904,27 @@
         copy.wait()
 
 
-def publish(*values):
+def publish(experts, small, bias_share, *values):
     count = len(values)
+    share = small.shape[1] // 32
     return call(
-        publish_kernel,
-        tuple(jax.ShapeDtypeStruct(value.shape, value.dtype) for value in values),
+        functools.partial(publish_kernel, experts),
+        tuple(
+            jax.ShapeDtypeStruct(shape, F32)
+            for shape in ((experts, share), (1, share), (1, share), (1, bias_share))
+        )
+        + tuple(jax.ShapeDtypeStruct(value.shape, value.dtype) for value in values),
         [pltpu.VMEM(value.shape, value.dtype) for value in values] + [DMA((count,)), DMA((count,))],
         60 * MB,
         0,
+        small,
         *values,
-        stay=tuple(range(count)),
-        land=tuple(range(count)),
-    )
-
-
-READY = 3
+        stay=tuple(range(1, count + 1)),
+        land=tuple(range(4, count + 4)),
+    )
+
+
+READY = 2
 
 
 def on_device(
@@ -1854,27 +1963,11 @@
         return lax.all_to_all(value, "expert", split_axis=0, concat_axis=0, tiled=True)
 
     rows_own, hidden = gate_weight.shape[1:]
-    down_full = gathered(down_weight[0], "dp")
-    if fast:
-        cut = (rows_own, READY, 1, CHUNK)
-        early = jnp.concatenate(
-            [value[0, :, : READY * CHUNK].reshape(cut) for value in (gate_weight, up_weight)],
-            axis=2,
-        ).reshape(rows_own, READY * TILE)
-        early = gathered(early, "dp")
-    else:
-        gate_full, up_full = (gathered(value[0], "dp") for value in (gate_weight, up_weight))
-
-    beside = jnp.concatenate(
-        [
-            router_weight,
-            first_gain[:, None],
-            second_gain[:, None],
-            jnp.pad(bias_table, (0, share - bias_share))[:, None],
-            jnp.zeros((share, 128 - expert_count - 3), BF16),
-        ],
-        axis=1,
-    )
+    if not fast:
+        gate_full, up_full, down_full = (
+            gathered(value[0], "dp") for value in (gate_weight, up_weight, down_weight)
+        )
+
     lane = np.arange(width)
     flat = lane // share * bias_share + lane % share
     in_table = lane % share < bias_share
@@ -1887,33 +1980,50 @@
             np.where(in_table[:, None], diagonal_onehot(ahead)[flat % BUCKETS], 0.0), BF16
         )
 
-    valid_rows = jnp.arange(slots, dtype=jnp.int32) < lengths[0, 0]
-    meta_own = jnp.concatenate(
-        [
-            routes.T,
-            priority,
-            valid_rows.astype(jnp.int32)[None, :],
-            jnp.zeros((4, slots), jnp.int32),
-        ],
-        axis=0,
-    )
-
     diagonals_hot = hot(np.where(ahead < slots, ahead, ahead - 2 * slots))
     if fast:
-        *kept, buffer, scaled, plain, select, gate_column, weights = forward(
+        *kept, buffer, scaled, plain, select, gate_column, meta_own, weights, early, down_full = forward(
+            READY,
             expert_count,
             tokens,
             heads,
             diagonals_hot,
             lengths,
             cotangent,
-            meta_own,
+            routes.T,
+            priority,
+            router_weight.T,
+            first_gain[None],
+            second_gain[None],
+            bias_table[None],
             qkv_weight,
             out_weight,
-            beside,
+            gate_weight[0],
+            up_weight[0],
+            down_weight[0],
         )
         out_full = weights
     else:
+        beside = jnp.concatenate(
+            [
+                router_weight,
+                first_gain[:, None],
+                second_gain[:, None],
+                jnp.pad(bias_table, (0, share - bias_share))[:, None],
+                jnp.zeros((share, 128 - expert_count - 3), BF16),
+            ],
+            axis=1,
+        )
+        valid_rows = jnp.arange(slots, dtype=jnp.int32) < lengths[0, 0]
+        meta_own = jnp.concatenate(
+            [
+                routes.T,
+                priority,
+                valid_rows.astype(jnp.int32)[None, :],
+                jnp.zeros((4, slots), jnp.int32),
+            ],
+            axis=0,
+        )
         weights = gathered(jnp.concatenate([qkv_weight, beside], axis=1), both)
         out_full = gathered(out_weight, both)
         kept = attention_forward(
@@ -1970,9 +2080,19 @@
         output, grad_tokens, grad_qkv, grad_out, grad_small, grad_down = backward(
             expert_count, *layer, grad_down
         )
-        output, grad_tokens, grad_qkv, grad_out, grad_gate, grad_up, grad_down = publish(
-            output, grad_tokens, grad_qkv, grad_out, grad_gate, grad_up, grad_down
-        )
+        grad_router, grad_first, grad_second, grad_bias, *large = publish(
+            expert_count,
+            grad_small,
+            bias_share,
+            output,
+            grad_tokens,
+            grad_qkv,
+            grad_out,
+            grad_gate,
+            grad_up,
+            grad_down,
+        )
+        output, grad_tokens, grad_qkv, grad_out, grad_gate, grad_up, grad_down = large
         grad_gate, grad_up, grad_down = grad_gate[None], grad_up[None], grad_down[None]
     else:
         output, grad_tokens, grad_small, *grad_weights = local_backward(expert_count, *layer)
@@ -1980,16 +2100,22 @@
         grad_qkv = jnp.stack([half.reshape(share, 3, width // 2) for half in halves], axis=2)
         grad_qkv = grad_qkv.reshape(share, 3 * width)
         grad_small = lax.psum(grad_small, both)
-    grad_small = lax.dynamic_slice(grad_small, (0, device * share), (small_rows, share))
+        grad_small = lax.dynamic_slice(grad_small, (0, device * share), (small_rows, share))
+        grad_router, grad_first, grad_second, grad_bias = (
+            grad_small[:expert_count],
+            grad_small[expert_count : expert_count + 1],
+            grad_small[expert_count + 1 : expert_count + 2],
+            grad_small[expert_count + 2 : expert_count + 3, :bias_share],
+        )
     return (
         output,
         grad_tokens,
         grad_qkv,
         grad_out,
-        grad_small[:expert_count].T,
-        grad_small[expert_count],
-        grad_small[expert_count + 1],
-        grad_small[expert_count + 2, :bias_share],
+        grad_router.T,
+        grad_first[0],
+        grad_second[0],
+        grad_bias[0],
         grad_gate,
         grad_up,
         grad_down,

time: 365 us -> 346 us (0.948)
  between operations: 14.9 us -> 1.5 us
  local copies, waits for them, and re-layouts: 7.45 us -> 0 us
  transfers between devices with their start and end apart: 2 -> 0, of which waited for: 0 -> 0; matrix products, arithmetic and copies ran while one was open for 1% -> 0% of each run, Pallas kernels for 31% -> 0%
where the time goes in v5:
time: 346 us; the launch traced here: 345 us
  Pallas kernels  344 us (99%)
    pallas_call x4, Pallas kernels, call(): pl.pallas_call(kernel, out_shape=out_shape, in_specs=[ANY_SPEC if i in st...  344 us

profile of v5, /device:TPU:0, one launch (start us, length us, event | category | flops | bytes accessed | tf_op | source)
XLA Modules:
  0.0 345.4 jit_solution(8175352671962846576)
XLA Ops:
  1.3 111.2 %shard_map.248 = (bf16[256,3072]{1,0:T(8,128)(2,1)}, bf16[256,1024]{1,0:T(8,128)(2,1)}, bf16[16,256,256]{2,1,0:T(8,128)(2,1)}, f32[256,1024]{1,0:T(8,128)}, bf16...) custom-call(bf16[256,1024]{1,0:T(8,128)(2,1)} %refs_0_.1, ...), custom_call_target="tpu_custom_call" | custom-call | flops 2415919104 | bytes 4558244 | tf_op jit(solution)/shard_map/pallas_call | solution.py:83
  112.5 138.7 %shard_map.249 = (f32[128,2816]{1,0:T(8,128)}, f32[128,2816]{1,0:T(8,128)}, bf16[2816,1024]{1,0:T(8,128)(2,1)}, bf16[4,256,1024]{2,1,0:T(8,128)(2,1)}, bf16[4,25...) custom-call(bf16[480,1024]{1,0:T(8,128)(2,1)} %get-tuple-element.52.buffer, bf16[480,1024]{1,0:T(8,128)(2,1)} %get-tuple-element.53.scaled, ...), custom_call_target="tpu_custom_call" | custom-call | flops 24914165760 | bytes 13484032 | tf_op jit(solution)/shard_map/pallas_call | solution.py:83
  251.2 87.3 %shard_map.250 = (bf16[256,1024]{1,0:T(8,128)(2,1)}, f32[256,1024]{1,0:T(8,128)}, f32[32,3072]{1,0:T(8,128)}, f32[32,1024]{1,0:T(8,128)}, f32[8,1024]{1,0:T(8,128)}, /*index=5*/f32[352,1024]{1,0:T(8,128)}) custom-call(bf16[256,1024]{1,0:T(8,128)(2,1)} %refs_0_.1, bf16[256,1024]{1,0:T(8,128)(2,1)} %refs_1_.1, ...), custom_call_target="tpu_custom_call" | custom-call | flops 4831838208 | bytes 35233800 | tf_op jit(solution)/shard_map/pallas_call | solution.py:83
  338.5 6.7 %shard_map.251 = (f32[4,32]{1,0:T(4,128)}, f32[1,32]{1,0:T(1,128)}, f32[1,32]{1,0:T(1,128)}, f32[1,16]{1,0:T(1,128)}, bf16[256,1024]{1,0:T(8,128)(2,1)}, /*index...) custom-call(f32[8,1024]{1,0:T(8,128)} %get-tuple-element.68.small, ...), custom_call_target="tpu_custom_call" | custom-call | bytes 6455296 | tf_op jit(solution)/shard_map/pallas_call | solution.py:83

commit v6 on v5

--- a/solution.py
+++ b/solution.py
@@ -775,11 +775,11 @@
     gate_own,
     up_own,
     down_own,
-    qkv,
-    attended,
-    probs,
-    resid,
-    normed_two,
+    qkv_kept,
+    attended_kept,
+    probs_kept,
+    resid_kept,
+    normed_kept,
     small,
     buffer,
     scaled,
@@ -809,6 +809,12 @@
     gather_recv,
     piece_stored,
     own_small,
+    qkv,
+    attended,
+    probs,
+    resid,
+    normed_two,
+    result_stored,
     *scratch,
 ):
     d, e, z, c = here()
@@ -933,6 +939,20 @@
     attend_forward(experts, tokens, projections, out_weight, heads, hot, length, out, between)
 
     rows_spread.start()
+    results = [
+        pltpu.make_async_copy(src, dst, result_stored.at[i])
+        for i, (src, dst) in enumerate(
+            (
+                (qkv, qkv_kept),
+                (attended, attended_kept),
+                (probs, probs_kept),
+                (resid, resid_kept),
+                (normed_two, normed_kept),
+            )
+        )
+    ]
+    for copy in results:
+        copy.start()
     own_cots.wait()
     cots_spread.finish()
     router_t = small[...].astype(BF16)
@@ -979,6 +999,8 @@
         spread.complete(j)
         store(i).start()
     rows_spread.sent()
+    for copy in results:
+        copy.wait()
     gather.settle()
     for i, (spread, j) in enumerate(pieces):
         spread.settle(j)
@@ -1014,6 +1036,8 @@
         DMA((5, 16)),
         DMA((pieces,)),
         pltpu.VMEM((8, 128), F32),
+        *[pltpu.VMEM(value.shape, value.dtype) for value in attention_shapes(experts, tokens)[:5]],
+        DMA((5,)),
         *LineSpread.scratch(ready),
         *LineSpread.scratch(width // CHUNK),
     ]
@@ -1027,7 +1051,7 @@
         2 * slots * width * (4 * width + 2 * slots),
         *args,
         stay=(4, 11, 12, 13, 14, 15),
-        land=tuple(len(shapes) + i for i in range(3)),
+        land=tuple(range(5)) + tuple(len(shapes) + i for i in range(3)),
         link=0,
     )
 
@@ -1187,6 +1211,12 @@
     down_stage,
     grads,
     inner_rows,
+    buffer_in,
+    scaled_in,
+    plain_in,
+    column_in,
+    select_in,
+    fetched,
     loaded,
     stored,
     local,
@@ -1220,15 +1250,30 @@
     def early_load(t):
         return pltpu.make_async_copy(early.at[t], both.at[t], loaded.at[t])
 
+    for j in range(min(DEPTH, coming)):
+        spread.start(j)
+    fetches = []
+    for i, (src, dst) in enumerate(
+        (
+            (buffer, buffer_in),
+            (scaled, scaled_in),
+            (plain, plain_in),
+            (gate_column, column_in),
+            (select, select_in),
+        )
+    ):
+        fetches.append(pltpu.make_async_copy(src, dst, fetched.at[i]))
+        fetches[-1].start()
+    buffer, scaled, plain, gate_column, select = buffer_in, scaled_in, plain_in, column_in, select_in
     down_load = pltpu.make_async_copy(down_full, down, loaded.at[tiles])
     for t in range(ready):
         early_load(t).start()
         if t == 0:
             down_load.start()
-    for j in range(min(DEPTH, coming)):
-        spread.start(j)
     acc_out[...] = jnp.zeros_like(acc_out)
     acc_grad[...] = jnp.zeros_like(acc_grad)
+    for copy in fetches:
+        copy.wait()
     down_load.wait()
 
     def down_rows(t):
@@ -1390,6 +1435,11 @@
         pltpu.VMEM((2, CHUNK, width), BF16),
         pltpu.VMEM(block, BF16),
         pltpu.VMEM(thin, F32),
+        *[
+            pltpu.VMEM(value.shape, value.dtype)
+            for value in (buffer, scaled, plain, gate_column, select)
+        ],
+        DMA((5,)),
         DMA((tiles + 1,)),
         DMA((2,)),
         DMA((3,)),
@@ -1412,7 +1462,7 @@
         up_own,
         early,
         down_full,
-        stay=(5, 6, 7, 8),
+        stay=tuple(range(9)),
         land=(0, 1, 2, 4, 5),
         link=2,
     )
@@ -1743,14 +1793,22 @@
     output, grad_tokens, qkv_sum, out_sum, small_sum, down_sum = take(6)
     grad_small, grad_out, *grad_halves = take(4)
     work = take(6)
-    half_sums, *brought, fetched = take(6)
-    cut = brought[0].shape[1]
+    (half_sums,) = take(1)
+    brought, (own_mixed, fetched) = take(len(FETCHED)), take(2)
+    cut = brought[FETCHED.index(2)].shape[1]
     ins[2], ins[3] = ins[2].at[:, :cut], ins[3].at[:, cut:]
-    fetches = []
+    fetches = {}
     for i, (at, ref) in enumerate(zip(FETCHED, brought)):
-        fetches.append(pltpu.make_async_copy(ins[at], ref, fetched.at[i]))
-        fetches[-1].start()
+        fetches[at] = pltpu.make_async_copy(ins[at], ref, fetched.at[i])
+        fetches[at].start()
         ins[at] = ref
+    fetches["mixed"] = pltpu.make_async_copy(mixed.at[0], own_mixed, fetched.at[len(FETCHED)])
+    fetches["mixed"].start()
+
+    def bring(names):
+        for name in names:
+            fetches.pop(name).wait()
+
     mixed_full, mixed_send, mixed_recv = take(3)
     d, e, z, _ = here()
     width = out_sum.shape[1]
@@ -1768,11 +1826,10 @@
 
     def reached(name):
         if name == "branch":
+            bring(tuple(fetches))
             down.halve(1)
         elif name == "out":
             out.begin()
-            for copy in fetches:
-                copy.wait()
         elif name == "attended":
             down.halve(2)
         elif name == "part0":
@@ -1799,6 +1856,7 @@
             halves[1].stage_one()
 
     outs = [grad_tokens, grad_small, grad_out] + grad_halves
+    bring((16, 10, 15, 1))
     backward_layer(experts, True, ins, outs, work, reached)
     halves[0].stage_three()
     every.step(0)
@@ -1821,7 +1879,7 @@
         down.finish(i, down_sum.at[:, i * CHUNK : (i + 1) * CHUNK])
     halves[1].line.pass_on(0)
     swap.finish()
-    add_mixed(output, ins[15], ins[7], [mixed.at[0]] + [mixed_full.at[q] for q in (1, 2, 3)])
+    add_mixed(output, ins[15], ins[7], [own_mixed] + [mixed_full.at[q] for q in (1, 2, 3)])
     out.line.finish(0, out_sum)
     wide = width // 2
     for half, sums in enumerate(halves):
@@ -1834,7 +1892,14 @@
     every.settle()
 
 
-FETCHED = (2, 3, 12, 14)
+FETCHED = (16, 10, 15, 1, 13, 3, 0, 12, 14, 2, 6)
+
+
+def fetched_shape(args, at):
+    width = args[0].shape[1]
+    if at in (2, 3):
+        return (width, args[2].shape[1] - width if at == 2 else width)
+    return args[at].shape
 
 
 def backward(experts, *args):
@@ -1849,10 +1914,9 @@
         pltpu.VMEM((width, half), BF16),
         *backward_scratch(slots, width),
         pltpu.VMEM((2, share, half), F32),
-        pltpu.VMEM((width, args[2].shape[1] - width), BF16),
-        pltpu.VMEM((width, width), BF16),
-        *[pltpu.VMEM(args[i].shape, BF16) for i in FETCHED[2:]],
-        DMA((len(FETCHED),)),
+        *[pltpu.VMEM(fetched_shape(args, i), args[i].dtype) for i in FETCHED],
+        pltpu.VMEM(mixed.shape[1:], BF16),
+        DMA((len(FETCHED) + 1,)),
         pltpu.VMEM(mixed.shape, BF16),
         DMA((4,)),
         DMA((4,)),
@@ -1876,7 +1940,7 @@
         63 * MB,
         4 * slots * width * (4 * width + 2 * slots),
         *args,
-        stay=(18,) + FETCHED,
+        stay=(17, 18) + FETCHED,
         link=3,
     )
 

time: 346 us -> 340 us (0.983)
  Pallas kernels: 344 us -> 338 us
    pallas_call x4, Pallas kernels: 344 us -> 338 us  [call(): pl.pallas_call(kernel, out_shape=out_shape, in_specs=[ANY_SPEC if i in st...]
where the time goes in v6:
time: 340 us; the launch traced here: 339 us
  Pallas kernels  338 us (99%)
    pallas_call x4, Pallas kernels, call(): pl.pallas_call(kernel, out_shape=out_shape, in_specs=[ANY_SPEC if i in st...  338 us

profile of v6, /device:TPU:0, one launch (start us, length us, event | category | flops | bytes accessed | tf_op | source)
XLA Modules:
  0.0 339.3 jit_solution(1127629851118905308)
XLA Ops:
  1.3 109.6 %shard_map.248 = (bf16[256,3072]{1,0:T(8,128)(2,1)}, bf16[256,1024]{1,0:T(8,128)(2,1)}, bf16[16,256,256]{2,1,0:T(8,128)(2,1)}, f32[256,1024]{1,0:T(8,128)}, bf16...) custom-call(bf16[256,1024]{1,0:T(8,128)(2,1)} %refs_0_.1, ...), custom_call_target="tpu_custom_call" | custom-call | flops 2415919104 | bytes 4558244 | tf_op jit(solution)/shard_map/pallas_call | solution.py:83
  110.9 136.6 %shard_map.249 = (f32[128,2816]{1,0:T(8,128)}, f32[128,2816]{1,0:T(8,128)}, bf16[2816,1024]{1,0:T(8,128)(2,1)}, bf16[4,256,1024]{2,1,0:T(8,128)(2,1)}, bf16[4,25...) custom-call(bf16[480,1024]{1,0:T(8,128)(2,1)} %get-tuple-element.52.buffer, bf16[480,1024]{1,0:T(8,128)(2,1)} %get-tuple-element.53.scaled, ...), custom_call_target="tpu_custom_call" | custom-call | flops 24914165760 | bytes 13484032 | tf_op jit(solution)/shard_map/pallas_call | solution.py:83
  247.5 84.8 %shard_map.250 = (bf16[256,1024]{1,0:T(8,128)(2,1)}, f32[256,1024]{1,0:T(8,128)}, f32[32,3072]{1,0:T(8,128)}, f32[32,1024]{1,0:T(8,128)}, f32[8,1024]{1,0:T(8,128)}, /*index=5*/f32[352,1024]{1,0:T(8,128)}) custom-call(bf16[256,1024]{1,0:T(8,128)(2,1)} %refs_0_.1, bf16[256,1024]{1,0:T(8,128)(2,1)} %refs_1_.1, ...), custom_call_target="tpu_custom_call" | custom-call | flops 4831838208 | bytes 35233800 | tf_op jit(solution)/shard_map/pallas_call | solution.py:83
  332.4 6.7 %shard_map.251 = (f32[4,32]{1,0:T(4,128)}, f32[1,32]{1,0:T(1,128)}, f32[1,32]{1,0:T(1,128)}, f32[1,16]{1,0:T(1,128)}, bf16[256,1024]{1,0:T(8,128)(2,1)}, /*index...) custom-call(f32[8,1024]{1,0:T(8,128)} %get-tuple-element.68.small, ...), custom_call_target="tpu_custom_call" | custom-call | bytes 6455296 | tf_op jit(solution)/shard_map/pallas_call | solution.py:83

commit v7 on v6

--- a/solution.py
+++ b/solution.py
@@ -1946,21 +1946,29 @@
 
 
 def publish_kernel(experts, small, *refs):
-    count = (len(refs) - 6) // 3
-    ins, refs = refs[:count], refs[count:]
-    router, first, second, bias, *refs = refs
-    outs, held = refs[:count], refs[count : 2 * count]
-    loads = [pltpu.make_async_copy(ins[i], held[i], refs[-2].at[i]) for i in range(count)]
-    stores = [pltpu.make_async_copy(held[i], outs[i], refs[-1].at[i]) for i in range(count)]
+    count = (len(refs) - 12) // 3
+    refs = list(refs)
+    ins, smalls, outs = refs[:count], refs[count : count + 4], refs[count + 4 : 2 * count + 4]
+    held, small_in = refs[2 * count + 4 : 3 * count + 4], refs[3 * count + 4]
+    parts, (loaded, stored, moved) = refs[3 * count + 5 : 3 * count + 9], refs[3 * count + 9 :]
+    fetch = pltpu.make_async_copy(small, small_in, moved.at[4])
+    loads = [pltpu.make_async_copy(ins[i], held[i], loaded.at[i]) for i in range(count)]
+    stores = [pltpu.make_async_copy(held[i], outs[i], stored.at[i]) for i in range(count)]
+    stores += [pltpu.make_async_copy(parts[i], smalls[i], moved.at[i]) for i in range(4)]
+    fetch.start()
     for copy in loads:
         copy.start()
-    width, share = small.shape[1], first.shape[1]
+    router, first, second, bias = parts
+    width, share = small_in.shape[1], first.shape[1]
     device = lax.axis_index("dp") * experts + lax.axis_index("expert")
-    turned = pltpu.roll(small[...], lax.rem(width - device * share, width), 1)
+    fetch.wait()
+    turned = pltpu.roll(small_in[...], lax.rem(width - device * share, width), 1)
     router[...] = turned[:experts, :share]
     first[...] = turned[experts : experts + 1, :share]
     second[...] = turned[experts + 1 : experts + 2, :share]
     bias[...] = turned[experts + 2 : experts + 3, : bias.shape[1]]
+    for copy in stores[count:]:
+        copy.start()
     for load, store in zip(loads, stores):
         load.wait()
         store.start()
@@ -1971,20 +1979,21 @@
 def publish(experts, small, bias_share, *values):
     count = len(values)
     share = small.shape[1] // 32
+    shapes = ((experts, share), (1, share), (1, share), (1, bias_share))
     return call(
         functools.partial(publish_kernel, experts),
-        tuple(
-            jax.ShapeDtypeStruct(shape, F32)
-            for shape in ((experts, share), (1, share), (1, share), (1, bias_share))
-        )
+        tuple(jax.ShapeDtypeStruct(shape, F32) for shape in shapes)
         + tuple(jax.ShapeDtypeStruct(value.shape, value.dtype) for value in values),
-        [pltpu.VMEM(value.shape, value.dtype) for value in values] + [DMA((count,)), DMA((count,))],
+        [pltpu.VMEM(value.shape, value.dtype) for value in values]
+        + [pltpu.VMEM(small.shape, F32)]
+        + [pltpu.VMEM(shape, F32) for shape in shapes]
+        + [DMA((count,)), DMA((count,)), DMA((5,))],
         60 * MB,
         0,
         small,
         *values,
-        stay=tuple(range(1, count + 1)),
-        land=tuple(range(4, count + 4)),
+        stay=tuple(range(count + 1)),
+        land=tuple(range(count + 4)),
     )
 
 

time: 340 us -> 338 us (level)
  no operation moved by 1% of the time
where the time goes in v7:
time: 338 us
  Pallas kernels  336 us (99%)
    pallas_call x4, Pallas kernels, call(): pl.pallas_call(kernel, out_shape=out_shape, in_specs=[ANY_SPEC if i in st...  336 us

profile of v7, /device:TPU:0, one launch (start us, length us, event | category | flops | bytes accessed | tf_op | source)
XLA Modules:
  0.0 337.8 jit_solution(12847837807240058821)
XLA Ops:
  1.3 109.6 %shard_map.248 = (bf16[256,3072]{1,0:T(8,128)(2,1)}, bf16[256,1024]{1,0:T(8,128)(2,1)}, bf16[16,256,256]{2,1,0:T(8,128)(2,1)}, f32[256,1024]{1,0:T(8,128)}, bf16...) custom-call(bf16[256,1024]{1,0:T(8,128)(2,1)} %refs_0_.1, ...), custom_call_target="tpu_custom_call" | custom-call | flops 2415919104 | bytes 4558244 | tf_op jit(solution)/shard_map/pallas_call | solution.py:83
  110.9 136.6 %shard_map.249 = (f32[128,2816]{1,0:T(8,128)}, f32[128,2816]{1,0:T(8,128)}, bf16[2816,1024]{1,0:T(8,128)(2,1)}, bf16[4,256,1024]{2,1,0:T(8,128)(2,1)}, bf16[4,25...) custom-call(bf16[480,1024]{1,0:T(8,128)(2,1)} %get-tuple-element.52.buffer, bf16[480,1024]{1,0:T(8,128)(2,1)} %get-tuple-element.53.scaled, ...), custom_call_target="tpu_custom_call" | custom-call | flops 24914165760 | bytes 13484032 | tf_op jit(solution)/shard_map/pallas_call | solution.py:83
  247.5 84.8 %shard_map.250 = (bf16[256,1024]{1,0:T(8,128)(2,1)}, f32[256,1024]{1,0:T(8,128)}, f32[32,3072]{1,0:T(8,128)}, f32[32,1024]{1,0:T(8,128)}, f32[8,1024]{1,0:T(8,128)}, /*index=5*/f32[352,1024]{1,0:T(8,128)}) custom-call(bf16[256,1024]{1,0:T(8,128)(2,1)} %refs_0_.1, bf16[256,1024]{1,0:T(8,128)(2,1)} %refs_1_.1, ...), custom_call_target="tpu_custom_call" | custom-call | flops 4831838208 | bytes 35233800 | tf_op jit(solution)/shard_map/pallas_call | solution.py:83
  332.4 5.3 %shard_map.251 = (f32[4,32]{1,0:T(4,128)}, f32[1,32]{1,0:T(1,128)}, f32[1,32]{1,0:T(1,128)}, f32[1,16]{1,0:T(1,128)}, bf16[256,1024]{1,0:T(8,128)(2,1)}, /*index...) custom-call(f32[8,1024]{1,0:T(8,128)} %get-tuple-element.68.small, ...), custom_call_target="tpu_custom_call" | custom-call | bytes 6455296 | tf_op jit(solution)/shard_map/pallas_call | solution.py:83

commit v8 on v7

--- a/solution.py
+++ b/solution.py
@@ -783,8 +783,8 @@
     small,
     buffer,
     scaled,
-    plain,
-    select,
+    plain_kept,
+    select_kept,
     gate_column,
     meta,
     kept,
@@ -814,6 +814,8 @@
     probs,
     resid,
     normed_two,
+    plain,
+    select,
     result_stored,
     *scratch,
 ):
@@ -983,6 +985,12 @@
     near(5)
     take_cots(3)
     plain[...] = acc_cot[...].astype(BF16)
+    results += [
+        pltpu.make_async_copy(plain, plain_kept, result_stored.at[5]),
+        pltpu.make_async_copy(select, select_kept, result_stored.at[6]),
+    ]
+    for copy in results[5:]:
+        copy.start()
     take_rows(0, normed_two)
     far(5)
     near(6)
@@ -1037,7 +1045,8 @@
         DMA((pieces,)),
         pltpu.VMEM((8, 128), F32),
         *[pltpu.VMEM(value.shape, value.dtype) for value in attention_shapes(experts, tokens)[:5]],
-        DMA((5,)),
+        *[pltpu.VMEM(value.shape, value.dtype) for value in dispatch_shapes(*block)[2:4]],
+        DMA((7,)),
         *LineSpread.scratch(ready),
         *LineSpread.scratch(width // CHUNK),
     ]
@@ -1051,7 +1060,7 @@
         2 * slots * width * (4 * width + 2 * slots),
         *args,
         stay=(4, 11, 12, 13, 14, 15),
-        land=tuple(range(5)) + tuple(len(shapes) + i for i in range(3)),
+        land=tuple(range(5)) + (8, 9) + tuple(len(shapes) + i for i in range(3)),
         link=0,
     )
 
@@ -1200,9 +1209,10 @@
     gate_sum,
     up_sum,
     grad_down,
-    mixed,
+    mixed_kept,
     returned,
     inner_full,
+    mixed,
     sums,
     both,
     down,
@@ -1368,6 +1378,8 @@
     weighted = (low.astype(F32) * gate_column[:, 0:1]).astype(BF16)
     for block in order:
         mixed[block] = dot_tn(select[block], weighted).astype(BF16)
+    own_copies.append(pltpu.make_async_copy(mixed, mixed_kept, local.at[3]))
+    own_copies[-1].start()
 
     @pl.loop(tiles - LAG, tiles + 1)
     def _(i):
@@ -1427,6 +1439,7 @@
         jax.ShapeDtypeStruct(thin, F32),
     )
     scratch = [
+        pltpu.VMEM(block, BF16),
         pltpu.VMEM((tiles, share, TILE), F32),
         pltpu.VMEM((tiles, width, TILE), BF16),
         pltpu.VMEM(down_full.shape, BF16),
@@ -1442,7 +1455,7 @@
         DMA((5,)),
         DMA((tiles + 1,)),
         DMA((2,)),
-        DMA((3,)),
+        DMA((4,)),
         DMA((2, 4)),
         DMA((2, 4)),
     ]
@@ -1463,7 +1476,7 @@
         early,
         down_full,
         stay=tuple(range(9)),
-        land=(0, 1, 2, 4, 5),
+        land=tuple(range(6)),
         link=2,
     )
 

time: 338 us -> 336 us (level)
  no operation moved by 1% of the time
where the time goes in v8:
time: 336 us
  Pallas kernels  334 us (99%)
    pallas_call x4, Pallas kernels, call(): pl.pallas_call(kernel, out_shape=out_shape, in_specs=[ANY_SPEC if i in st...  334 us

profile of v8, /device:TPU:0, one launch (start us, length us, event | category | flops | bytes accessed | tf_op | source)
XLA Modules:
  0.0 335.8 jit_solution(18226526100327731827)
XLA Ops:
  1.3 108.9 %shard_map.248 = (bf16[256,3072]{1,0:T(8,128)(2,1)}, bf16[256,1024]{1,0:T(8,128)(2,1)}, bf16[16,256,256]{2,1,0:T(8,128)(2,1)}, f32[256,1024]{1,0:T(8,128)}, bf16...) custom-call(bf16[256,1024]{1,0:T(8,128)(2,1)} %refs_0_.1, ...), custom_call_target="tpu_custom_call" | custom-call | flops 2415919104 | bytes 4558244 | tf_op jit(solution)/shard_map/pallas_call | solution.py:83
  110.2 135.3 %shard_map.249 = (f32[128,2816]{1,0:T(8,128)}, f32[128,2816]{1,0:T(8,128)}, bf16[2816,1024]{1,0:T(8,128)(2,1)}, bf16[4,256,1024]{2,1,0:T(8,128)(2,1)}, bf16[4,25...) custom-call(bf16[480,1024]{1,0:T(8,128)(2,1)} %get-tuple-element.52.buffer, bf16[480,1024]{1,0:T(8,128)(2,1)} %get-tuple-element.53.scaled, ...), custom_call_target="tpu_custom_call" | custom-call | flops 24914165760 | bytes 13484032 | tf_op jit(solution)/shard_map/pallas_call | solution.py:83
  245.5 84.8 %shard_map.250 = (bf16[256,1024]{1,0:T(8,128)(2,1)}, f32[256,1024]{1,0:T(8,128)}, f32[32,3072]{1,0:T(8,128)}, f32[32,1024]{1,0:T(8,128)}, f32[8,1024]{1,0:T(8,128)}, /*index=5*/f32[352,1024]{1,0:T(8,128)}) custom-call(bf16[256,1024]{1,0:T(8,128)(2,1)} %refs_0_.1, bf16[256,1024]{1,0:T(8,128)(2,1)} %refs_1_.1, ...), custom_call_target="tpu_custom_call" | custom-call | flops 4831838208 | bytes 35233800 | tf_op jit(solution)/shard_map/pallas_call | solution.py:83
  330.4 5.3 %shard_map.251 = (f32[4,32]{1,0:T(4,128)}, f32[1,32]{1,0:T(1,128)}, f32[1,32]{1,0:T(1,128)}, f32[1,16]{1,0:T(1,128)}, bf16[256,1024]{1,0:T(8,128)(2,1)}, /*index...) custom-call(f32[8,1024]{1,0:T(8,128)} %get-tuple-element.68.small, ...), custom_call_target="tpu_custom_call" | custom-call | bytes 6455296 | tf_op jit(solution)/shard_map/pallas_call | solution.py:83
